TPU v7x, 32 devices: a whole 2x2x4 slice. The times are simulated.
32 devices in a mesh: dp: 8 (over y, x, core), expert: 4 (over z).
Axes of the slice: x: 2, y: 2, z: 4, core: 2. Of those that a mesh axis runs over, the one named last changes fastest.
Arguments:
- out_grad: bfloat16 [8, 1024, 2048], P('dp', 'expert'), may hold values from -6 to 6
- gates: bfloat16 [8, 1024, 8], P('dp', 'expert'), may hold values from 0.019897461 to 0.5
- expert_ids: int32 [8, 1024, 8], P('dp', 'expert'), may hold values from 0 to 127, as said below
- route_slots: int32 [8, 1024, 8], P('dp', 'expert'), may hold values from -1 to 20, as said below
- saved_hidden: bfloat16 [8, 4, 84, 768], P('dp', 'expert'), may hold values from -0.21582031 to 0.21582031
- down_weight: bfloat16 [4, 768, 2048], P('expert'), may hold values from -0.21875 to 0.21875
Outputs:
- hidden_grad: bfloat16 [8, 4, 84, 768], P('dp', 'expert')
- weight_grad: float32 [4, 768, 2048], P('expert', 'dp')
- gate_grad: float32 [8, 1024, 8], P('dp', 'expert')
Inputs may be any that keep to these rules, and one draw needn't show every extreme that they name: `expert_ids`: each token names 8 different experts. `route_slots`: for each replica, each block of 256 tokens and each expert e below 4, the routes of that block to e that have a slot take the numbers 0, 1, 2 and on without gaps in the order of tokens and ranks, at most 21 of them; routes to experts 4 and above have -1. In every replica some expert below 4 holds 21 routes from every block, and routes beyond that are -1.
All inputs are finite; a program needn't handle non-finite values.
Results may differ from a plain program's by a relative error of at most 0.0095.
Values may be sent and summed in bfloat16 or wider, within the bound.
No kernel may reach another device: no remote copies, remote signals or barrier semaphores. Data moves between devices by JAX's collectives and lax.ppermute only.
A program may use at most 64 MiB of HBM per device.

v0:
```python
import functools
import math

import jax
import jax.numpy as jnp
from jax import lax
from jax.experimental import pallas as pl
from jax.experimental.pallas import tpu as pltpu
from jax.sharding import PartitionSpec as P


F32 = jnp.float32
BF16 = jnp.bfloat16
LIMIT = 24 * 1024 * 1024


def params(**kw):
    return pltpu.CompilerParams(vmem_limit_bytes=LIMIT, **kw)


def pad8(n):
    return -(-n // 8) * 8


def matmul_t(a, b, contract):
    return lax.dot_general(a, b, ((contract[:1], contract[1:]), ((), ())), preferred_element_type=F32)


def pack_kernel(experts, padded, ids_ref, slots_ref, gates_ref, grad_ref, *out_refs):
    me = lax.axis_index("expert")
    ids = ids_ref[...]
    slots = slots_ref[...]
    gates = gates_ref[...].astype(F32)
    valid = (ids < experts) & (slots >= 0)
    target = jnp.where(valid, (ids ^ me) * padded + slots, -1)
    row = lax.broadcasted_iota(jnp.int32, (experts * padded, ids.shape[1]), 0)
    chosen = jnp.zeros(row.shape, F32)
    for k in range(ids.shape[0]):
        chosen = jnp.where(row == target[k : k + 1, :], gates[k : k + 1, :], chosen)
    rows = jnp.dot(chosen.astype(BF16), grad_ref[...], preferred_element_type=F32)
    for k, out in enumerate(out_refs):
        out[...] = rows[k * padded : (k + 1) * padded, :].astype(BF16)


def pack(ids, slots, gates, grad, experts, padded):
    ranks, tokens = ids.shape
    width = grad.shape[1]
    steps = 4
    block = width // steps
    whole = pl.BlockSpec((ranks, tokens), lambda i: (0, 0))
    return pl.pallas_call(
        functools.partial(pack_kernel, experts, padded),
        grid=(steps,),
        in_specs=[whole, whole, whole, pl.BlockSpec((tokens, block), lambda i: (0, i))],
        out_specs=[pl.BlockSpec((padded, block), lambda i: (0, i))] * experts,
        out_shape=[jax.ShapeDtypeStruct((padded, width), BF16)] * experts,
        compiler_params=params(),
        name="pack",
    )(ids, slots, gates, grad)


def join_kernel(experts, capacity, *refs):
    blocks = refs[:experts]
    full_ref, own_ref, other_ref = refs[experts:]
    me = lax.axis_index("expert")
    core = lax.axis_index("dp") % 2
    slots = experts * capacity
    padded = blocks[0].shape[0]
    half = full_ref.shape[1] // 2
    total = jnp.zeros(full_ref.shape, F32)
    for k, block in enumerate(blocks):
        row = lax.broadcasted_iota(jnp.int32, (slots, padded), 0)
        col = lax.broadcasted_iota(jnp.int32, (slots, padded), 1)
        place = (row == (me ^ k) * capacity + col) & (col < capacity)
        total += jnp.dot(place.astype(BF16), block[...], preferred_element_type=F32)
    full_ref[...] = total.astype(BF16)
    own_ref[...] = full_ref[:, pl.ds(pl.multiple_of(core * half, 128), half)]
    other_ref[...] = full_ref[:, pl.ds(pl.multiple_of((1 - core) * half, 128), half)]


def join(blocks, capacity):
    experts = len(blocks)
    slots, width = experts * capacity, blocks[0].shape[1]
    vmem = pl.BlockSpec(memory_space=pltpu.VMEM)
    return pl.pallas_call(
        functools.partial(join_kernel, experts, capacity),
        in_specs=[vmem] * experts,
        out_specs=[vmem] * 3,
        out_shape=[
            jax.ShapeDtypeStruct((slots, width), BF16),
            jax.ShapeDtypeStruct((slots, width // 2), BF16),
            jax.ShapeDtypeStruct((slots, width // 2), BF16),
        ],
        compiler_params=params(),
        name="join",
    )(*blocks)


def hidden_kernel(full_ref, weight_ref, hidden_ref, grad_ref, row_ref, acc_ref):
    step = pl.program_id(0)
    unit = matmul_t(full_ref[...], weight_ref[...], (1, 1))
    grad_ref[...] = unit.astype(BF16)
    product = unit * hidden_ref[...].astype(F32)
    lanes = product[:, :128]
    for j in range(1, product.shape[1] // 128):
        lanes += product[:, j * 128 : (j + 1) * 128]

    @pl.when(step == 0)
    def _():
        acc_ref[...] = jnp.zeros_like(acc_ref)

    slots = lanes.shape[0]
    acc_ref[:slots, :] += lanes

    @pl.when(step == pl.num_programs(0) - 1)
    def _():
        row_ref[...] = jnp.sum(acc_ref[...].T, axis=0, keepdims=True)


def hidden_part(full, weight, hidden):
    slots, width = full.shape
    units = weight.shape[0]
    steps = 3
    block = units // steps
    lanes = -(-slots // 128) * 128
    return pl.pallas_call(
        hidden_kernel,
        grid=(steps,),
        in_specs=[
            pl.BlockSpec((slots, width), lambda i: (0, 0)),
            pl.BlockSpec((block, width), lambda i: (i, 0)),
            pl.BlockSpec((slots, block), lambda i: (0, i)),
        ],
        out_specs=[
            pl.BlockSpec((slots, block), lambda i: (0, i)),
            pl.BlockSpec((1, lanes), lambda i: (0, 0)),
        ],
        out_shape=[
            jax.ShapeDtypeStruct((slots, units), BF16),
            jax.ShapeDtypeStruct((1, lanes), F32),
        ],
        scratch_shapes=[pltpu.VMEM((lanes, 128), F32)],
        compiler_params=params(),
        name="hidden",
    )(full, weight, hidden)


def partial_kernel(side, count, *refs):
    hiddens, rows = refs[:count], refs[count : 2 * count]
    outs, total_ref = refs[2 * count : -1], refs[-1]
    index = lax.axis_index("dp")
    core = index % 2
    total = matmul_t(hiddens[0][...], rows[0][...], (0, 0))
    for hidden, row in zip(hiddens[1:], rows[1:]):
        total += matmul_t(hidden[...], row[...], (0, 0))
    total_ref[...] = total
    height = outs[0].shape[0]
    for out, mask in zip(outs, owner_masks(side)):
        owner = index ^ jnp.where(core == 0, mask[0], mask[1])
        start = pl.multiple_of(owner * height, 8)
        out[...] = total_ref[pl.ds(start, height), :].astype(out.dtype)


def partial(hiddens, rows, side, height):
    count = len(hiddens)
    units, half = hiddens[0].shape[1], rows[0].shape[1]
    slots = rows[0].shape[0]
    steps = 2
    block = half // steps
    masks = owner_masks(side)
    return pl.pallas_call(
        functools.partial(partial_kernel, side, count),
        grid=(steps,),
        in_specs=[pl.BlockSpec((slots, units), lambda i: (0, 0))] * count
        + [pl.BlockSpec((slots, block), lambda i: (0, i))] * count,
        out_specs=[pl.BlockSpec((height, block), lambda i: (0, i))] * len(masks),
        out_shape=[
            jax.ShapeDtypeStruct((height, half), F32 if n == 0 else BF16) for n in range(len(masks))
        ],
        scratch_shapes=[pltpu.VMEM((units, block), F32)],
        compiler_params=params(),
        name="partial",
    )(*hiddens, *rows)


def gather_masks(side):
    inner = [(d * 2) for d in range(1, side)]
    outer = [(d * side * 2) for d in range(1, side)]
    same = [(i, o) for i, o in zip(inner, outer)]
    cross = [(o ^ 1, i ^ 1) for i, o in zip(inner, outer)]
    return same, cross


def owner_masks(side):
    same = [(d * side * 2, d * 2) for d in range(1, side)]
    cross = [(a ^ 1, b ^ 1) for a, b in same]
    return [(0, 0), (1, 1)] + same + cross


def exchange(value, count, mask):
    pairs = [(i, i ^ mask[i % 2]) for i in range(count)]
    return lax.ppermute(value, "dp", pairs)


def total_kernel(terms, own_ref, *refs):
    own_terms, other_terms, out_ref = refs[:terms], refs[terms:-1], refs[-1]
    core = lax.axis_index("dp") % 2
    half = own_ref.shape[1]
    own = own_ref[...]
    for term in own_terms:
        own += term[...].astype(F32)
    other = other_terms[0][...].astype(F32)
    for term in other_terms[1:]:
        other += term[...].astype(F32)
    out_ref[:, pl.ds(pl.multiple_of(core * half, 128), half)] = own
    out_ref[:, pl.ds(pl.multiple_of((1 - core) * half, 128), half)] = other


def total(own, own_terms, other_terms):
    height, half = own.shape
    vmem = pl.BlockSpec(memory_space=pltpu.VMEM)
    return pl.pallas_call(
        functools.partial(total_kernel, len(own_terms)),
        in_specs=[vmem] * (1 + len(own_terms) + len(other_terms)),
        out_specs=vmem,
        out_shape=jax.ShapeDtypeStruct((height, 2 * half), F32),
        compiler_params=params(),
        name="total",
    )(own, *own_terms, *other_terms)


def gate_kernel(experts, capacity, *refs):
    tables = refs[:experts]
    ids_ref, slots_ref, gates_ref, out_ref = refs[experts:]
    me = lax.axis_index("expert")
    ids = ids_ref[...]
    slots = slots_ref[...]
    valid = (ids < experts) & (slots >= 0)
    target = jnp.where(valid, (ids ^ me) * capacity + slots, -1)
    value = jnp.zeros(ids.shape, F32)
    for k, table in enumerate(tables):
        for c in range(capacity):
            value = jnp.where(target == k * capacity + c, table[0, me * capacity + c], value)
    out_ref[...] = value / gates_ref[...].astype(F32)


def gate_part(tables, ids, slots, gates, capacity):
    experts = len(tables)
    vmem = pl.BlockSpec(memory_space=pltpu.VMEM)
    smem = pl.BlockSpec(memory_space=pltpu.SMEM)
    return pl.pallas_call(
        functools.partial(gate_kernel, experts, capacity),
        in_specs=[smem] * experts + [vmem] * 3,
        out_specs=vmem,
        out_shape=jax.ShapeDtypeStruct(ids.shape, F32),
        compiler_params=params(),
        name="gate",
    )(*tables, ids, slots, gates)


def on_device(out_grad, gates, expert_ids, route_slots, saved_hidden, down_weight):
    experts = lax.axis_size("expert")
    replicas = lax.axis_size("dp")
    side = math.isqrt(replicas // 2)
    assert 2 * side * side == replicas
    hidden = saved_hidden[0, 0]
    weight = down_weight[0]
    capacity = hidden.shape[0] // experts
    ids, slots, gate = expert_ids[0].T, route_slots[0].T, gates[0].T

    sent = pack(ids, slots, gate, out_grad[0], experts, pad8(capacity))
    blocks = [sent[0]]
    for k in range(1, experts):
        pairs = [(i, i ^ k) for i in range(experts)]
        blocks.append(lax.ppermute(sent[k], "expert", pairs))

    same, cross = gather_masks(side)
    routes = [(1, 1)] + same + cross
    hiddens = [hidden]
    for mask in routes:
        hiddens.append(exchange(hidden, replicas, mask))

    blocks, hiddens = lax.optimization_barrier((blocks, hiddens))
    full, own, other = join(blocks, capacity)
    rows = [own]
    for mask in routes:
        rows.append(exchange(own if mask in same else other, replicas, mask))

    hidden_grad, row_sums = hidden_part(full, weight, hidden)
    tables = [row_sums]
    for k in range(1, experts):
        pairs = [(i, i ^ k) for i in range(experts)]
        tables.append(lax.ppermute(row_sums, "expert", pairs))

    height = hidden.shape[1] // replicas
    cut = partial(hiddens, rows, side, height)
    moved = []
    for n, mask in enumerate(owner_masks(side)[1:]):
        moved.append(exchange(cut[n + 1], replicas, mask))
    weight_grad = total(cut[0], moved[1:side], [moved[0]] + moved[side:])

    gate_grad = gate_part(tables, ids, slots, gate, capacity)
    return hidden_grad[None, None], weight_grad[None], gate_grad.T[None]


def solution(mesh):
    in_specs = (
        P("dp", "expert", None),
        P("dp", "expert", None),
        P("dp", "expert", None),
        P("dp", "expert", None),
        P("dp", "expert", None, None),
        P("expert", None, None),
    )
    out_specs = (P("dp", "expert", None, None), P("expert", "dp", None), P("dp", "expert", None))
    return jax.shard_map(
        on_device, mesh=mesh, in_specs=in_specs, out_specs=out_specs, check_vma=False
    )
```

profile of v0, /device:TPU:0, one launch (start us, length us, event | category | flops | bytes accessed | tf_op | source)
XLA Modules:
  0.0 50.3 jit_solution(5063551038077228566)
XLA Ops:
  0.6 0.0 copy-start.1
  0.6 1.2 %copy-done.1 = bf16[1,256,2048]{2,1,0:T(8,128)(2,1)S(1)} copy-done((bf16[1,256,2048]{2,1,0:T(8,128)(2,1)S(1)}, bf16[1,256,2048]{2,1,0:T(8,128)(2,1)}, u32[]{:S(2)}) %copy-start.1) | copy-done | bytes 1048600
  1.9 0.0 copy-start.4
  1.9 0.7 %copy-done.4 = s32[1,256,8]{1,2,0:T(8,128)S(1)} copy-done((s32[1,256,8]{1,2,0:T(8,128)S(1)}, s32[1,256,8]{1,2,0:T(8,128)}, u32[]{:S(2)}) %copy-start.4) | copy-done | bytes 8216
  2.6 0.7 %copy-done.6 = s32[1,256,8]{1,2,0:T(8,128)S(1)} copy-done((s32[1,256,8]{1,2,0:T(8,128)S(1)}, s32[1,256,8]{1,2,0:T(8,128)}, u32[]{:S(2)}) %copy-start.6) | copy-done | bytes 8216
  3.3 0.7 %copy-done.8 = bf16[1,256,8]{1,2,0:T(8,128)(2,1)S(1)} copy-done((bf16[1,256,8]{1,2,0:T(8,128)(2,1)S(1)}, bf16[1,256,8]{1,2,0:T(8,128)(2,1)}, u32[]{:S(2)}) %copy-start.8) | copy-done | bytes 4120
  3.9 1.0 %pack.1 = (bf16[24,2048]{1,0:T(8,128)(2,1)S(1)}, bf16[24,2048]{1,0:T(8,128)(2,1)S(1)}, bf16[24,2048]{1,0:T(8,128)(2,1)S(1)}, bf16[24,2048]{1,0:T(8,128)(2,1)S(1)}) custom-call(s32[8,256]{1,0:T(8,128)S(1)} %bitcast.24, s32[8,256]{1,0:T(8,128)S(1)} %bitcast.26, bf16[8,256]{1,0:T(8,128)(2,1)S(1)} %bitcast.28, bf16[256,2048]{1,0:T(8,128)(2,1)S(1)} %bitcast.18), custom_call_target="tpu_custom_call" | custom-call | tf_op jit(solution)/shard_map/pack/pallas_call | solution.py:51
  4.9 3.1 %collective-permute-start = (bf16[24,2048]{1,0:T(8,128)(2,1)S(1)}, bf16[24,2048]{1,0:T(8,128)(2,1)S(1)}, u32[]{:S(2)}, u32[]{:S(2)}) collective-permute-start(bf16[24,2048]{1,0:T(8,128)(2,1)S(1)} %get-tuple-element.25), channel_id=1, source_target_pairs={{0,1},{1,0},{2,3},{3,2},{4,5},{5,4},{6,7},{7,6},{8,9},{9,8},{10,11... | collective-permute-start | bytes 294920 | tf_op jit(solution)/shard_map/ppermute | solution.py:275
  8.0 0.0 collective-permute-start.3
  8.0 1.5 %collective-permute-start.4 = (bf16[84,768]{1,0:T(8,128)(2,1)}, bf16[84,768]{1,0:T(8,128)(2,1)S(1)}, u32[]{:S(2)}, u32[]{:S(2)}) collective-permute-start(bf16[84,768]{1,0:T(8,128)(2,1)} %bitcast.20), channel_id=1, source_target_pairs={{0,8},{4,20},{8,0},{12,28},{16,24},{20,4},{24,16},{28,12},{1,9},{5... | collective-permute-start | bytes 387080 | tf_op jit(solution)/shard_map/ppermute | solution.py:202
  9.5 0.4 collective-permute-start.5
  9.9 2.6 %collective-permute-start.1 = (bf16[24,2048]{1,0:T(8,128)(2,1)S(1)}, bf16[24,2048]{1,0:T(8,128)(2,1)S(1)}, u32[]{:S(2)}, u32[]{:S(2)}) collective-permute-start(bf16[24,2048]{1,0:T(8,128)(2,1)S(1)} %get-tuple-element.26), channel_id=1, source_target_pairs={{0,2},{1,3},{2,0},{3,1},{4,6},{5,7},{6,4},{7,5},{8,10},{9,11},{10,... | collective-permute-start | bytes 294920 | tf_op jit(solution)/shard_map/ppermute | solution.py:275
  12.5 0.0 collective-permute-done.refs_1_
  12.5 2.2 %collective-permute-start.2 = (bf16[24,2048]{1,0:T(8,128)(2,1)S(1)}, bf16[24,2048]{1,0:T(8,128)(2,1)S(1)}, u32[]{:S(2)}, u32[]{:S(2)}) collective-permute-start(bf16[24,2048]{1,0:T(8,128)(2,1)S(1)} %get-tuple-element.27), channel_id=1, source_target_pairs={{0,3},{1,2},{2,1},{3,0},{4,7},{5,6},{6,5},{7,4},{8,11},{9,10},{10,... | collective-permute-start | bytes 294920 | tf_op jit(solution)/shard_map/ppermute | solution.py:275
  14.7 5.2 %collective-permute-done.1.refs_2_ = bf16[24,2048]{1,0:T(8,128)(2,1)S(1)} collective-permute-done((bf16[24,2048]{1,0:T(8,128)(2,1)S(1)}, bf16[24,2048]{1,0:T(8,128)(2,1)S(1)}, u32[]{:S(2)}, u32[]{:S(2)}) %collective-permute-start.1) | collective-permute-done | bytes 98336 | tf_op jit(solution)/shard_map/ppermute | solution.py:275
  19.9 0.0 collective-permute-done.2.refs_3_
  19.9 0.0 collective-permute-done.3.refs_1_
  19.9 0.0 collective-permute-done.4.refs_2_
  19.9 0.0 collective-permute-done.5.refs_3_
  19.9 0.6 %join.1 = (bf16[84,2048]{1,0:T(8,128)(2,1)S(1)}, bf16[84,1024]{1,0:T(8,128)(2,1)S(1)}, bf16[84,1024]{1,0:T(8,128)(2,1)S(1)}) custom-call(bf16[24,2048]{1,0:T(8,128)(2,1)S(1)} %get-tuple-element.28.refs_0_, bf16[24,2048]{1,0:T(8,128)(2,1)S(1)} %collective-permute-done.refs_1_, bf16[24,2048]{1,0:T(8,128)(2,1)S(1)} %collective-permute-done.1.refs_2_, ...), custom_call_target="tpu_custom_call" | custom-call | tf_op jit(solution)/shard_map/join/pallas_call | solution.py:85
  20.5 0.1 collective-permute-start.6
  20.6 1.6 %collective-permute-start.7 = (bf16[84,1024]{1,0:T(8,128)(2,1)S(1)}, bf16[84,1024]{1,0:T(8,128)(2,1)S(1)}, u32[]{:S(2)}, u32[]{:S(2)}) collective-permute-start(bf16[84,1024]{1,0:T(8,128)(2,1)S(1)} %get-tuple-element.38.refs_4_), channel_id=1, source_target_pairs={{0,8},{4,20},{8,0},{12,28},{16,24},{20,4},{24,16},{28,12},{1,9},{5... | collective-permute-start | bytes 516104 | tf_op jit(solution)/shard_map/ppermute | solution.py:202
  22.2 0.2 collective-permute-start.8
  22.4 0.0 collective-permute-done.6.refs_5_
  22.4 4.7 %collective-permute-done.7.refs_6_ = bf16[84,1024]{1,0:T(8,128)(2,1)S(1)} collective-permute-done((bf16[84,1024]{1,0:T(8,128)(2,1)S(1)}, bf16[84,1024]{1,0:T(8,128)(2,1)S(1)}, u32[]{:S(2)}, u32[]{:S(2)}) %collective-permute-start.7) | collective-permute-done | bytes 172064 | tf_op jit(solution)/shard_map/ppermute | solution.py:202
  27.1 1.0 %collective-permute-done.8.refs_7_ = bf16[84,1024]{1,0:T(8,128)(2,1)S(1)} collective-permute-done((bf16[84,1024]{1,0:T(8,128)(2,1)S(1)}, bf16[84,1024]{1,0:T(8,128)(2,1)S(1)}, u32[]{:S(2)}, u32[]{:S(2)}) %collective-permute-start.8) | collective-permute-done | bytes 172064 | tf_op jit(solution)/shard_map/ppermute | solution.py:202
  28.1 0.9 %copy-done.2 = bf16[1,1,84,768]{3,2,1,0:T(8,128)(2,1)S(1)} copy-done((bf16[1,1,84,768]{3,2,1,0:T(8,128)(2,1)S(1)}, bf16[1,1,84,768]{3,2,1,0:T(8,128)(2,1)}, u32[]{:S(2)}) %copy-start.2) | copy-done | bytes 129048
  29.0 2.3 %partial.1 = (f32[96,1024]{1,0:T(8,128)S(1)}, bf16[96,1024]{1,0:T(8,128)(2,1)S(1)}, bf16[96,1024]{1,0:T(8,128)(2,1)S(1)}, bf16[96,1024]{1,0:T(8,128)(2,1)S(1)}) custom-call(bf16[84,768]{1,0:T(8,128)(2,1)S(1)} %bitcast.22, bf16[84,768]{1,0:T(8,128)(2,1)S(1)} %collective-permute-done.3.refs_1_, bf16[84,768]{1,0:T(8,128)(2,1)S(1)} %collective-permute-done.4.refs_2_, ...), custom_call_target="tpu_custom_call" | custom-call | tf_op jit(solution)/shard_map/partial/pallas_call | solution.py:171
  31.2 1.6 %collective-permute-start.9 = (bf16[96,1024]{1,0:T(8,128)(2,1)S(1)}, bf16[96,1024]{1,0:T(8,128)(2,1)S(1)}, u32[]{:S(2)}, u32[]{:S(2)}) collective-permute-start(bf16[96,1024]{1,0:T(8,128)(2,1)S(1)} %get-tuple-element.41), channel_id=1, source_target_pairs={{0,16},{4,12},{8,24},{12,4},{16,0},{20,28},{24,8},{28,20},{1,17},{... | collective-permute-start | bytes 589832 | tf_op jit(solution)/shard_map/ppermute | solution.py:202
  32.9 0.0 collective-permute-start.10
  32.9 0.6 %collective-permute-start.11 = (bf16[96,1024]{1,0:T(8,128)(2,1)S(1)}, bf16[96,1024]{1,0:T(8,128)(2,1)S(1)}, u32[]{:S(2)}, u32[]{:S(2)}) collective-permute-start(bf16[96,1024]{1,0:T(8,128)(2,1)S(1)} %get-tuple-element.43), channel_id=1, source_target_pairs={{0,20},{4,8},{8,28},{12,0},{16,4},{20,24},{24,12},{28,16},{1,21},{... | collective-permute-start | bytes 589832 | tf_op jit(solution)/shard_map/ppermute | solution.py:202
  33.5 1.9 %copy-done = bf16[1,768,2048]{2,1,0:T(8,128)(2,1)S(1)} copy-done((bf16[1,768,2048]{2,1,0:T(8,128)(2,1)S(1)}, bf16[1,768,2048]{2,1,0:T(8,128)(2,1)}, u32[]{:S(2)}) %copy-start) | copy-done | bytes 3145752
  35.3 0.9 %copy-done.3 = bf16[1,1,84,768]{3,2,1,0:T(8,128)(2,1)S(1)} copy-done((bf16[1,1,84,768]{3,2,1,0:T(8,128)(2,1)S(1)}, bf16[1,1,84,768]{3,2,1,0:T(8,128)(2,1)}, u32[]{:S(2)}) %copy-start.3) | copy-done | bytes 129048
  36.2 2.3 %hidden.1 = (bf16[84,768]{1,0:T(8,128)(2,1)}, f32[1,128]{1,0:T(1,128)S(1)}) custom-call(bf16[84,2048]{1,0:T(8,128)(2,1)S(1)} %get-tuple-element.32.full_ref, bf16[768,2048]{1,0:T(8,128)(2,1)S(1)} %bitcast.17, bf16[84,768]{1,0:T(8,128)(2,1)S(1)} %bitcast.23), custom_call_target="tpu_custom_call" | custom-call | tf_op jit(solution)/shard_map/hidden/pallas_call | solution.py:126
  38.5 2.6 %collective-permute-start.12 = (f32[1,128]{1,0:T(1,128)S(1)}, f32[1,128]{1,0:T(1,128)S(1)}, u32[]{:S(2)}, u32[]{:S(2)}) collective-permute-start(f32[1,128]{1,0:T(1,128)S(1)} %get-tuple-element.44.refs_0_), channel_id=1, source_target_pairs={{0,1},{1,0},{2,3},{3,2},{4,5},{5,4},{6,7},{7,6},{8,9},{9,8},{10,11... | collective-permute-start | bytes 1544 | tf_op jit(solution)/shard_map/ppermute | solution.py:293
  41.1 1.2 %collective-permute-start.13 = (f32[1,128]{1,0:T(1,128)S(1)}, f32[1,128]{1,0:T(1,128)S(1)}, u32[]{:S(2)}, u32[]{:S(2)}) collective-permute-start(f32[1,128]{1,0:T(1,128)S(1)} %get-tuple-element.44.refs_0_), channel_id=1, source_target_pairs={{0,2},{1,3},{2,0},{3,1},{4,6},{5,7},{6,4},{7,5},{8,10},{9,11},{10,... | collective-permute-start | bytes 1544 | tf_op jit(solution)/shard_map/ppermute | solution.py:293
  42.4 0.3 collective-permute-done.12.refs_1_
  42.7 2.7 %collective-permute-start.14 = (f32[1,128]{1,0:T(1,128)S(1)}, f32[1,128]{1,0:T(1,128)S(1)}, u32[]{:S(2)}, u32[]{:S(2)}) collective-permute-start(f32[1,128]{1,0:T(1,128)S(1)} %get-tuple-element.44.refs_0_), channel_id=1, source_target_pairs={{0,3},{1,2},{2,1},{3,0},{4,7},{5,6},{6,5},{7,4},{8,11},{9,10},{10,... | collective-permute-start | bytes 1544 | tf_op jit(solution)/shard_map/ppermute | solution.py:293
  45.4 0.2 collective-permute-done.13.refs_2_
  45.6 2.4 %collective-permute-done.14.refs_3_ = f32[1,128]{1,0:T(1,128)S(1)} collective-permute-done((f32[1,128]{1,0:T(1,128)S(1)}, f32[1,128]{1,0:T(1,128)S(1)}, u32[]{:S(2)}, u32[]{:S(2)}) %collective-permute-start.14) | collective-permute-done | bytes 544 | tf_op jit(solution)/shard_map/ppermute | solution.py:293
  48.1 0.0 copy-done.5
  48.1 0.0 copy-done.7
  48.1 0.0 copy-done.9
  48.1 1.2 %gate.1 = f32[8,256]{1,0:T(8,128)} custom-call(f32[1,128]{1,0:T(1,128)S(1)} %get-tuple-element.44.refs_0_, f32[1,128]{1,0:T(1,128)S(1)} %collective-permute-done.12.refs_1_, f32[1,128]{1,0:T(1,128)S(1)} %collective-permute-done.13.refs_2_, f32[1,128]{1,0:T(1,128)S(1)} %collective-permute-done.14.refs_3_, s32[8,256]{1,0:T(8,128)S(1)} %bitcast.25, ...), custom_call_target="tpu_custom_call" | custom-call | tf_op jit(solution)/shard_map/gate/pallas_call | solution.py:251
  49.3 0.0 collective-permute-done.9.refs_0_
  49.3 0.0 collective-permute-done.10.refs_1_
  49.3 0.0 collective-permute-done.11.refs_2_
  49.3 1.0 %total.1 = f32[96,2048]{1,0:T(8,128)} custom-call(f32[96,1024]{1,0:T(8,128)S(1)} %get-tuple-element.40.own_ref, bf16[96,1024]{1,0:T(8,128)(2,1)S(1)} %collective-permute-done.9.refs_0_, bf16[96,1024]{1,0:T(8,128)(2,1)S(1)} %collective-permute-done.10.refs_1_, bf16[96,1024]{1,0:T(8,128)(2,1)S(1)} %collective-permute-done.11.refs_2_), custom_call_target="tpu_custom_call" | custom-call | tf_op jit(solution)/shard_map/total/pallas_call | solution.py:222
  (8 shorter events, 0.0 us)
Async XLA Ops:
  0.6 1.2 %copy-start.1 = (bf16[1,256,2048]{2,1,0:T(8,128)(2,1)S(1)}, bf16[1,256,2048]{2,1,0:T(8,128)(2,1)}, u32[]{:S(2)}) copy-start(bf16[1,256,2048]{2,1,0:T(8,128)(2,1)} %param.6) | copy-start | bytes 3145732
  1.9 0.7 %copy-start.4 = (s32[1,256,8]{1,2,0:T(8,128)S(1)}, s32[1,256,8]{1,2,0:T(8,128)}, u32[]{:S(2)}) copy-start(s32[1,256,8]{1,2,0:T(8,128)} %param.8) | copy-start | bytes 24580
  2.6 0.7 %copy-start.6 = (s32[1,256,8]{1,2,0:T(8,128)S(1)}, s32[1,256,8]{1,2,0:T(8,128)}, u32[]{:S(2)}) copy-start(s32[1,256,8]{1,2,0:T(8,128)} %param.9) | copy-start | bytes 24580
  3.3 0.7 %copy-start.8 = (bf16[1,256,8]{1,2,0:T(8,128)(2,1)S(1)}, bf16[1,256,8]{1,2,0:T(8,128)(2,1)}, u32[]{:S(2)}) copy-start(bf16[1,256,8]{1,2,0:T(8,128)(2,1)} %param.7) | copy-start | bytes 12292
  3.9 44.1 %copy-start.5 = (s32[1,256,8]{1,2,0:T(8,128)S(1)}, s32[1,256,8]{1,2,0:T(8,128)}, u32[]{:S(2)}) copy-start(s32[1,256,8]{1,2,0:T(8,128)} %param.8) | copy-start | bytes 24580
  3.9 44.1 %copy-start.7 = (s32[1,256,8]{1,2,0:T(8,128)S(1)}, s32[1,256,8]{1,2,0:T(8,128)}, u32[]{:S(2)}) copy-start(s32[1,256,8]{1,2,0:T(8,128)} %param.9) | copy-start | bytes 24580
  3.9 44.1 %copy-start.9 = (bf16[1,256,8]{1,2,0:T(8,128)(2,1)S(1)}, bf16[1,256,8]{1,2,0:T(8,128)(2,1)}, u32[]{:S(2)}) copy-start(bf16[1,256,8]{1,2,0:T(8,128)(2,1)} %param.7) | copy-start | bytes 12292
  4.9 7.6 %collective-permute-start = (bf16[24,2048]{1,0:T(8,128)(2,1)S(1)}, bf16[24,2048]{1,0:T(8,128)(2,1)S(1)}, u32[]{:S(2)}, u32[]{:S(2)}) collective-permute-start(bf16[24,2048]{1,0:T(8,128)(2,1)S(1)} %get-tuple-element.25), channel_id=1, source_target_pairs={{0,1},{1,0},{2,3},{3,2},{4,5},{5,4},{6,7},{7,6},{8,9},{9,8},{10,11... | collective-permute-start | bytes 294920 | tf_op jit(solution)/shard_map/ppermute | solution.py:275
  8.0 11.9 %collective-permute-start.3 = (bf16[84,768]{1,0:T(8,128)(2,1)}, bf16[84,768]{1,0:T(8,128)(2,1)S(1)}, u32[]{:S(2)}, u32[]{:S(2)}) collective-permute-start(bf16[84,768]{1,0:T(8,128)(2,1)} %bitcast.19), channel_id=1, source_target_pairs={{0,4},{4,0},{8,12},{12,8},{16,20},{20,16},{24,28},{28,24},{1,5},{5... | collective-permute-start | bytes 387080 | tf_op jit(solution)/shard_map/ppermute | solution.py:202
  8.0 11.9 %collective-permute-start.4 = (bf16[84,768]{1,0:T(8,128)(2,1)}, bf16[84,768]{1,0:T(8,128)(2,1)S(1)}, u32[]{:S(2)}, u32[]{:S(2)}) collective-permute-start(bf16[84,768]{1,0:T(8,128)(2,1)} %bitcast.20), channel_id=1, source_target_pairs={{0,8},{4,20},{8,0},{12,28},{16,24},{20,4},{24,16},{28,12},{1,9},{5... | collective-permute-start | bytes 387080 | tf_op jit(solution)/shard_map/ppermute | solution.py:202
  9.5 10.4 %collective-permute-start.5 = (bf16[84,768]{1,0:T(8,128)(2,1)}, bf16[84,768]{1,0:T(8,128)(2,1)S(1)}, u32[]{:S(2)}, u32[]{:S(2)}) collective-permute-start(bf16[84,768]{1,0:T(8,128)(2,1)} %bitcast.21), channel_id=1, source_target_pairs={{0,20},{4,8},{8,28},{12,0},{16,4},{20,24},{24,12},{28,16},{1,21},{... | collective-permute-start | bytes 387080 | tf_op jit(solution)/shard_map/ppermute | solution.py:202
  9.9 10.0 %collective-permute-start.1 = (bf16[24,2048]{1,0:T(8,128)(2,1)S(1)}, bf16[24,2048]{1,0:T(8,128)(2,1)S(1)}, u32[]{:S(2)}, u32[]{:S(2)}) collective-permute-start(bf16[24,2048]{1,0:T(8,128)(2,1)S(1)} %get-tuple-element.26), channel_id=1, source_target_pairs={{0,2},{1,3},{2,0},{3,1},{4,6},{5,7},{6,4},{7,5},{8,10},{9,11},{10,... | collective-permute-start | bytes 294920 | tf_op jit(solution)/shard_map/ppermute | solution.py:275
  12.5 7.4 %collective-permute-start.2 = (bf16[24,2048]{1,0:T(8,128)(2,1)S(1)}, bf16[24,2048]{1,0:T(8,128)(2,1)S(1)}, u32[]{:S(2)}, u32[]{:S(2)}) collective-permute-start(bf16[24,2048]{1,0:T(8,128)(2,1)S(1)} %get-tuple-element.27), channel_id=1, source_target_pairs={{0,3},{1,2},{2,1},{3,0},{4,7},{5,6},{6,5},{7,4},{8,11},{9,10},{10,... | collective-permute-start | bytes 294920 | tf_op jit(solution)/shard_map/ppermute | solution.py:275
  20.5 1.9 %collective-permute-start.6 = (bf16[84,1024]{1,0:T(8,128)(2,1)S(1)}, bf16[84,1024]{1,0:T(8,128)(2,1)S(1)}, u32[]{:S(2)}, u32[]{:S(2)}) collective-permute-start(bf16[84,1024]{1,0:T(8,128)(2,1)S(1)} %get-tuple-element.39), channel_id=1, source_target_pairs={{0,4},{4,0},{8,12},{12,8},{16,20},{20,16},{24,28},{28,24},{1,5},{5... | collective-permute-start | bytes 516104 | tf_op jit(solution)/shard_map/ppermute | solution.py:202
  20.6 6.5 %collective-permute-start.7 = (bf16[84,1024]{1,0:T(8,128)(2,1)S(1)}, bf16[84,1024]{1,0:T(8,128)(2,1)S(1)}, u32[]{:S(2)}, u32[]{:S(2)}) collective-permute-start(bf16[84,1024]{1,0:T(8,128)(2,1)S(1)} %get-tuple-element.38.refs_4_), channel_id=1, source_target_pairs={{0,8},{4,20},{8,0},{12,28},{16,24},{20,4},{24,16},{28,12},{1,9},{5... | collective-permute-start | bytes 516104 | tf_op jit(solution)/shard_map/ppermute | solution.py:202
  22.2 5.9 %collective-permute-start.8 = (bf16[84,1024]{1,0:T(8,128)(2,1)S(1)}, bf16[84,1024]{1,0:T(8,128)(2,1)S(1)}, u32[]{:S(2)}, u32[]{:S(2)}) collective-permute-start(bf16[84,1024]{1,0:T(8,128)(2,1)S(1)} %get-tuple-element.39), channel_id=1, source_target_pairs={{0,20},{4,8},{8,28},{12,0},{16,4},{20,24},{24,12},{28,16},{1,21},{... | collective-permute-start | bytes 516104 | tf_op jit(solution)/shard_map/ppermute | solution.py:202
  28.1 0.9 %copy-start.2 = (bf16[1,1,84,768]{3,2,1,0:T(8,128)(2,1)S(1)}, bf16[1,1,84,768]{3,2,1,0:T(8,128)(2,1)}, u32[]{:S(2)}) copy-start(bf16[1,1,84,768]{3,2,1,0:T(8,128)(2,1)} %param.10) | copy-start | bytes 387076
  31.2 18.1 %collective-permute-start.9 = (bf16[96,1024]{1,0:T(8,128)(2,1)S(1)}, bf16[96,1024]{1,0:T(8,128)(2,1)S(1)}, u32[]{:S(2)}, u32[]{:S(2)}) collective-permute-start(bf16[96,1024]{1,0:T(8,128)(2,1)S(1)} %get-tuple-element.41), channel_id=1, source_target_pairs={{0,16},{4,12},{8,24},{12,4},{16,0},{20,28},{24,8},{28,20},{1,17},{... | collective-permute-start | bytes 589832 | tf_op jit(solution)/shard_map/ppermute | solution.py:202
  32.9 16.4 %collective-permute-start.10 = (bf16[96,1024]{1,0:T(8,128)(2,1)S(1)}, bf16[96,1024]{1,0:T(8,128)(2,1)S(1)}, u32[]{:S(2)}, u32[]{:S(2)}) collective-permute-start(bf16[96,1024]{1,0:T(8,128)(2,1)S(1)} %get-tuple-element.42), channel_id=1, source_target_pairs={{0,4},{4,0},{8,12},{12,8},{16,20},{20,16},{24,28},{28,24},{1,5},{5... | collective-permute-start | bytes 589832 | tf_op jit(solution)/shard_map/ppermute | solution.py:202
  32.9 16.4 %collective-permute-start.11 = (bf16[96,1024]{1,0:T(8,128)(2,1)S(1)}, bf16[96,1024]{1,0:T(8,128)(2,1)S(1)}, u32[]{:S(2)}, u32[]{:S(2)}) collective-permute-start(bf16[96,1024]{1,0:T(8,128)(2,1)S(1)} %get-tuple-element.43), channel_id=1, source_target_pairs={{0,20},{4,8},{8,28},{12,0},{16,4},{20,24},{24,12},{28,16},{1,21},{... | collective-permute-start | bytes 589832 | tf_op jit(solution)/shard_map/ppermute | solution.py:202
  33.4 1.9 %copy-start = (bf16[1,768,2048]{2,1,0:T(8,128)(2,1)S(1)}, bf16[1,768,2048]{2,1,0:T(8,128)(2,1)}, u32[]{:S(2)}) copy-start(bf16[1,768,2048]{2,1,0:T(8,128)(2,1)} %param.11) | copy-start | bytes 9437188
  35.3 0.9 %copy-start.3 = (bf16[1,1,84,768]{3,2,1,0:T(8,128)(2,1)S(1)}, bf16[1,1,84,768]{3,2,1,0:T(8,128)(2,1)}, u32[]{:S(2)}) copy-start(bf16[1,1,84,768]{3,2,1,0:T(8,128)(2,1)} %param.10) | copy-start | bytes 387076
  38.5 4.2 %collective-permute-start.12 = (f32[1,128]{1,0:T(1,128)S(1)}, f32[1,128]{1,0:T(1,128)S(1)}, u32[]{:S(2)}, u32[]{:S(2)}) collective-permute-start(f32[1,128]{1,0:T(1,128)S(1)} %get-tuple-element.44.refs_0_), channel_id=1, source_target_pairs={{0,1},{1,0},{2,3},{3,2},{4,5},{5,4},{6,7},{7,6},{8,9},{9,8},{10,11... | collective-permute-start | bytes 1544 | tf_op jit(solution)/shard_map/ppermute | solution.py:293
  41.1 4.5 %collective-permute-start.13 = (f32[1,128]{1,0:T(1,128)S(1)}, f32[1,128]{1,0:T(1,128)S(1)}, u32[]{:S(2)}, u32[]{:S(2)}) collective-permute-start(f32[1,128]{1,0:T(1,128)S(1)} %get-tuple-element.44.refs_0_), channel_id=1, source_target_pairs={{0,2},{1,3},{2,0},{3,1},{4,6},{5,7},{6,4},{7,5},{8,10},{9,11},{10,... | collective-permute-start | bytes 1544 | tf_op jit(solution)/shard_map/ppermute | solution.py:293
  42.7 5.4 %collective-permute-start.14 = (f32[1,128]{1,0:T(1,128)S(1)}, f32[1,128]{1,0:T(1,128)S(1)}, u32[]{:S(2)}, u32[]{:S(2)}) collective-permute-start(f32[1,128]{1,0:T(1,128)S(1)} %get-tuple-element.44.refs_0_), channel_id=1, source_target_pairs={{0,3},{1,2},{2,1},{3,0},{4,7},{5,6},{6,5},{7,4},{8,11},{9,10},{10,... | collective-permute-start | bytes 1544 | tf_op jit(solution)/shard_map/ppermute | solution.py:293
where the time goes:
time: 50.6 us; the launch traced here: 50.3 us
  starting transfers between devices  20.4 us (40%)
  waiting for transfers between devices  13.9 us (27%)
  Pallas kernels  8.3 us (16%)
  local copies, waits for them, and re-layouts  7.01 us (14%)
  between operations  0.71 us (1%)
    ppermute x3, starting transfers between devices, on_device(): blocks.append(lax.ppermute(sent[k], 'expert', pairs))  7.89 us
    unnamed x20, local copies, waits for them, and re-layouts  7.01 us
    ppermute x3, starting transfers between devices, on_device(): tables.append(lax.ppermute(row_sums, 'expert', pairs))  6.52 us
    ppermute x9, starting transfers between devices, exchange(): return lax.ppermute(value, 'dp', pairs)  5.98 us
    ppermute x9, waiting for transfers between devices, exchange(): return lax.ppermute(value, 'dp', pairs)  5.66 us
    ppermute x3, waiting for transfers between devices, on_device(): blocks.append(lax.ppermute(sent[k], 'expert', pairs))  5.21 us
    ppermute x3, waiting for transfers between devices, on_device(): tables.append(lax.ppermute(row_sums, 'expert', pairs))  3 us
    pallas_call x1, Pallas kernels, hidden_part(): pl.pallas_call(hidden_kernel, grid=(steps,), in_specs=[pl.BlockSpec((slot...  2.29 us
  transfers between devices with their start and end apart: 15, of which 6 were waited for; matrix products, arithmetic and copies ran while one was open for 0% of the time, Pallas kernels for 7%

commit v1 on v0

v1 whole, which is shorter than its diff:
```python
import functools
import math

import jax
import jax.numpy as jnp
from jax import lax
from jax.experimental import pallas as pl
from jax.experimental.pallas import tpu as pltpu
from jax.sharding import PartitionSpec as P


F32 = jnp.float32
BF16 = jnp.bfloat16
LIMIT = 24 * 1024 * 1024


def params(**kw):
    return pltpu.CompilerParams(vmem_limit_bytes=LIMIT, **kw)


def in_hbm(x):
    return pltpu.with_memory_space_constraint(x, pltpu.HBM)


def pad8(n):
    return -(-n // 8) * 8


def matmul_t(a, b, contract):
    return lax.dot_general(a, b, ((contract[:1], contract[1:]), ((), ())), preferred_element_type=F32)


def pack_kernel(experts, padded, pieces, *refs):
    arrays, out_refs = refs[:4], refs[4 : 4 + experts]
    ids_ref, slots_ref, gates_ref, grad_ref, small_sems, grad_sems = refs[4 + experts :]
    small = [
        pltpu.make_async_copy(src, dst, small_sems.at[n])
        for n, (src, dst) in enumerate(zip(arrays[:3], (ids_ref, slots_ref, gates_ref)))
    ]
    for copy in small:
        copy.start()
    width = grad_ref.shape[1] // pieces
    large = []
    for n in range(pieces):
        columns = pl.ds(n * width, width)
        large.append(
            pltpu.make_async_copy(arrays[3].at[:, columns], grad_ref.at[:, columns], grad_sems.at[n])
        )
        large[-1].start()
    for copy in small:
        copy.wait()
    me = lax.axis_index("expert")
    ids = ids_ref[...]
    slots = slots_ref[...]
    gates = gates_ref[...].astype(F32)
    valid = (ids < experts) & (slots >= 0)
    target = jnp.where(valid, (ids ^ me) * padded + slots, -1)
    row = lax.broadcasted_iota(jnp.int32, (experts * padded, ids.shape[1]), 0)
    chosen = jnp.zeros(row.shape, F32)
    for k in range(ids.shape[0]):
        chosen = jnp.where(row == target[k : k + 1, :], gates[k : k + 1, :], chosen)
    chosen = chosen.astype(BF16)
    for n in range(pieces):
        columns = slice(n * width, (n + 1) * width)
        large[n].wait()
        rows = jnp.dot(chosen, grad_ref[:, columns], preferred_element_type=F32)
        for k, out in enumerate(out_refs):
            out[:, columns] = rows[k * padded : (k + 1) * padded, :].astype(BF16)


def pack(ids, slots, gates, grad, experts, padded):
    width = grad.shape[1]
    pieces = 4
    arrays = (ids, slots, gates, grad)
    return pl.pallas_call(
        functools.partial(pack_kernel, experts, padded, pieces),
        in_specs=[pl.BlockSpec(memory_space=pltpu.HBM)] * 4,
        out_specs=[pl.BlockSpec(memory_space=pltpu.VMEM)] * experts,
        out_shape=[jax.ShapeDtypeStruct((padded, width), BF16)] * experts,
        scratch_shapes=[pltpu.VMEM(a.shape, a.dtype) for a in arrays]
        + [pltpu.SemaphoreType.DMA((3,)), pltpu.SemaphoreType.DMA((pieces,))],
        compiler_params=params(),
        name="pack",
    )(*map(in_hbm, arrays))


def join_kernel(experts, capacity, *refs):
    blocks = refs[:experts]
    full_ref, own_ref, other_ref = refs[experts:]
    me = lax.axis_index("expert")
    core = lax.axis_index("dp") % 2
    slots = experts * capacity
    padded = blocks[0].shape[0]
    half = full_ref.shape[1] // 2
    total = jnp.zeros(full_ref.shape, F32)
    for k, block in enumerate(blocks):
        row = lax.broadcasted_iota(jnp.int32, (slots, padded), 0)
        col = lax.broadcasted_iota(jnp.int32, (slots, padded), 1)
        place = (row == (me ^ k) * capacity + col) & (col < capacity)
        total += jnp.dot(place.astype(BF16), block[...], preferred_element_type=F32)
    full_ref[...] = total.astype(BF16)
    own_ref[...] = full_ref[:, pl.ds(pl.multiple_of(core * half, 128), half)]
    other_ref[...] = full_ref[:, pl.ds(pl.multiple_of((1 - core) * half, 128), half)]


def join(blocks, capacity):
    experts = len(blocks)
    slots, width = experts * capacity, blocks[0].shape[1]
    vmem = pl.BlockSpec(memory_space=pltpu.VMEM)
    return pl.pallas_call(
        functools.partial(join_kernel, experts, capacity),
        in_specs=[vmem] * experts,
        out_specs=[vmem] * 3,
        out_shape=[
            jax.ShapeDtypeStruct((slots, width), BF16),
            jax.ShapeDtypeStruct((slots, width // 2), BF16),
            jax.ShapeDtypeStruct((slots, width // 2), BF16),
        ],
        compiler_params=params(),
        name="join",
    )(*blocks)


def load_kernel(weight_hbm, hidden_hbm, weight_ref, hidden_ref, sems):
    copies = [
        pltpu.make_async_copy(weight_hbm, weight_ref, sems.at[0]),
        pltpu.make_async_copy(hidden_hbm, hidden_ref, sems.at[1]),
    ]
    for copy in copies:
        copy.start()
    for copy in copies:
        copy.wait()


def load(weight, hidden):
    return pl.pallas_call(
        load_kernel,
        in_specs=[pl.BlockSpec(memory_space=pltpu.HBM)] * 2,
        out_specs=[pl.BlockSpec(memory_space=pltpu.VMEM)] * 2,
        out_shape=[jax.ShapeDtypeStruct(a.shape, a.dtype) for a in (weight, hidden)],
        scratch_shapes=[pltpu.SemaphoreType.DMA((2,))],
        compiler_params=params(),
        name="load",
    )(in_hbm(weight), in_hbm(hidden))


def stack_kernel(side, count, depth, *refs):
    hiddens, (left_ref, stack_ref, turned_ref) = refs[:count], refs[count:]
    slots = hiddens[0].shape[0]
    for n, hidden in enumerate(hiddens):
        stack_ref[n * depth : n * depth + slots, :] = hidden[...].astype(F32)
        if slots < depth:
            stack_ref[n * depth + slots : (n + 1) * depth, :] = jnp.zeros(
                (depth - slots, stack_ref.shape[1]), F32
            )
    turned_ref[...] = stack_ref[...].T
    index = lax.axis_index("dp")
    masks = owner_masks(side)
    height = left_ref.shape[0] // len(masks)
    for n, mask in enumerate(masks):
        owner = index ^ jnp.where(index % 2 == 0, mask[0], mask[1])
        start = pl.multiple_of(owner * height, 8)
        left_ref[n * height : (n + 1) * height, :] = turned_ref[pl.ds(start, height), :].astype(BF16)


def stack(hiddens, side, depth, height):
    count = len(hiddens)
    units = hiddens[0].shape[1]
    vmem = pl.BlockSpec(memory_space=pltpu.VMEM)
    return pl.pallas_call(
        functools.partial(stack_kernel, side, count, depth),
        in_specs=[vmem] * count,
        out_specs=vmem,
        out_shape=jax.ShapeDtypeStruct((2 * side * height, count * depth), BF16),
        scratch_shapes=[
            pltpu.VMEM((count * depth, units), F32),
            pltpu.VMEM((units, count * depth), F32),
        ],
        compiler_params=params(),
        name="stack",
    )(*hiddens)


def unit_kernel(capacity, full_ref, weight_ref, hidden_ref, grad_ref, *refs):
    tables, sums_ref = refs[:-1], refs[-1]
    me = lax.axis_index("expert")
    unit = matmul_t(full_ref[...], weight_ref[...], (1, 1))
    grad_ref[...] = unit.astype(BF16)
    sums = jnp.sum(unit * hidden_ref[...].astype(F32), axis=1, keepdims=True)
    sums_ref[...] = jnp.zeros_like(sums_ref)
    sums_ref[: sums.shape[0], :] = jnp.broadcast_to(sums, (sums.shape[0], sums_ref.shape[1]))
    for k, table in enumerate(tables):
        table[...] = sums_ref[pl.ds((me ^ k) * capacity, table.shape[0]), :]


def unit_part(full, weight, hidden, experts):
    slots, _ = full.shape
    units = weight.shape[0]
    capacity = slots // experts
    vmem = pl.BlockSpec(memory_space=pltpu.VMEM)
    return pl.pallas_call(
        functools.partial(unit_kernel, capacity),
        in_specs=[vmem] * 3,
        out_specs=[vmem] * (1 + experts),
        out_shape=[jax.ShapeDtypeStruct((slots, units), BF16)]
        + [jax.ShapeDtypeStruct((pad8(capacity), 128), F32)] * experts,
        scratch_shapes=[pltpu.VMEM((pad8(slots) + 8, 128), F32)],
        compiler_params=params(),
        name="unit",
    )(full, weight, hidden)


def partial_kernel(depth, left_ref, *refs):
    masks = (len(refs) - 1) // 2
    rows, outs, right_ref = refs[:masks], refs[masks : 2 * masks], refs[-1]
    slots = rows[0].shape[0]
    for n, row in enumerate(rows):
        right_ref[n * depth : n * depth + slots, :] = row[...]
        if slots < depth:
            right_ref[n * depth + slots : (n + 1) * depth, :] = jnp.zeros(
                (depth - slots, right_ref.shape[1]), BF16
            )
    height = outs[0].shape[0]
    total = jnp.dot(left_ref[...], right_ref[...], preferred_element_type=F32)
    for n, out in enumerate(outs):
        out[...] = total[n * height : (n + 1) * height, :].astype(out.dtype)


def partial(left, rows, depth):
    count = len(rows)
    half = rows[0].shape[1]
    height = left.shape[0] // count
    vmem = pl.BlockSpec(memory_space=pltpu.VMEM)
    return pl.pallas_call(
        functools.partial(partial_kernel, depth),
        in_specs=[vmem] * (1 + count),
        out_specs=[vmem] * count,
        out_shape=[jax.ShapeDtypeStruct((height, half), F32 if n == 0 else BF16) for n in range(count)],
        scratch_shapes=[pltpu.VMEM((count * depth, half), BF16)],
        compiler_params=params(),
        name="partial",
    )(left, *rows)


def gather_masks(side):
    inner = [(d * 2) for d in range(1, side)]
    outer = [(d * side * 2) for d in range(1, side)]
    same = [(i, o) for i, o in zip(inner, outer)]
    cross = [(o ^ 1, i ^ 1) for i, o in zip(inner, outer)]
    return same, cross


def owner_masks(side):
    same = [(d * side * 2, d * 2) for d in range(1, side)]
    cross = [(a ^ 1, b ^ 1) for a, b in same]
    return [(0, 0), (1, 1)] + same + cross


def exchange(value, count, mask):
    pairs = [(i, i ^ mask[i % 2]) for i in range(count)]
    return lax.ppermute(value, "dp", pairs)


def total_kernel(terms, own_ref, *refs):
    own_terms, other_terms, out_ref = refs[:terms], refs[terms:-1], refs[-1]
    core = lax.axis_index("dp") % 2
    half = own_ref.shape[1]
    own = own_ref[...]
    for term in own_terms:
        own += term[...].astype(F32)
    other = other_terms[0][...].astype(F32)
    for term in other_terms[1:]:
        other += term[...].astype(F32)
    out_ref[:, pl.ds(pl.multiple_of(core * half, 128), half)] = own
    out_ref[:, pl.ds(pl.multiple_of((1 - core) * half, 128), half)] = other


def total(own, own_terms, other_terms):
    height, half = own.shape
    vmem = pl.BlockSpec(memory_space=pltpu.VMEM)
    return pl.pallas_call(
        functools.partial(total_kernel, len(own_terms)),
        in_specs=[vmem] * (1 + len(own_terms) + len(other_terms)),
        out_specs=vmem,
        out_shape=jax.ShapeDtypeStruct((height, 2 * half), F32),
        compiler_params=params(),
        name="total",
    )(own, *own_terms, *other_terms)


def gate_kernel(experts, *refs):
    tables = refs[:experts]
    ids_ref, slots_ref, gates_ref, out_ref = refs[experts:]
    me = lax.axis_index("expert")
    padded, lanes = tables[0].shape
    ids = ids_ref[...]
    slots = slots_ref[...]
    gates = gates_ref[...].astype(F32)
    valid = (ids < experts) & (slots >= 0)
    target = jnp.where(valid, (ids ^ me) * padded + slots, -1)
    column = jnp.concatenate([table[...] for table in tables], axis=0)
    row = lax.broadcasted_iota(jnp.int32, column.shape, 0)
    for c in range(0, ids.shape[1], lanes):
        found = [
            jnp.sum(jnp.where(row == target[k : k + 1, c : c + lanes], column, 0.0), axis=0, keepdims=True)
            for k in range(ids.shape[0])
        ]
        out_ref[:, c : c + lanes] = jnp.concatenate(found, axis=0) / gates[:, c : c + lanes]


def gate_part(tables, ids, slots, gates):
    experts = len(tables)
    vmem = pl.BlockSpec(memory_space=pltpu.VMEM)
    return pl.pallas_call(
        functools.partial(gate_kernel, experts),
        in_specs=[vmem] * (experts + 3),
        out_specs=vmem,
        out_shape=jax.ShapeDtypeStruct(ids.shape, F32),
        compiler_params=params(),
        name="gate",
    )(*tables, ids, slots, gates)


def on_device(out_grad, gates, expert_ids, route_slots, saved_hidden, down_weight):
    experts = lax.axis_size("expert")
    replicas = lax.axis_size("dp")
    side = math.isqrt(replicas // 2)
    assert 2 * side * side == replicas
    hidden = saved_hidden[0, 0]
    weight = down_weight[0]
    capacity = hidden.shape[0] // experts
    ids, slots, gate = expert_ids[0].T, route_slots[0].T, gates[0].T

    sent = pack(ids, slots, gate, out_grad[0], experts, pad8(capacity))
    blocks = [sent[0]]
    for k in range(1, experts):
        pairs = [(i, i ^ k) for i in range(experts)]
        blocks.append(lax.ppermute(sent[k], "expert", pairs))

    same, cross = gather_masks(side)
    routes = [(1, 1)] + same + cross
    moved_hiddens = []
    for mask in routes:
        moved_hiddens.append(exchange(hidden, replicas, mask))

    depth = -(-hidden.shape[0] // 32) * 32
    height = hidden.shape[1] // replicas
    weight, hidden = load(weight, hidden)
    left = stack([hidden] + moved_hiddens, side, depth, height)
    full, own, other = join(blocks, capacity)
    rows = [own]
    for mask in routes:
        rows.append(exchange(own if mask in same else other, replicas, mask))

    hidden_grad, *sums = unit_part(full, weight, hidden, experts)
    tables = [sums[0]]
    for k in range(1, experts):
        pairs = [(i, i ^ k) for i in range(experts)]
        tables.append(lax.ppermute(sums[k], "expert", pairs))

    cut = partial(left, rows, depth)
    moved = []
    for n, mask in enumerate(owner_masks(side)[1:]):
        moved.append(exchange(cut[n + 1], replicas, mask))
    weight_grad = total(cut[0], moved[1:side], [moved[0]] + moved[side:])

    gate_grad = gate_part(tables, ids, slots, gate)
    return hidden_grad[None, None], weight_grad[None], gate_grad.T[None]


def solution(mesh):
    in_specs = (
        P("dp", "expert", None),
        P("dp", "expert", None),
        P("dp", "expert", None),
        P("dp", "expert", None),
        P("dp", "expert", None, None),
        P("expert", None, None),
    )
    out_specs = (P("dp", "expert", None, None), P("expert", "dp", None), P("dp", "expert", None))
    return jax.shard_map(
        on_device, mesh=mesh, in_specs=in_specs, out_specs=out_specs, check_vma=False
    )
```

time: 50.6 us -> 43 us (0.85)
  local copies, waits for them, and re-layouts: 7.01 us -> 0.02 us
  starting transfers between devices: 20.4 us -> 17 us
  waiting for transfers between devices: 13.9 us -> 16.4 us
    unnamed x20 -> x6, local copies, waits for them, and re-layouts: 7.01 us -> 0.02 us
    ppermute x3, waiting for transfers between devices: 5.21 us -> 7.83 us  [on_device(): blocks.append(lax.ppermute(sent[k], 'expert', pairs))]
    ppermute x3, starting transfers between devices: 7.89 us -> 5.71 us  [on_device(): blocks.append(lax.ppermute(sent[k], 'expert', pairs))]
    ppermute x3, starting transfers between devices: 6.52 us -> 5.5 us  [on_device(): tables.append(lax.ppermute(sums[k], 'expert', pairs))]
    ppermute x9, waiting for transfers between devices: 5.66 us -> 4.89 us  [exchange(): return lax.ppermute(value, 'dp', pairs)]
    ppermute x3, waiting for transfers between devices: 3 us -> 3.69 us  [on_device(): tables.append(lax.ppermute(sums[k], 'expert', pairs))]
    pallas_call x4 -> x6, Pallas kernels: 6.76 us -> 7.09 us  [the longest x1 1.91 us: load(): pl.pallas_call(load_kernel, in_specs=[pl.BlockSpec(memory_space=pltpu.HBM...]
  transfers between devices with their start and end apart: 15 -> 15, of which waited for: 6 -> 6; matrix products, arithmetic and copies ran while one was open for 0% -> 0% of each run, Pallas kernels for 7% -> 12%
where the time goes in v1:
time: 43 us; the launch traced here: 42.8 us
  starting transfers between devices  17 us (40%)
  waiting for transfers between devices  16.4 us (38%)
  Pallas kernels  8.63 us (20%)
  between operations  0.75 us (2%)
    ppermute x3, waiting for transfers between devices, on_device(): blocks.append(lax.ppermute(sent[k], 'expert', pairs))  7.83 us
    ppermute x9, starting transfers between devices, exchange(): return lax.ppermute(value, 'dp', pairs)  5.83 us
    ppermute x3, starting transfers between devices, on_device(): blocks.append(lax.ppermute(sent[k], 'expert', pairs))  5.71 us
    ppermute x3, starting transfers between devices, on_device(): tables.append(lax.ppermute(sums[k], 'expert', pairs))  5.5 us
    ppermute x9, waiting for transfers between devices, exchange(): return lax.ppermute(value, 'dp', pairs)  4.89 us
    ppermute x3, waiting for transfers between devices, on_device(): tables.append(lax.ppermute(sums[k], 'expert', pairs))  3.69 us
    pallas_call x1, Pallas kernels, load(): pl.pallas_call(load_kernel, in_specs=[pl.BlockSpec(memory_space=pltpu.HBM...  1.91 us
    pallas_call x1, Pallas kernels, pack(): pl.pallas_call(functools.partial(pack_kernel, experts, padded, pieces), i...  1.87 us
  transfers between devices with their start and end apart: 15, of which 6 were waited for; matrix products, arithmetic and copies ran while one was open for 0% of the time, Pallas kernels for 12%

profile of v1, /device:TPU:0, one launch (start us, length us, event | category | flops | bytes accessed | tf_op | source)
XLA Modules:
  0.0 42.8 jit_solution(5894041276851872861)
XLA Ops:
  0.6 1.9 %pack.1 = (bf16[24,2048]{1,0:T(8,128)(2,1)S(1)}, bf16[24,2048]{1,0:T(8,128)(2,1)S(1)}, bf16[24,2048]{1,0:T(8,128)(2,1)S(1)}, bf16[24,2048]{1,0:T(8,128)(2,1)S(1)}) custom-call(s32[8,256]{1,0:T(8,128)} %bitcast.17, s32[8,256]{1,0:T(8,128)} %bitcast.19, bf16[8,256]{1,0:T(8,128)(2,1)} %bitcast.21, bf16[256,2048]{1,0:T(8,128)(2,1)} %bitcast.24), custom_call_target="tpu_custom_call" | custom-call | tf_op jit(solution)/shard_map/pack/pallas_call | solution.py:75
  2.5 3.1 %collective-permute-start = (bf16[24,2048]{1,0:T(8,128)(2,1)S(1)}, bf16[24,2048]{1,0:T(8,128)(2,1)S(1)}, u32[]{:S(2)}, u32[]{:S(2)}) collective-permute-start(bf16[24,2048]{1,0:T(8,128)(2,1)S(1)} %get-tuple-element.22), channel_id=1, source_target_pairs={{0,1},{1,0},{2,3},{3,2},{4,5},{5,4},{6,7},{7,6},{8,9},{9,8},{10,11... | collective-permute-start | bytes 294920 | tf_op jit(solution)/shard_map/ppermute | solution.py:338
  5.6 2.6 %collective-permute-start.1 = (bf16[24,2048]{1,0:T(8,128)(2,1)S(1)}, bf16[24,2048]{1,0:T(8,128)(2,1)S(1)}, u32[]{:S(2)}, u32[]{:S(2)}) collective-permute-start(bf16[24,2048]{1,0:T(8,128)(2,1)S(1)} %get-tuple-element.23), channel_id=1, source_target_pairs={{0,2},{1,3},{2,0},{3,1},{4,6},{5,7},{6,4},{7,5},{8,10},{9,11},{10,... | collective-permute-start | bytes 294920 | tf_op jit(solution)/shard_map/ppermute | solution.py:338
  8.2 0.0 collective-permute-start.2
  8.2 0.0 collective-permute-start.3
  8.2 0.2 collective-permute-done.refs_1_
  8.4 7.6 %collective-permute-done.1.refs_2_ = bf16[24,2048]{1,0:T(8,128)(2,1)S(1)} collective-permute-done((bf16[24,2048]{1,0:T(8,128)(2,1)S(1)}, bf16[24,2048]{1,0:T(8,128)(2,1)S(1)}, u32[]{:S(2)}, u32[]{:S(2)}) %collective-permute-start.1) | collective-permute-done | bytes 98336 | tf_op jit(solution)/shard_map/ppermute | solution.py:338
  16.1 0.0 collective-permute-done.2.refs_3_
  16.1 0.6 %join.1 = (bf16[84,2048]{1,0:T(8,128)(2,1)S(1)}, bf16[84,1024]{1,0:T(8,128)(2,1)S(1)}, bf16[84,1024]{1,0:T(8,128)(2,1)S(1)}) custom-call(bf16[24,2048]{1,0:T(8,128)(2,1)S(1)} %get-tuple-element.21.refs_0_, bf16[24,2048]{1,0:T(8,128)(2,1)S(1)} %collective-permute-done.refs_1_, bf16[24,2048]{1,0:T(8,128)(2,1)S(1)} %collective-permute-done.1.refs_2_, ...), custom_call_target="tpu_custom_call" | custom-call | tf_op jit(solution)/shard_map/join/pallas_call | solution.py:110
  16.6 0.1 collective-permute-start.6
  16.7 1.6 %collective-permute-start.7 = (bf16[84,1024]{1,0:T(8,128)(2,1)S(1)}, bf16[84,1024]{1,0:T(8,128)(2,1)S(1)}, u32[]{:S(2)}, u32[]{:S(2)}) collective-permute-start(bf16[84,1024]{1,0:T(8,128)(2,1)S(1)} %get-tuple-element.29.refs_0_), channel_id=1, source_target_pairs={{0,8},{4,20},{8,0},{12,28},{16,24},{20,4},{24,16},{28,12},{1,9},{5... | collective-permute-start | bytes 516104 | tf_op jit(solution)/shard_map/ppermute | solution.py:261
  18.3 0.3 collective-permute-start.8
  18.6 1.5 %collective-permute-start.4 = (bf16[84,768]{1,0:T(8,128)(2,1)}, bf16[84,768]{1,0:T(8,128)(2,1)S(1)}, u32[]{:S(2)}, u32[]{:S(2)}) collective-permute-start(bf16[84,768]{1,0:T(8,128)(2,1)} %bitcast.27), channel_id=1, source_target_pairs={{0,8},{4,20},{8,0},{12,28},{16,24},{20,4},{24,16},{28,12},{1,9},{5... | collective-permute-start | bytes 387080 | tf_op jit(solution)/shard_map/ppermute | solution.py:261
  20.0 0.0 collective-permute-done.3.refs_1_
  20.1 0.2 collective-permute-start.5
  20.3 1.9 %load.1 = (bf16[768,2048]{1,0:T(8,128)(2,1)S(1)}, bf16[84,768]{1,0:T(8,128)(2,1)S(1)}) custom-call(bf16[768,2048]{1,0:T(8,128)(2,1)} %bitcast.23, bf16[84,768]{1,0:T(8,128)(2,1)} %bitcast.29), custom_call_target="tpu_custom_call" | custom-call | tf_op jit(solution)/shard_map/load/pallas_call | solution.py:136
  22.2 0.0 copy-start
  22.2 0.0 copy-start.1
  22.2 0.0 copy-start.2
  22.2 4.0 %collective-permute-done.4.refs_2_ = bf16[84,768]{1,0:T(8,128)(2,1)S(1)} collective-permute-done((bf16[84,768]{1,0:T(8,128)(2,1)}, bf16[84,768]{1,0:T(8,128)(2,1)S(1)}, u32[]{:S(2)}, u32[]{:S(2)}) %collective-permute-start.4) | collective-permute-done | bytes 129056 | tf_op jit(solution)/shard_map/ppermute | solution.py:261
  26.2 0.9 %collective-permute-done.5.refs_3_ = bf16[84,768]{1,0:T(8,128)(2,1)S(1)} collective-permute-done((bf16[84,768]{1,0:T(8,128)(2,1)}, bf16[84,768]{1,0:T(8,128)(2,1)S(1)}, u32[]{:S(2)}, u32[]{:S(2)}) %collective-permute-start.5) | collective-permute-done | bytes 129056 | tf_op jit(solution)/shard_map/ppermute | solution.py:261
  27.1 0.3 stack.1.left_ref
  27.4 0.0 collective-permute-done.6.refs_1_
  27.4 0.0 collective-permute-done.7.refs_2_
  27.4 0.0 collective-permute-done.8.refs_3_
  27.4 0.6 %partial.1 = (f32[96,1024]{1,0:T(8,128)S(1)}, bf16[96,1024]{1,0:T(8,128)(2,1)S(1)}, bf16[96,1024]{1,0:T(8,128)(2,1)S(1)}, bf16[96,1024]{1,0:T(8,128)(2,1)S(1)}) custom-call(bf16[384,384]{1,0:T(8,128)(2,1)S(1)} %stack.1.left_ref, bf16[84,1024]{1,0:T(8,128)(2,1)S(1)} %get-tuple-element.29.refs_0_, bf16[84,1024]{1,0:T(8,128)(2,1)S(1)} %collective-permute-done.6.refs_1_, ...), custom_call_target="tpu_custom_call" | custom-call | tf_op jit(solution)/shard_map/partial/pallas_call | solution.py:234
  28.0 0.1 collective-permute-start.10
  28.1 1.6 %collective-permute-start.11 = (bf16[96,1024]{1,0:T(8,128)(2,1)S(1)}, bf16[96,1024]{1,0:T(8,128)(2,1)S(1)}, u32[]{:S(2)}, u32[]{:S(2)}) collective-permute-start(bf16[96,1024]{1,0:T(8,128)(2,1)S(1)} %get-tuple-element.34), channel_id=1, source_target_pairs={{0,20},{4,8},{8,28},{12,0},{16,4},{20,24},{24,12},{28,16},{1,21},{... | collective-permute-start | bytes 589832 | tf_op jit(solution)/shard_map/ppermute | solution.py:261
  29.7 0.5 %collective-permute-start.9 = (bf16[96,1024]{1,0:T(8,128)(2,1)S(1)}, bf16[96,1024]{1,0:T(8,128)(2,1)S(1)}, u32[]{:S(2)}, u32[]{:S(2)}) collective-permute-start(bf16[96,1024]{1,0:T(8,128)(2,1)S(1)} %get-tuple-element.32), channel_id=1, source_target_pairs={{0,16},{4,12},{8,24},{12,4},{16,0},{20,28},{24,8},{28,20},{1,17},{... | collective-permute-start | bytes 589832 | tf_op jit(solution)/shard_map/ppermute | solution.py:261
  30.2 1.7 %unit.1 = (bf16[84,768]{1,0:T(8,128)(2,1)}, f32[24,128]{1,0:T(8,128)S(1)}, f32[24,128]{1,0:T(8,128)S(1)}, f32[24,128]{1,0:T(8,128)S(1)}, f32[24,128]{1,0:T(8,128)S(1)}) custom-call(bf16[84,2048]{1,0:T(8,128)(2,1)S(1)} %get-tuple-element.25.full_ref, bf16[768,2048]{1,0:T(8,128)(2,1)S(1)} %get-tuple-element.26.weight_ref, ...), custom_call_target="tpu_custom_call" | custom-call | tf_op jit(solution)/shard_map/unit/pallas_call | solution.py:201
  31.9 1.6 %collective-permute-start.12 = (f32[24,128]{1,0:T(8,128)S(1)}, f32[24,128]{1,0:T(8,128)S(1)}, u32[]{:S(2)}, u32[]{:S(2)}) collective-permute-start(f32[24,128]{1,0:T(8,128)S(1)} %get-tuple-element.36), channel_id=1, source_target_pairs={{0,1},{1,0},{2,3},{3,2},{4,5},{5,4},{6,7},{7,6},{8,9},{9,8},{10,11... | collective-permute-start | bytes 36872 | tf_op jit(solution)/shard_map/ppermute | solution.py:359
  33.6 1.4 %collective-permute-start.13 = (f32[24,128]{1,0:T(8,128)S(1)}, f32[24,128]{1,0:T(8,128)S(1)}, u32[]{:S(2)}, u32[]{:S(2)}) collective-permute-start(f32[24,128]{1,0:T(8,128)S(1)} %get-tuple-element.37), channel_id=1, source_target_pairs={{0,2},{1,3},{2,0},{3,1},{4,6},{5,7},{6,4},{7,5},{8,10},{9,11},{10,... | collective-permute-start | bytes 36872 | tf_op jit(solution)/shard_map/ppermute | solution.py:359
  35.0 0.7 %collective-permute-done.12.refs_1_ = f32[24,128]{1,0:T(8,128)S(1)} collective-permute-done((f32[24,128]{1,0:T(8,128)S(1)}, f32[24,128]{1,0:T(8,128)S(1)}, u32[]{:S(2)}, u32[]{:S(2)}) %collective-permute-start.12) | collective-permute-done | bytes 12320 | tf_op jit(solution)/shard_map/ppermute | solution.py:359
  35.6 2.5 %collective-permute-start.14 = (f32[24,128]{1,0:T(8,128)S(1)}, f32[24,128]{1,0:T(8,128)S(1)}, u32[]{:S(2)}, u32[]{:S(2)}) collective-permute-start(f32[24,128]{1,0:T(8,128)S(1)} %get-tuple-element.38), channel_id=1, source_target_pairs={{0,3},{1,2},{2,1},{3,0},{4,7},{5,6},{6,5},{7,4},{8,11},{9,10},{10,... | collective-permute-start | bytes 36872 | tf_op jit(solution)/shard_map/ppermute | solution.py:359
  38.1 0.0 collective-permute-done.13.refs_2_
  38.2 3.0 %collective-permute-done.14.refs_3_ = f32[24,128]{1,0:T(8,128)S(1)} collective-permute-done((f32[24,128]{1,0:T(8,128)S(1)}, f32[24,128]{1,0:T(8,128)S(1)}, u32[]{:S(2)}, u32[]{:S(2)}) %collective-permute-start.14) | collective-permute-done | bytes 12320 | tf_op jit(solution)/shard_map/ppermute | solution.py:359
  41.1 0.0 copy-done
  41.1 0.0 copy-done.1
  41.1 0.0 copy-done.2
  41.1 0.7 %gate.1 = f32[8,256]{1,0:T(8,128)} custom-call(f32[24,128]{1,0:T(8,128)S(1)} %get-tuple-element.35.refs_0_, f32[24,128]{1,0:T(8,128)S(1)} %collective-permute-done.12.refs_1_, f32[24,128]{1,0:T(8,128)S(1)} %collective-permute-done.13.refs_2_, f32[24,128]{1,0:T(8,128)S(1)} %collective-permute-done.14.refs_3_, s32[8,256]{1,0:T(8,128)S(1)} %bitcast.18, ...), custom_call_target="tpu_custom_call" | custom-call | tf_op jit(solution)/shard_map/gate/pallas_call | solution.py:314
  41.9 0.0 collective-permute-done.10.refs_1_
  41.9 0.0 collective-permute-done.11.refs_2_
  41.9 0.0 collective-permute-done.9.refs_0_
  41.9 1.0 %total.1 = f32[96,2048]{1,0:T(8,128)} custom-call(f32[96,1024]{1,0:T(8,128)S(1)} %get-tuple-element.31.own_ref, bf16[96,1024]{1,0:T(8,128)(2,1)S(1)} %collective-permute-done.9.refs_0_, bf16[96,1024]{1,0:T(8,128)(2,1)S(1)} %collective-permute-done.10.refs_1_, bf16[96,1024]{1,0:T(8,128)(2,1)S(1)} %collective-permute-done.11.refs_2_), custom_call_target="tpu_custom_call" | custom-call | tf_op jit(solution)/shard_map/total/pallas_call | solution.py:281
Async XLA Ops:
  2.5 5.9 %collective-permute-start = (bf16[24,2048]{1,0:T(8,128)(2,1)S(1)}, bf16[24,2048]{1,0:T(8,128)(2,1)S(1)}, u32[]{:S(2)}, u32[]{:S(2)}) collective-permute-start(bf16[24,2048]{1,0:T(8,128)(2,1)S(1)} %get-tuple-element.22), channel_id=1, source_target_pairs={{0,1},{1,0},{2,3},{3,2},{4,5},{5,4},{6,7},{7,6},{8,9},{9,8},{10,11... | collective-permute-start | bytes 294920 | tf_op jit(solution)/shard_map/ppermute | solution.py:338
  5.6 10.4 %collective-permute-start.1 = (bf16[24,2048]{1,0:T(8,128)(2,1)S(1)}, bf16[24,2048]{1,0:T(8,128)(2,1)S(1)}, u32[]{:S(2)}, u32[]{:S(2)}) collective-permute-start(bf16[24,2048]{1,0:T(8,128)(2,1)S(1)} %get-tuple-element.23), channel_id=1, source_target_pairs={{0,2},{1,3},{2,0},{3,1},{4,6},{5,7},{6,4},{7,5},{8,10},{9,11},{10,... | collective-permute-start | bytes 294920 | tf_op jit(solution)/shard_map/ppermute | solution.py:338
  8.2 7.8 %collective-permute-start.2 = (bf16[24,2048]{1,0:T(8,128)(2,1)S(1)}, bf16[24,2048]{1,0:T(8,128)(2,1)S(1)}, u32[]{:S(2)}, u32[]{:S(2)}) collective-permute-start(bf16[24,2048]{1,0:T(8,128)(2,1)S(1)} %get-tuple-element.24), channel_id=1, source_target_pairs={{0,3},{1,2},{2,1},{3,0},{4,7},{5,6},{6,5},{7,4},{8,11},{9,10},{10,... | collective-permute-start | bytes 294920 | tf_op jit(solution)/shard_map/ppermute | solution.py:338
  8.2 11.8 %collective-permute-start.3 = (bf16[84,768]{1,0:T(8,128)(2,1)}, bf16[84,768]{1,0:T(8,128)(2,1)S(1)}, u32[]{:S(2)}, u32[]{:S(2)}) collective-permute-start(bf16[84,768]{1,0:T(8,128)(2,1)} %bitcast.26), channel_id=1, source_target_pairs={{0,4},{4,0},{8,12},{12,8},{16,20},{20,16},{24,28},{28,24},{1,5},{5... | collective-permute-start | bytes 387080 | tf_op jit(solution)/shard_map/ppermute | solution.py:261
  16.6 10.7 %collective-permute-start.6 = (bf16[84,1024]{1,0:T(8,128)(2,1)S(1)}, bf16[84,1024]{1,0:T(8,128)(2,1)S(1)}, u32[]{:S(2)}, u32[]{:S(2)}) collective-permute-start(bf16[84,1024]{1,0:T(8,128)(2,1)S(1)} %get-tuple-element.30), channel_id=1, source_target_pairs={{0,4},{4,0},{8,12},{12,8},{16,20},{20,16},{24,28},{28,24},{1,5},{5... | collective-permute-start | bytes 516104 | tf_op jit(solution)/shard_map/ppermute | solution.py:261
  16.7 10.7 %collective-permute-start.7 = (bf16[84,1024]{1,0:T(8,128)(2,1)S(1)}, bf16[84,1024]{1,0:T(8,128)(2,1)S(1)}, u32[]{:S(2)}, u32[]{:S(2)}) collective-permute-start(bf16[84,1024]{1,0:T(8,128)(2,1)S(1)} %get-tuple-element.29.refs_0_), channel_id=1, source_target_pairs={{0,8},{4,20},{8,0},{12,28},{16,24},{20,4},{24,16},{28,12},{1,9},{5... | collective-permute-start | bytes 516104 | tf_op jit(solution)/shard_map/ppermute | solution.py:261
  18.3 9.1 %collective-permute-start.8 = (bf16[84,1024]{1,0:T(8,128)(2,1)S(1)}, bf16[84,1024]{1,0:T(8,128)(2,1)S(1)}, u32[]{:S(2)}, u32[]{:S(2)}) collective-permute-start(bf16[84,1024]{1,0:T(8,128)(2,1)S(1)} %get-tuple-element.30), channel_id=1, source_target_pairs={{0,20},{4,8},{8,28},{12,0},{16,4},{20,24},{24,12},{28,16},{1,21},{... | collective-permute-start | bytes 516104 | tf_op jit(solution)/shard_map/ppermute | solution.py:261
  18.6 7.6 %collective-permute-start.4 = (bf16[84,768]{1,0:T(8,128)(2,1)}, bf16[84,768]{1,0:T(8,128)(2,1)S(1)}, u32[]{:S(2)}, u32[]{:S(2)}) collective-permute-start(bf16[84,768]{1,0:T(8,128)(2,1)} %bitcast.27), channel_id=1, source_target_pairs={{0,8},{4,20},{8,0},{12,28},{16,24},{20,4},{24,16},{28,12},{1,9},{5... | collective-permute-start | bytes 387080 | tf_op jit(solution)/shard_map/ppermute | solution.py:261
  20.1 7.0 %collective-permute-start.5 = (bf16[84,768]{1,0:T(8,128)(2,1)}, bf16[84,768]{1,0:T(8,128)(2,1)S(1)}, u32[]{:S(2)}, u32[]{:S(2)}) collective-permute-start(bf16[84,768]{1,0:T(8,128)(2,1)} %bitcast.28), channel_id=1, source_target_pairs={{0,20},{4,8},{8,28},{12,0},{16,4},{20,24},{24,12},{28,16},{1,21},{... | collective-permute-start | bytes 387080 | tf_op jit(solution)/shard_map/ppermute | solution.py:261
  22.2 18.9 %copy-start = (s32[1,256,8]{1,2,0:T(8,128)S(1)}, s32[1,256,8]{1,2,0:T(8,128)}, u32[]{:S(2)}) copy-start(s32[1,256,8]{1,2,0:T(8,128)} %param.8) | copy-start | bytes 24580
  22.2 18.9 %copy-start.1 = (s32[1,256,8]{1,2,0:T(8,128)S(1)}, s32[1,256,8]{1,2,0:T(8,128)}, u32[]{:S(2)}) copy-start(s32[1,256,8]{1,2,0:T(8,128)} %param.9) | copy-start | bytes 24580
  22.2 18.9 %copy-start.2 = (bf16[1,256,8]{1,2,0:T(8,128)(2,1)S(1)}, bf16[1,256,8]{1,2,0:T(8,128)(2,1)}, u32[]{:S(2)}) copy-start(bf16[1,256,8]{1,2,0:T(8,128)(2,1)} %param.7) | copy-start | bytes 12292
  28.0 13.9 %collective-permute-start.10 = (bf16[96,1024]{1,0:T(8,128)(2,1)S(1)}, bf16[96,1024]{1,0:T(8,128)(2,1)S(1)}, u32[]{:S(2)}, u32[]{:S(2)}) collective-permute-start(bf16[96,1024]{1,0:T(8,128)(2,1)S(1)} %get-tuple-element.33), channel_id=1, source_target_pairs={{0,4},{4,0},{8,12},{12,8},{16,20},{20,16},{24,28},{28,24},{1,5},{5... | collective-permute-start | bytes 589832 | tf_op jit(solution)/shard_map/ppermute | solution.py:261
  28.1 13.8 %collective-permute-start.11 = (bf16[96,1024]{1,0:T(8,128)(2,1)S(1)}, bf16[96,1024]{1,0:T(8,128)(2,1)S(1)}, u32[]{:S(2)}, u32[]{:S(2)}) collective-permute-start(bf16[96,1024]{1,0:T(8,128)(2,1)S(1)} %get-tuple-element.34), channel_id=1, source_target_pairs={{0,20},{4,8},{8,28},{12,0},{16,4},{20,24},{24,12},{28,16},{1,21},{... | collective-permute-start | bytes 589832 | tf_op jit(solution)/shard_map/ppermute | solution.py:261
  29.7 12.2 %collective-permute-start.9 = (bf16[96,1024]{1,0:T(8,128)(2,1)S(1)}, bf16[96,1024]{1,0:T(8,128)(2,1)S(1)}, u32[]{:S(2)}, u32[]{:S(2)}) collective-permute-start(bf16[96,1024]{1,0:T(8,128)(2,1)S(1)} %get-tuple-element.32), channel_id=1, source_target_pairs={{0,16},{4,12},{8,24},{12,4},{16,0},{20,28},{24,8},{28,20},{1,17},{... | collective-permute-start | bytes 589832 | tf_op jit(solution)/shard_map/ppermute | solution.py:261
  31.9 3.7 %collective-permute-start.12 = (f32[24,128]{1,0:T(8,128)S(1)}, f32[24,128]{1,0:T(8,128)S(1)}, u32[]{:S(2)}, u32[]{:S(2)}) collective-permute-start(f32[24,128]{1,0:T(8,128)S(1)} %get-tuple-element.36), channel_id=1, source_target_pairs={{0,1},{1,0},{2,3},{3,2},{4,5},{5,4},{6,7},{7,6},{8,9},{9,8},{10,11... | collective-permute-start | bytes 36872 | tf_op jit(solution)/shard_map/ppermute | solution.py:359
  33.6 4.6 %collective-permute-start.13 = (f32[24,128]{1,0:T(8,128)S(1)}, f32[24,128]{1,0:T(8,128)S(1)}, u32[]{:S(2)}, u32[]{:S(2)}) collective-permute-start(f32[24,128]{1,0:T(8,128)S(1)} %get-tuple-element.37), channel_id=1, source_target_pairs={{0,2},{1,3},{2,0},{3,1},{4,6},{5,7},{6,4},{7,5},{8,10},{9,11},{10,... | collective-permute-start | bytes 36872 | tf_op jit(solution)/shard_map/ppermute | solution.py:359
  35.6 5.5 %collective-permute-start.14 = (f32[24,128]{1,0:T(8,128)S(1)}, f32[24,128]{1,0:T(8,128)S(1)}, u32[]{:S(2)}, u32[]{:S(2)}) collective-permute-start(f32[24,128]{1,0:T(8,128)S(1)} %get-tuple-element.38), channel_id=1, source_target_pairs={{0,3},{1,2},{2,1},{3,0},{4,7},{5,6},{6,5},{7,4},{8,11},{9,10},{10,... | collective-permute-start | bytes 36872 | tf_op jit(solution)/shard_map/ppermute | solution.py:359

commit v2 on v1

--- a/solution.py
+++ b/solution.py
@@ -84,38 +84,41 @@
     )(*map(in_hbm, arrays))
 
 
-def join_kernel(experts, capacity, *refs):
-    blocks = refs[:experts]
-    full_ref, own_ref, other_ref = refs[experts:]
+def rows_of(block, row_of_first, rows, capacity):
+    padded = block.shape[0]
+    row = lax.broadcasted_iota(jnp.int32, (rows, padded), 0)
+    col = lax.broadcasted_iota(jnp.int32, (rows, padded), 1)
+    place = (row == row_of_first + col) & (col < capacity)
+    return jnp.dot(place.astype(BF16), block[...], preferred_element_type=F32)
+
+
+def store_halves(rows, part_ref, own_ref, other_ref):
+    core = lax.axis_index("dp") % 2
+    half = own_ref.shape[1]
+    part_ref[...] = rows.astype(BF16)
+    own_ref[...] = part_ref[:, pl.ds(pl.multiple_of(core * half, 128), half)]
+    other_ref[...] = part_ref[:, pl.ds(pl.multiple_of((1 - core) * half, 128), half)]
+
+
+def join_kernel(first, capacity, *refs):
+    count = len(refs) - 3
     me = lax.axis_index("expert")
-    core = lax.axis_index("dp") % 2
-    slots = experts * capacity
-    padded = blocks[0].shape[0]
-    half = full_ref.shape[1] // 2
-    total = jnp.zeros(full_ref.shape, F32)
-    for k, block in enumerate(blocks):
-        row = lax.broadcasted_iota(jnp.int32, (slots, padded), 0)
-        col = lax.broadcasted_iota(jnp.int32, (slots, padded), 1)
-        place = (row == (me ^ k) * capacity + col) & (col < capacity)
-        total += jnp.dot(place.astype(BF16), block[...], preferred_element_type=F32)
-    full_ref[...] = total.astype(BF16)
-    own_ref[...] = full_ref[:, pl.ds(pl.multiple_of(core * half, 128), half)]
-    other_ref[...] = full_ref[:, pl.ds(pl.multiple_of((1 - core) * half, 128), half)]
-
-
-def join(blocks, capacity):
-    experts = len(blocks)
-    slots, width = experts * capacity, blocks[0].shape[1]
-    vmem = pl.BlockSpec(memory_space=pltpu.VMEM)
-    return pl.pallas_call(
-        functools.partial(join_kernel, experts, capacity),
-        in_specs=[vmem] * experts,
+    part_ref, own_ref, other_ref = refs[count:]
+    rows = part_ref.shape[0]
+    total = jnp.zeros(part_ref.shape, F32)
+    for k, block in enumerate(refs[:count]):
+        total += rows_of(block, ((me ^ (first + k)) % count) * capacity, rows, capacity)
+    store_halves(total, part_ref, own_ref, other_ref)
+
+
+def join(blocks, first, capacity):
+    rows, width = len(blocks) * capacity, blocks[0].shape[1]
+    vmem = pl.BlockSpec(memory_space=pltpu.VMEM)
+    return pl.pallas_call(
+        functools.partial(join_kernel, first, capacity),
+        in_specs=[vmem] * len(blocks),
         out_specs=[vmem] * 3,
-        out_shape=[
-            jax.ShapeDtypeStruct((slots, width), BF16),
-            jax.ShapeDtypeStruct((slots, width // 2), BF16),
-            jax.ShapeDtypeStruct((slots, width // 2), BF16),
-        ],
+        out_shape=[jax.ShapeDtypeStruct((rows, w), BF16) for w in (width, width // 2, width // 2)],
         compiler_params=params(),
         name="join",
     )(*blocks)
@@ -146,13 +149,17 @@
 
 def stack_kernel(side, count, depth, *refs):
     hiddens, (left_ref, stack_ref, turned_ref) = refs[:count], refs[count:]
-    slots = hiddens[0].shape[0]
+    slots, units = hiddens[0].shape
+    rows = slots // 2
+    upper = lax.axis_index("expert") // (lax.axis_size("expert") // 2)
     for n, hidden in enumerate(hiddens):
-        stack_ref[n * depth : n * depth + slots, :] = hidden[...].astype(F32)
-        if slots < depth:
-            stack_ref[n * depth + slots : (n + 1) * depth, :] = jnp.zeros(
-                (depth - slots, stack_ref.shape[1]), F32
-            )
+        values = hidden[...].astype(F32)
+        lower, higher = values[:rows, :], values[rows:, :]
+        for part in range(2):
+            at = (2 * n + part) * depth
+            stack_ref[at : at + rows, :] = jnp.where(upper == part, lower, higher)
+            if rows < depth:
+                stack_ref[at + rows : at + depth, :] = jnp.zeros((depth - rows, units), F32)
     turned_ref[...] = stack_ref[...].T
     index = lax.axis_index("dp")
     masks = owner_masks(side)
@@ -165,54 +172,109 @@
 
 def stack(hiddens, side, depth, height):
     count = len(hiddens)
-    units = hiddens[0].shape[1]
+    _, units = hiddens[0].shape
     vmem = pl.BlockSpec(memory_space=pltpu.VMEM)
     return pl.pallas_call(
         functools.partial(stack_kernel, side, count, depth),
         in_specs=[vmem] * count,
         out_specs=vmem,
-        out_shape=jax.ShapeDtypeStruct((2 * side * height, count * depth), BF16),
+        out_shape=jax.ShapeDtypeStruct((2 * side * height, 2 * count * depth), BF16),
         scratch_shapes=[
-            pltpu.VMEM((count * depth, units), F32),
-            pltpu.VMEM((units, count * depth), F32),
+            pltpu.VMEM((2 * count * depth, units), F32),
+            pltpu.VMEM((units, 2 * count * depth), F32),
         ],
         compiler_params=params(),
         name="stack",
     )(*hiddens)
 
 
-def unit_kernel(capacity, full_ref, weight_ref, hidden_ref, grad_ref, *refs):
-    tables, sums_ref = refs[:-1], refs[-1]
+def unit_kernel(experts, capacity, near_ref, far_ref, weight_ref, hidden_ref, *refs):
+    grad_ref, kept_ref, sent_ref, full_ref, sums_ref = refs
     me = lax.axis_index("expert")
+    rows = near_ref.shape[0]
+    lower = me // (experts // 2) == 0
+    near = near_ref[...]
+    far = far_ref[...]
+    full_ref[:rows, :] = jnp.where(lower, near, far)
+    full_ref[rows : 2 * rows, :] = jnp.where(lower, far, near)
     unit = matmul_t(full_ref[...], weight_ref[...], (1, 1))
     grad_ref[...] = unit.astype(BF16)
     sums = jnp.sum(unit * hidden_ref[...].astype(F32), axis=1, keepdims=True)
     sums_ref[...] = jnp.zeros_like(sums_ref)
     sums_ref[: sums.shape[0], :] = jnp.broadcast_to(sums, (sums.shape[0], sums_ref.shape[1]))
-    for k, table in enumerate(tables):
-        table[...] = sums_ref[pl.ds((me ^ k) * capacity, table.shape[0]), :]
-
-
-def unit_part(full, weight, hidden, experts):
-    slots, _ = full.shape
+    padded = pad8(capacity)
+    for k in range(experts):
+        out = sent_ref if k % 2 else kept_ref
+        at = k // 2 * padded
+        out[at : at + padded, :] = sums_ref[pl.ds((me ^ k) * capacity, padded), :]
+
+
+def unit_part(near, far, weight, hidden, experts):
+    rows, width = near.shape
+    slots = 2 * rows
     units = weight.shape[0]
     capacity = slots // experts
-    vmem = pl.BlockSpec(memory_space=pltpu.VMEM)
-    return pl.pallas_call(
-        functools.partial(unit_kernel, capacity),
-        in_specs=[vmem] * 3,
-        out_specs=[vmem] * (1 + experts),
-        out_shape=[jax.ShapeDtypeStruct((slots, units), BF16)]
-        + [jax.ShapeDtypeStruct((pad8(capacity), 128), F32)] * experts,
-        scratch_shapes=[pltpu.VMEM((pad8(slots) + 8, 128), F32)],
+    table = jax.ShapeDtypeStruct((experts // 2 * pad8(capacity), 128), F32)
+    vmem = pl.BlockSpec(memory_space=pltpu.VMEM)
+    return pl.pallas_call(
+        functools.partial(unit_kernel, experts, capacity),
+        in_specs=[vmem] * 4,
+        out_specs=[vmem] * 3,
+        out_shape=[jax.ShapeDtypeStruct((slots, units), BF16), table, table],
+        scratch_shapes=[
+            pltpu.VMEM((slots, width), BF16),
+            pltpu.VMEM((pad8(slots) + 8, 128), F32),
+        ],
         compiler_params=params(),
         name="unit",
-    )(full, weight, hidden)
+    )(near, far, weight, hidden)
+
+
+def merge_kernel(plan, padded, kept_ref, got_ref, next_kept_ref, next_sent_ref):
+    for out, blocks in zip((next_kept_ref, next_sent_ref), plan):
+        for n, (source, block) in enumerate(blocks):
+            ref = got_ref if source else kept_ref
+            out[n * padded : (n + 1) * padded, :] = ref[block * padded : (block + 1) * padded, :]
+
+
+def merge(kept, got, plan, padded):
+    vmem = pl.BlockSpec(memory_space=pltpu.VMEM)
+    return pl.pallas_call(
+        functools.partial(merge_kernel, plan, padded),
+        in_specs=[vmem] * 2,
+        out_specs=[vmem] * 2,
+        out_shape=[jax.ShapeDtypeStruct((len(blocks) * padded, 128), F32) for blocks in plan],
+        compiler_params=params(),
+        name="merge",
+    )(kept, got)
+
+
+def return_tables(kept, sent, experts, padded):
+    slots, origins, bit = list(range(0, experts, 2)), [0], 1
+    while True:
+        got = lax.ppermute(sent, "expert", [(i, i ^ bit) for i in range(experts)])
+        if len(slots) == 1:
+            return [kept, got], origins + [o ^ bit for o in origins]
+        width = len(origins)
+        bit *= 2
+
+        def blocks(wanted):
+            return [
+                (source, i * width + o)
+                for i, slot in enumerate(slots)
+                if bool(slot & bit) == wanted
+                for source in range(2)
+                for o in range(width)
+            ]
+
+        kept, sent = merge(kept, got, (blocks(False), blocks(True)), padded)
+        origins = origins + [o ^ (bit // 2) for o in origins]
+        slots = [slot for slot in slots if not slot & bit]
 
 
 def partial_kernel(depth, left_ref, *refs):
-    masks = (len(refs) - 1) // 2
-    rows, outs, right_ref = refs[:masks], refs[masks : 2 * masks], refs[-1]
+    count = (len(refs) - 1) // 3 * 2
+    rows, outs, right_ref = refs[:count], refs[count:-1], refs[-1]
     slots = rows[0].shape[0]
     for n, row in enumerate(rows):
         right_ref[n * depth : n * depth + slots, :] = row[...]
@@ -229,13 +291,14 @@
 def partial(left, rows, depth):
     count = len(rows)
     half = rows[0].shape[1]
-    height = left.shape[0] // count
+    owners = count // 2
+    height = left.shape[0] // owners
     vmem = pl.BlockSpec(memory_space=pltpu.VMEM)
     return pl.pallas_call(
         functools.partial(partial_kernel, depth),
         in_specs=[vmem] * (1 + count),
-        out_specs=[vmem] * count,
-        out_shape=[jax.ShapeDtypeStruct((height, half), F32 if n == 0 else BF16) for n in range(count)],
+        out_specs=[vmem] * owners,
+        out_shape=[jax.ShapeDtypeStruct((height, half), F32 if n == 0 else BF16) for n in range(owners)],
         scratch_shapes=[pltpu.VMEM((count * depth, half), BF16)],
         compiler_params=params(),
         name="partial",
@@ -288,16 +351,20 @@
     )(own, *own_terms, *other_terms)
 
 
-def gate_kernel(experts, *refs):
-    tables = refs[:experts]
-    ids_ref, slots_ref, gates_ref, out_ref = refs[experts:]
+def gate_kernel(origins, padded, *refs):
+    tables = refs[:-4]
+    ids_ref, slots_ref, gates_ref, out_ref = refs[-4:]
+    experts = len(origins)
     me = lax.axis_index("expert")
-    padded, lanes = tables[0].shape
+    lanes = tables[0].shape[1]
     ids = ids_ref[...]
     slots = slots_ref[...]
     gates = gates_ref[...].astype(F32)
     valid = (ids < experts) & (slots >= 0)
-    target = jnp.where(valid, (ids ^ me) * padded + slots, -1)
+    place = ids ^ me
+    if list(origins) != list(range(experts)):
+        place = sum(jnp.where(place == o, n, 0) for n, o in enumerate(origins))
+    target = jnp.where(valid, place * padded + slots, -1)
     column = jnp.concatenate([table[...] for table in tables], axis=0)
     row = lax.broadcasted_iota(jnp.int32, column.shape, 0)
     for c in range(0, ids.shape[1], lanes):
@@ -308,12 +375,12 @@
         out_ref[:, c : c + lanes] = jnp.concatenate(found, axis=0) / gates[:, c : c + lanes]
 
 
-def gate_part(tables, ids, slots, gates):
-    experts = len(tables)
-    vmem = pl.BlockSpec(memory_space=pltpu.VMEM)
-    return pl.pallas_call(
-        functools.partial(gate_kernel, experts),
-        in_specs=[vmem] * (experts + 3),
+def gate_part(tables, origins, ids, slots, gates):
+    vmem = pl.BlockSpec(memory_space=pltpu.VMEM)
+    padded = sum(t.shape[0] for t in tables) // len(origins)
+    return pl.pallas_call(
+        functools.partial(gate_kernel, tuple(origins), padded),
+        in_specs=[vmem] * (len(tables) + 3),
         out_specs=vmem,
         out_shape=jax.ShapeDtypeStruct(ids.shape, F32),
         compiler_params=params(),
@@ -343,28 +410,29 @@
     for mask in routes:
         moved_hiddens.append(exchange(hidden, replicas, mask))
 
-    depth = -(-hidden.shape[0] // 32) * 32
+    depth = -(-hidden.shape[0] // 32) * 16
     height = hidden.shape[1] // replicas
     weight, hidden = load(weight, hidden)
     left = stack([hidden] + moved_hiddens, side, depth, height)
-    full, own, other = join(blocks, capacity)
-    rows = [own]
-    for mask in routes:
-        rows.append(exchange(own if mask in same else other, replicas, mask))
-
-    hidden_grad, *sums = unit_part(full, weight, hidden, experts)
-    tables = [sums[0]]
-    for k in range(1, experts):
-        pairs = [(i, i ^ k) for i in range(experts)]
-        tables.append(lax.ppermute(sums[k], "expert", pairs))
-
-    cut = partial(left, rows, depth)
+
+    parts, rows = [], []
+    for first in (0, experts // 2):
+        part, own, other = join(blocks[first : first + experts // 2], first, capacity)
+        parts.append(part)
+        rows.append([own])
+        for mask in routes:
+            rows[-1].append(exchange(own if mask in same else other, replicas, mask))
+
+    hidden_grad, kept, sent = unit_part(*parts, weight, hidden, experts)
+    tables, origins = return_tables(kept, sent, experts, pad8(capacity))
+
+    cut = partial(left, [r for pair in zip(*rows) for r in pair], depth)
     moved = []
     for n, mask in enumerate(owner_masks(side)[1:]):
         moved.append(exchange(cut[n + 1], replicas, mask))
     weight_grad = total(cut[0], moved[1:side], [moved[0]] + moved[side:])
 
-    gate_grad = gate_part(tables, ids, slots, gate)
+    gate_grad = gate_part(tables, origins, ids, slots, gate)
     return hidden_grad[None, None], weight_grad[None], gate_grad.T[None]
 
 

time: 43 us -> 42.4 us (0.986)
  starting transfers between devices: 17 us -> 15.7 us
  waiting for transfers between devices: 16.4 us -> 17.1 us
    ppermute x3 -> x2, starting transfers between devices: 5.5 us -> 1.41 us  [return_tables(): got = lax.ppermute(sent, 'expert', [(i, i ^ bit) for i in range(experts)])]
    ppermute x3 -> x2, waiting for transfers between devices: 3.69 us -> 7.14 us  [return_tables(): got = lax.ppermute(sent, 'expert', [(i, i ^ bit) for i in range(experts)])]
    ppermute x9 -> x12, waiting for transfers between devices: 4.89 us -> 1.8 us  [exchange(): return lax.ppermute(value, 'dp', pairs)]
    ppermute x9 -> x12, starting transfers between devices: 5.83 us -> 8.81 us  [exchange(): return lax.ppermute(value, 'dp', pairs)]
    pallas_call x3 -> x5, Pallas kernels: 3.04 us -> 3.01 us  [the longest x1 1.75 us: unit_part(): pl.pallas_call(functools.partial(unit_kernel, experts, capacity), in_spec...]
  transfers between devices with their start and end apart: 15 -> 17, of which waited for: 6 -> 6; matrix products, arithmetic and copies ran while one was open for 0% -> 0% of each run, Pallas kernels for 12% -> 12%
where the time goes in v2:
time: 42.4 us; the launch traced here: 42.3 us
  waiting for transfers between devices  17.1 us (40%)
  starting transfers between devices  15.7 us (37%)
  Pallas kernels  8.66 us (20%)
  between operations  0.74 us (2%)
    ppermute x12, starting transfers between devices, exchange(): return lax.ppermute(value, 'dp', pairs)  8.81 us
    ppermute x3, waiting for transfers between devices, on_device(): blocks.append(lax.ppermute(sent[k], 'expert', pairs))  8.21 us
    ppermute x2, waiting for transfers between devices, return_tables(): got = lax.ppermute(sent, 'expert', [(i, i ^ bit) for i in range(experts)])  7.14 us
    ppermute x3, starting transfers between devices, on_device(): blocks.append(lax.ppermute(sent[k], 'expert', pairs))  5.48 us
    pallas_call x1, Pallas kernels, load(): pl.pallas_call(load_kernel, in_specs=[pl.BlockSpec(memory_space=pltpu.HBM...  1.91 us
    pallas_call x1, Pallas kernels, pack(): pl.pallas_call(functools.partial(pack_kernel, experts, padded, pieces), i...  1.87 us
    ppermute x12, waiting for transfers between devices, exchange(): return lax.ppermute(value, 'dp', pairs)  1.8 us
    pallas_call x1, Pallas kernels, unit_part(): pl.pallas_call(functools.partial(unit_kernel, experts, capacity), in_spec...  1.75 us
  transfers between devices with their start and end apart: 17, of which 6 were waited for; matrix products, arithmetic and copies ran while one was open for 0% of the time, Pallas kernels for 12%

profile of v2, /device:TPU:0, one launch (start us, length us, event | category | flops | bytes accessed | tf_op | source)
XLA Modules:
  0.0 42.3 jit_solution(13578665476489780824)
XLA Ops:
  0.6 1.9 %pack.1 = (bf16[24,2048]{1,0:T(8,128)(2,1)S(1)}, bf16[24,2048]{1,0:T(8,128)(2,1)S(1)}, bf16[24,2048]{1,0:T(8,128)(2,1)S(1)}, bf16[24,2048]{1,0:T(8,128)(2,1)S(1)}) custom-call(s32[8,256]{1,0:T(8,128)} %bitcast.17, s32[8,256]{1,0:T(8,128)} %bitcast.19, bf16[8,256]{1,0:T(8,128)(2,1)} %bitcast.21, bf16[256,2048]{1,0:T(8,128)(2,1)} %bitcast.24), custom_call_target="tpu_custom_call" | custom-call | tf_op jit(solution)/shard_map/pack/pallas_call | solution.py:75
  2.5 4.1 %collective-permute-start.1 = (bf16[24,2048]{1,0:T(8,128)(2,1)S(1)}, bf16[24,2048]{1,0:T(8,128)(2,1)S(1)}, u32[]{:S(2)}, u32[]{:S(2)}) collective-permute-start(bf16[24,2048]{1,0:T(8,128)(2,1)S(1)} %get-tuple-element.27), channel_id=1, source_target_pairs={{0,2},{1,3},{2,0},{3,1},{4,6},{5,7},{6,4},{7,5},{8,10},{9,11},{10,... | collective-permute-start | bytes 294920 | tf_op jit(solution)/shard_map/ppermute | solution.py:405
  6.6 1.3 %collective-permute-start.2 = (bf16[24,2048]{1,0:T(8,128)(2,1)S(1)}, bf16[24,2048]{1,0:T(8,128)(2,1)S(1)}, u32[]{:S(2)}, u32[]{:S(2)}) collective-permute-start(bf16[24,2048]{1,0:T(8,128)(2,1)S(1)} %get-tuple-element.28), channel_id=1, source_target_pairs={{0,3},{1,2},{2,1},{3,0},{4,7},{5,6},{6,5},{7,4},{8,11},{9,10},{10,... | collective-permute-start | bytes 294920 | tf_op jit(solution)/shard_map/ppermute | solution.py:405
  8.0 0.0 collective-permute-start.3
  8.0 1.5 %collective-permute-start.4 = (bf16[84,768]{1,0:T(8,128)(2,1)}, bf16[84,768]{1,0:T(8,128)(2,1)S(1)}, u32[]{:S(2)}, u32[]{:S(2)}) collective-permute-start(bf16[84,768]{1,0:T(8,128)(2,1)} %bitcast.27), channel_id=1, source_target_pairs={{0,8},{4,20},{8,0},{12,28},{16,24},{20,4},{24,16},{28,12},{1,9},{5... | collective-permute-start | bytes 387080 | tf_op jit(solution)/shard_map/ppermute | solution.py:324
  9.5 0.4 collective-permute-start.5
  9.9 4.6 %collective-permute-done.1.refs_0_ = bf16[24,2048]{1,0:T(8,128)(2,1)S(1)} collective-permute-done((bf16[24,2048]{1,0:T(8,128)(2,1)S(1)}, bf16[24,2048]{1,0:T(8,128)(2,1)S(1)}, u32[]{:S(2)}, u32[]{:S(2)}) %collective-permute-start.1) | collective-permute-done | bytes 98336 | tf_op jit(solution)/shard_map/ppermute | solution.py:405
  14.5 0.0 collective-permute-start
  14.5 0.0 collective-permute-done.2.refs_1_
  14.5 0.3 join.3
  14.8 0.8 %collective-permute-start.11 = (bf16[42,1024]{1,0:T(8,128)(2,1)S(1)}, bf16[42,1024]{1,0:T(8,128)(2,1)S(1)}, u32[]{:S(2)}, u32[]{:S(2)}) collective-permute-start(bf16[42,1024]{1,0:T(8,128)(2,1)S(1)} %get-tuple-element.36), channel_id=1, source_target_pairs={{0,20},{4,8},{8,28},{12,0},{16,4},{20,24},{24,12},{28,16},{1,21},{... | collective-permute-start | bytes 258056 | tf_op jit(solution)/shard_map/ppermute | solution.py:324
  15.6 3.6 %collective-permute-done.refs_1_ = bf16[24,2048]{1,0:T(8,128)(2,1)S(1)} collective-permute-done((bf16[24,2048]{1,0:T(8,128)(2,1)S(1)}, bf16[24,2048]{1,0:T(8,128)(2,1)S(1)}, u32[]{:S(2)}, u32[]{:S(2)}) %collective-permute-start) | collective-permute-done | bytes 98336 | tf_op jit(solution)/shard_map/ppermute | solution.py:405
  19.1 0.0 collective-permute-start.7
  19.1 0.3 join.2
  19.4 0.0 collective-permute-done.3.refs_1_
  19.4 1.9 %collective-permute-start.10 = (bf16[42,1024]{1,0:T(8,128)(2,1)S(1)}, bf16[42,1024]{1,0:T(8,128)(2,1)S(1)}, u32[]{:S(2)}, u32[]{:S(2)}) collective-permute-start(bf16[42,1024]{1,0:T(8,128)(2,1)S(1)} %get-tuple-element.35), channel_id=1, source_target_pairs={{0,20},{4,8},{8,28},{12,0},{16,4},{20,24},{24,12},{28,16},{1,21},{... | collective-permute-start | bytes 258056 | tf_op jit(solution)/shard_map/ppermute | solution.py:324
  21.3 0.0 collective-permute-done.4.refs_2_
  21.3 0.0 collective-permute-start.6
  21.3 0.0 collective-permute-done.5.refs_3_
  21.3 1.6 %collective-permute-start.9 = (bf16[42,1024]{1,0:T(8,128)(2,1)S(1)}, bf16[42,1024]{1,0:T(8,128)(2,1)S(1)}, u32[]{:S(2)}, u32[]{:S(2)}) collective-permute-start(bf16[42,1024]{1,0:T(8,128)(2,1)S(1)} %get-tuple-element.34.refs_1_), channel_id=1, source_target_pairs={{0,8},{4,20},{8,0},{12,28},{16,24},{20,4},{24,16},{28,12},{1,9},{5... | collective-permute-start | bytes 258056 | tf_op jit(solution)/shard_map/ppermute | solution.py:324
  22.8 0.0 collective-permute-done.11.refs_7_
  22.8 0.5 %collective-permute-start.8 = (bf16[42,1024]{1,0:T(8,128)(2,1)S(1)}, bf16[42,1024]{1,0:T(8,128)(2,1)S(1)}, u32[]{:S(2)}, u32[]{:S(2)}) collective-permute-start(bf16[42,1024]{1,0:T(8,128)(2,1)S(1)} %get-tuple-element.33.refs_0_), channel_id=1, source_target_pairs={{0,8},{4,20},{8,0},{12,28},{16,24},{20,4},{24,16},{28,12},{1,9},{5... | collective-permute-start | bytes 258056 | tf_op jit(solution)/shard_map/ppermute | solution.py:324
  23.4 1.9 %load.1 = (bf16[768,2048]{1,0:T(8,128)(2,1)S(1)}, bf16[84,768]{1,0:T(8,128)(2,1)S(1)}) custom-call(bf16[768,2048]{1,0:T(8,128)(2,1)} %bitcast.23, bf16[84,768]{1,0:T(8,128)(2,1)} %bitcast.29), custom_call_target="tpu_custom_call" | custom-call | tf_op jit(solution)/shard_map/load/pallas_call | solution.py:139
  25.3 0.0 copy-start
  25.3 0.0 copy-start.1
  25.3 0.0 copy-start.2
  25.3 0.3 stack.1.left_ref
  25.7 0.0 collective-permute-done.7.refs_3_
  25.7 0.3 collective-permute-done.9.refs_5_
  26.0 0.0 collective-permute-done.10.refs_6_
  26.0 0.0 collective-permute-done.6.refs_2_
  26.0 1.5 %collective-permute-done.8.refs_4_ = bf16[42,1024]{1,0:T(8,128)(2,1)S(1)} collective-permute-done((bf16[42,1024]{1,0:T(8,128)(2,1)S(1)}, bf16[42,1024]{1,0:T(8,128)(2,1)S(1)}, u32[]{:S(2)}, u32[]{:S(2)}) %collective-permute-start.8) | collective-permute-done | bytes 86048 | tf_op jit(solution)/shard_map/ppermute | solution.py:324
  27.5 0.6 %partial.1 = (f32[96,1024]{1,0:T(8,128)S(1)}, bf16[96,1024]{1,0:T(8,128)(2,1)S(1)}, bf16[96,1024]{1,0:T(8,128)(2,1)S(1)}, bf16[96,1024]{1,0:T(8,128)(2,1)S(1)}) custom-call(bf16[384,384]{1,0:T(8,128)(2,1)S(1)} %stack.1.left_ref, bf16[42,1024]{1,0:T(8,128)(2,1)S(1)} %get-tuple-element.33.refs_0_, bf16[42,1024]{1,0:T(8,128)(2,1)S(1)} %get-tuple-element.34.refs_1_, ...), custom_call_target="tpu_custom_call" | custom-call | tf_op jit(solution)/shard_map/partial/pallas_call | solution.py:297
  28.1 1.1 %collective-permute-start.12 = (bf16[96,1024]{1,0:T(8,128)(2,1)S(1)}, bf16[96,1024]{1,0:T(8,128)(2,1)S(1)}, u32[]{:S(2)}, u32[]{:S(2)}) collective-permute-start(bf16[96,1024]{1,0:T(8,128)(2,1)S(1)} %get-tuple-element.38), channel_id=1, source_target_pairs={{0,16},{4,12},{8,24},{12,4},{16,0},{20,28},{24,8},{28,20},{1,17},{... | collective-permute-start | bytes 589832 | tf_op jit(solution)/shard_map/ppermute | solution.py:324
  29.1 0.0 collective-permute-start.13
  29.1 1.1 %collective-permute-start.14 = (bf16[96,1024]{1,0:T(8,128)(2,1)S(1)}, bf16[96,1024]{1,0:T(8,128)(2,1)S(1)}, u32[]{:S(2)}, u32[]{:S(2)}) collective-permute-start(bf16[96,1024]{1,0:T(8,128)(2,1)S(1)} %get-tuple-element.40), channel_id=1, source_target_pairs={{0,20},{4,8},{8,28},{12,0},{16,4},{20,24},{24,12},{28,16},{1,21},{... | collective-permute-start | bytes 589832 | tf_op jit(solution)/shard_map/ppermute | solution.py:324
  30.3 1.8 %unit.1 = (bf16[84,768]{1,0:T(8,128)(2,1)}, f32[48,128]{1,0:T(8,128)S(1)}, f32[48,128]{1,0:T(8,128)S(1)}) custom-call(bf16[42,2048]{1,0:T(8,128)(2,1)S(1)} %get-tuple-element.26.near_ref, bf16[42,2048]{1,0:T(8,128)(2,1)S(1)} %get-tuple-element.29.far_ref, bf16[768,2048]{1,0:T(8,128)(2,1)S(1)} %get-tuple-element.30.weight_ref, ...), custom_call_target="tpu_custom_call" | custom-call | tf_op jit(solution)/shard_map/unit/pallas_call | solution.py:219
  32.0 0.0 collective-permute-start.15
  32.0 3.8 %collective-permute-done.15.got_ref = f32[48,128]{1,0:T(8,128)S(1)} collective-permute-done((f32[48,128]{1,0:T(8,128)S(1)}, f32[48,128]{1,0:T(8,128)S(1)}, u32[]{:S(2)}, u32[]{:S(2)}) %collective-permute-start.15) | collective-permute-done | bytes 24608 | tf_op jit(solution)/shard_map/ppermute | solution.py:255
  35.9 1.4 %collective-permute-start.16 = (f32[48,128]{1,0:T(8,128)S(1)}, f32[48,128]{1,0:T(8,128)S(1)}, u32[]{:S(2)}, u32[]{:S(2)}) collective-permute-start(f32[48,128]{1,0:T(8,128)S(1)} %get-tuple-element.44), channel_id=1, source_target_pairs={{0,2},{1,3},{2,0},{3,1},{4,6},{5,7},{6,4},{7,5},{8,10},{9,11},{10,... | collective-permute-start | bytes 73736 | tf_op jit(solution)/shard_map/ppermute | solution.py:255
  37.3 3.3 %collective-permute-done.16.refs_1_ = f32[48,128]{1,0:T(8,128)S(1)} collective-permute-done((f32[48,128]{1,0:T(8,128)S(1)}, f32[48,128]{1,0:T(8,128)S(1)}, u32[]{:S(2)}, u32[]{:S(2)}) %collective-permute-start.16) | collective-permute-done | bytes 24608 | tf_op jit(solution)/shard_map/ppermute | solution.py:255
  40.6 0.0 copy-done
  40.6 0.0 copy-done.1
  40.6 0.7 %gate.1 = f32[8,256]{1,0:T(8,128)} custom-call(f32[48,128]{1,0:T(8,128)S(1)} %get-tuple-element.43.refs_0_, f32[48,128]{1,0:T(8,128)S(1)} %collective-permute-done.16.refs_1_, s32[8,256]{1,0:T(8,128)S(1)} %bitcast.18, s32[8,256]{1,0:T(8,128)S(1)} %bitcast.20, bf16[8,256]{1,0:T(8,128)(2,1)S(1)} %bitcast.22), custom_call_target="tpu_custom_call" | custom-call | tf_op jit(solution)/shard_map/gate/pallas_call | solution.py:381
  41.3 0.0 collective-permute-done.12.refs_0_
  41.3 0.0 collective-permute-done.13.refs_1_
  41.3 0.0 collective-permute-done.14.refs_2_
  41.3 1.0 %total.1 = f32[96,2048]{1,0:T(8,128)} custom-call(f32[96,1024]{1,0:T(8,128)S(1)} %get-tuple-element.37.own_ref, bf16[96,1024]{1,0:T(8,128)(2,1)S(1)} %collective-permute-done.12.refs_0_, bf16[96,1024]{1,0:T(8,128)(2,1)S(1)} %collective-permute-done.13.refs_1_, bf16[96,1024]{1,0:T(8,128)(2,1)S(1)} %collective-permute-done.14.refs_2_), custom_call_target="tpu_custom_call" | custom-call | tf_op jit(solution)/shard_map/total/pallas_call | solution.py:344
  (2 shorter events, 0.0 us)
Async XLA Ops:
  2.5 12.0 %collective-permute-start.1 = (bf16[24,2048]{1,0:T(8,128)(2,1)S(1)}, bf16[24,2048]{1,0:T(8,128)(2,1)S(1)}, u32[]{:S(2)}, u32[]{:S(2)}) collective-permute-start(bf16[24,2048]{1,0:T(8,128)(2,1)S(1)} %get-tuple-element.27), channel_id=1, source_target_pairs={{0,2},{1,3},{2,0},{3,1},{4,6},{5,7},{6,4},{7,5},{8,10},{9,11},{10,... | collective-permute-start | bytes 294920 | tf_op jit(solution)/shard_map/ppermute | solution.py:405
  6.6 7.9 %collective-permute-start.2 = (bf16[24,2048]{1,0:T(8,128)(2,1)S(1)}, bf16[24,2048]{1,0:T(8,128)(2,1)S(1)}, u32[]{:S(2)}, u32[]{:S(2)}) collective-permute-start(bf16[24,2048]{1,0:T(8,128)(2,1)S(1)} %get-tuple-element.28), channel_id=1, source_target_pairs={{0,3},{1,2},{2,1},{3,0},{4,7},{5,6},{6,5},{7,4},{8,11},{9,10},{10,... | collective-permute-start | bytes 294920 | tf_op jit(solution)/shard_map/ppermute | solution.py:405
  8.0 11.4 %collective-permute-start.3 = (bf16[84,768]{1,0:T(8,128)(2,1)}, bf16[84,768]{1,0:T(8,128)(2,1)S(1)}, u32[]{:S(2)}, u32[]{:S(2)}) collective-permute-start(bf16[84,768]{1,0:T(8,128)(2,1)} %bitcast.26), channel_id=1, source_target_pairs={{0,4},{4,0},{8,12},{12,8},{16,20},{20,16},{24,28},{28,24},{1,5},{5... | collective-permute-start | bytes 387080 | tf_op jit(solution)/shard_map/ppermute | solution.py:324
  8.0 13.3 %collective-permute-start.4 = (bf16[84,768]{1,0:T(8,128)(2,1)}, bf16[84,768]{1,0:T(8,128)(2,1)S(1)}, u32[]{:S(2)}, u32[]{:S(2)}) collective-permute-start(bf16[84,768]{1,0:T(8,128)(2,1)} %bitcast.27), channel_id=1, source_target_pairs={{0,8},{4,20},{8,0},{12,28},{16,24},{20,4},{24,16},{28,12},{1,9},{5... | collective-permute-start | bytes 387080 | tf_op jit(solution)/shard_map/ppermute | solution.py:324
  9.5 11.8 %collective-permute-start.5 = (bf16[84,768]{1,0:T(8,128)(2,1)}, bf16[84,768]{1,0:T(8,128)(2,1)S(1)}, u32[]{:S(2)}, u32[]{:S(2)}) collective-permute-start(bf16[84,768]{1,0:T(8,128)(2,1)} %bitcast.28), channel_id=1, source_target_pairs={{0,20},{4,8},{8,28},{12,0},{16,4},{20,24},{24,12},{28,16},{1,21},{... | collective-permute-start | bytes 387080 | tf_op jit(solution)/shard_map/ppermute | solution.py:324
  14.5 4.6 %collective-permute-start = (bf16[24,2048]{1,0:T(8,128)(2,1)S(1)}, bf16[24,2048]{1,0:T(8,128)(2,1)S(1)}, u32[]{:S(2)}, u32[]{:S(2)}) collective-permute-start(bf16[24,2048]{1,0:T(8,128)(2,1)S(1)} %get-tuple-element.25), channel_id=1, source_target_pairs={{0,1},{1,0},{2,3},{3,2},{4,5},{5,4},{6,7},{7,6},{8,9},{9,8},{10,11... | collective-permute-start | bytes 294920 | tf_op jit(solution)/shard_map/ppermute | solution.py:405
  14.8 8.1 %collective-permute-start.11 = (bf16[42,1024]{1,0:T(8,128)(2,1)S(1)}, bf16[42,1024]{1,0:T(8,128)(2,1)S(1)}, u32[]{:S(2)}, u32[]{:S(2)}) collective-permute-start(bf16[42,1024]{1,0:T(8,128)(2,1)S(1)} %get-tuple-element.36), channel_id=1, source_target_pairs={{0,20},{4,8},{8,28},{12,0},{16,4},{20,24},{24,12},{28,16},{1,21},{... | collective-permute-start | bytes 258056 | tf_op jit(solution)/shard_map/ppermute | solution.py:324
  19.1 6.6 %collective-permute-start.7 = (bf16[42,1024]{1,0:T(8,128)(2,1)S(1)}, bf16[42,1024]{1,0:T(8,128)(2,1)S(1)}, u32[]{:S(2)}, u32[]{:S(2)}) collective-permute-start(bf16[42,1024]{1,0:T(8,128)(2,1)S(1)} %get-tuple-element.36), channel_id=1, source_target_pairs={{0,4},{4,0},{8,12},{12,8},{16,20},{20,16},{24,28},{28,24},{1,5},{5... | collective-permute-start | bytes 258056 | tf_op jit(solution)/shard_map/ppermute | solution.py:324
  19.4 6.6 %collective-permute-start.10 = (bf16[42,1024]{1,0:T(8,128)(2,1)S(1)}, bf16[42,1024]{1,0:T(8,128)(2,1)S(1)}, u32[]{:S(2)}, u32[]{:S(2)}) collective-permute-start(bf16[42,1024]{1,0:T(8,128)(2,1)S(1)} %get-tuple-element.35), channel_id=1, source_target_pairs={{0,20},{4,8},{8,28},{12,0},{16,4},{20,24},{24,12},{28,16},{1,21},{... | collective-permute-start | bytes 258056 | tf_op jit(solution)/shard_map/ppermute | solution.py:324
  21.3 4.7 %collective-permute-start.6 = (bf16[42,1024]{1,0:T(8,128)(2,1)S(1)}, bf16[42,1024]{1,0:T(8,128)(2,1)S(1)}, u32[]{:S(2)}, u32[]{:S(2)}) collective-permute-start(bf16[42,1024]{1,0:T(8,128)(2,1)S(1)} %get-tuple-element.35), channel_id=1, source_target_pairs={{0,4},{4,0},{8,12},{12,8},{16,20},{20,16},{24,28},{28,24},{1,5},{5... | collective-permute-start | bytes 258056 | tf_op jit(solution)/shard_map/ppermute | solution.py:324
  21.3 4.7 %collective-permute-start.9 = (bf16[42,1024]{1,0:T(8,128)(2,1)S(1)}, bf16[42,1024]{1,0:T(8,128)(2,1)S(1)}, u32[]{:S(2)}, u32[]{:S(2)}) collective-permute-start(bf16[42,1024]{1,0:T(8,128)(2,1)S(1)} %get-tuple-element.34.refs_1_), channel_id=1, source_target_pairs={{0,8},{4,20},{8,0},{12,28},{16,24},{20,4},{24,16},{28,12},{1,9},{5... | collective-permute-start | bytes 258056 | tf_op jit(solution)/shard_map/ppermute | solution.py:324
  22.8 4.6 %collective-permute-start.8 = (bf16[42,1024]{1,0:T(8,128)(2,1)S(1)}, bf16[42,1024]{1,0:T(8,128)(2,1)S(1)}, u32[]{:S(2)}, u32[]{:S(2)}) collective-permute-start(bf16[42,1024]{1,0:T(8,128)(2,1)S(1)} %get-tuple-element.33.refs_0_), channel_id=1, source_target_pairs={{0,8},{4,20},{8,0},{12,28},{16,24},{20,4},{24,16},{28,12},{1,9},{5... | collective-permute-start | bytes 258056 | tf_op jit(solution)/shard_map/ppermute | solution.py:324
  25.3 15.3 %copy-start = (s32[1,256,8]{1,2,0:T(8,128)S(1)}, s32[1,256,8]{1,2,0:T(8,128)}, u32[]{:S(2)}) copy-start(s32[1,256,8]{1,2,0:T(8,128)} %param.8) | copy-start | bytes 24580
  25.3 15.3 %copy-start.1 = (s32[1,256,8]{1,2,0:T(8,128)S(1)}, s32[1,256,8]{1,2,0:T(8,128)}, u32[]{:S(2)}) copy-start(s32[1,256,8]{1,2,0:T(8,128)} %param.9) | copy-start | bytes 24580
  25.3 15.3 %copy-start.2 = (bf16[1,256,8]{1,2,0:T(8,128)(2,1)S(1)}, bf16[1,256,8]{1,2,0:T(8,128)(2,1)}, u32[]{:S(2)}) copy-start(bf16[1,256,8]{1,2,0:T(8,128)(2,1)} %param.7) | copy-start | bytes 12292
  28.1 13.2 %collective-permute-start.12 = (bf16[96,1024]{1,0:T(8,128)(2,1)S(1)}, bf16[96,1024]{1,0:T(8,128)(2,1)S(1)}, u32[]{:S(2)}, u32[]{:S(2)}) collective-permute-start(bf16[96,1024]{1,0:T(8,128)(2,1)S(1)} %get-tuple-element.38), channel_id=1, source_target_pairs={{0,16},{4,12},{8,24},{12,4},{16,0},{20,28},{24,8},{28,20},{1,17},{... | collective-permute-start | bytes 589832 | tf_op jit(solution)/shard_map/ppermute | solution.py:324
  29.1 12.2 %collective-permute-start.13 = (bf16[96,1024]{1,0:T(8,128)(2,1)S(1)}, bf16[96,1024]{1,0:T(8,128)(2,1)S(1)}, u32[]{:S(2)}, u32[]{:S(2)}) collective-permute-start(bf16[96,1024]{1,0:T(8,128)(2,1)S(1)} %get-tuple-element.39), channel_id=1, source_target_pairs={{0,4},{4,0},{8,12},{12,8},{16,20},{20,16},{24,28},{28,24},{1,5},{5... | collective-permute-start | bytes 589832 | tf_op jit(solution)/shard_map/ppermute | solution.py:324
  29.1 12.2 %collective-permute-start.14 = (bf16[96,1024]{1,0:T(8,128)(2,1)S(1)}, bf16[96,1024]{1,0:T(8,128)(2,1)S(1)}, u32[]{:S(2)}, u32[]{:S(2)}) collective-permute-start(bf16[96,1024]{1,0:T(8,128)(2,1)S(1)} %get-tuple-element.40), channel_id=1, source_target_pairs={{0,20},{4,8},{8,28},{12,0},{16,4},{20,24},{24,12},{28,16},{1,21},{... | collective-permute-start | bytes 589832 | tf_op jit(solution)/shard_map/ppermute | solution.py:324
  32.0 3.8 %collective-permute-start.15 = (f32[48,128]{1,0:T(8,128)S(1)}, f32[48,128]{1,0:T(8,128)S(1)}, u32[]{:S(2)}, u32[]{:S(2)}) collective-permute-start(f32[48,128]{1,0:T(8,128)S(1)} %get-tuple-element.42), channel_id=1, source_target_pairs={{0,1},{1,0},{2,3},{3,2},{4,5},{5,4},{6,7},{7,6},{8,9},{9,8},{10,11... | collective-permute-start | bytes 73736 | tf_op jit(solution)/shard_map/ppermute | solution.py:255
  35.9 4.7 %collective-permute-start.16 = (f32[48,128]{1,0:T(8,128)S(1)}, f32[48,128]{1,0:T(8,128)S(1)}, u32[]{:S(2)}, u32[]{:S(2)}) collective-permute-start(f32[48,128]{1,0:T(8,128)S(1)} %get-tuple-element.44), channel_id=1, source_target_pairs={{0,2},{1,3},{2,0},{3,1},{4,6},{5,7},{6,4},{7,5},{8,10},{9,11},{10,... | collective-permute-start | bytes 73736 | tf_op jit(solution)/shard_map/ppermute | solution.py:255

commit v3 on v2

--- a/solution.py
+++ b/solution.py
@@ -12,6 +12,7 @@
 F32 = jnp.float32
 BF16 = jnp.bfloat16
 LIMIT = 24 * 1024 * 1024
+CHUNKS = 8
 
 
 def params(**kw):
@@ -30,9 +31,11 @@
     return lax.dot_general(a, b, ((contract[:1], contract[1:]), ((), ())), preferred_element_type=F32)
 
 
-def pack_kernel(experts, padded, pieces, *refs):
+def pack_kernel(experts, capacity, pieces, *refs):
     arrays, out_refs = refs[:4], refs[4 : 4 + experts]
-    ids_ref, slots_ref, gates_ref, grad_ref, small_sems, grad_sems = refs[4 + experts :]
+    ids_ref, slots_ref, gates_ref, grad_ref, dense_ref, small_sems, grad_sems = refs[4 + experts :]
+    padded = pad8(capacity)
+    chunk = dense_ref.shape[2]
     small = [
         pltpu.make_async_copy(src, dst, small_sems.at[n])
         for n, (src, dst) in enumerate(zip(arrays[:3], (ids_ref, slots_ref, gates_ref)))
@@ -64,55 +67,60 @@
         columns = slice(n * width, (n + 1) * width)
         large[n].wait()
         rows = jnp.dot(chosen, grad_ref[:, columns], preferred_element_type=F32)
-        for k, out in enumerate(out_refs):
-            out[:, columns] = rows[k * padded : (k + 1) * padded, :].astype(BF16)
-
-
-def pack(ids, slots, gates, grad, experts, padded):
-    width = grad.shape[1]
+        for k in range(experts):
+            for c in range(CHUNKS // pieces):
+                at = (n * (CHUNKS // pieces) + c) * capacity
+                dense_ref[k, at : at + capacity, :] = rows[
+                    k * padded : k * padded + capacity, c * chunk : (c + 1) * chunk
+                ]
+    for k, out in enumerate(out_refs):
+        out[...] = dense_ref[k].astype(BF16)
+
+
+def pack(ids, slots, gates, grad, experts, capacity):
+    dense = (CHUNKS * capacity, grad.shape[1] // CHUNKS)
     pieces = 4
     arrays = (ids, slots, gates, grad)
     return pl.pallas_call(
-        functools.partial(pack_kernel, experts, padded, pieces),
+        functools.partial(pack_kernel, experts, capacity, pieces),
         in_specs=[pl.BlockSpec(memory_space=pltpu.HBM)] * 4,
         out_specs=[pl.BlockSpec(memory_space=pltpu.VMEM)] * experts,
-        out_shape=[jax.ShapeDtypeStruct((padded, width), BF16)] * experts,
+        out_shape=[jax.ShapeDtypeStruct(dense, BF16)] * experts,
         scratch_shapes=[pltpu.VMEM(a.shape, a.dtype) for a in arrays]
-        + [pltpu.SemaphoreType.DMA((3,)), pltpu.SemaphoreType.DMA((pieces,))],
+        + [pltpu.VMEM((experts, *dense), F32), pltpu.SemaphoreType.DMA((3,)), pltpu.SemaphoreType.DMA((pieces,))],
         compiler_params=params(),
         name="pack",
     )(*map(in_hbm, arrays))
 
 
-def rows_of(block, row_of_first, rows, capacity):
-    padded = block.shape[0]
-    row = lax.broadcasted_iota(jnp.int32, (rows, padded), 0)
-    col = lax.broadcasted_iota(jnp.int32, (rows, padded), 1)
-    place = (row == row_of_first + col) & (col < capacity)
-    return jnp.dot(place.astype(BF16), block[...], preferred_element_type=F32)
-
-
-def store_halves(rows, part_ref, own_ref, other_ref):
-    core = lax.axis_index("dp") % 2
-    half = own_ref.shape[1]
-    part_ref[...] = rows.astype(BF16)
-    own_ref[...] = part_ref[:, pl.ds(pl.multiple_of(core * half, 128), half)]
-    other_ref[...] = part_ref[:, pl.ds(pl.multiple_of((1 - core) * half, 128), half)]
+def rows_of(block, first, rows, capacity):
+    shape = (CHUNKS, -(-rows // 16) * 16, CHUNKS * capacity)
+    chunk = lax.broadcasted_iota(jnp.int32, shape, 0)
+    slot = lax.broadcasted_iota(jnp.int32, shape, 1) - first
+    source = lax.broadcasted_iota(jnp.int32, shape, 2)
+    place = (source == chunk * capacity + slot) & (slot >= 0) & (slot < capacity)
+    place = place.astype(BF16).reshape(shape[0] * shape[1], shape[2])
+    return jnp.dot(place, block[...], preferred_element_type=F32)
 
 
 def join_kernel(first, capacity, *refs):
     count = len(refs) - 3
     me = lax.axis_index("expert")
+    core = lax.axis_index("dp") % 2
     part_ref, own_ref, other_ref = refs[count:]
-    rows = part_ref.shape[0]
-    total = jnp.zeros(part_ref.shape, F32)
+    rows, half = own_ref.shape
+    total = 0.0
     for k, block in enumerate(refs[:count]):
         total += rows_of(block, ((me ^ (first + k)) % count) * capacity, rows, capacity)
-    store_halves(total, part_ref, own_ref, other_ref)
+    tall, chunk = total.shape[0] // CHUNKS, total.shape[1]
+    for c in range(CHUNKS):
+        part_ref[:, c * chunk : (c + 1) * chunk] = total[c * tall : c * tall + rows, :].astype(BF16)
+    own_ref[...] = part_ref[:, pl.ds(pl.multiple_of(core * half, 128), half)]
+    other_ref[...] = part_ref[:, pl.ds(pl.multiple_of((1 - core) * half, 128), half)]
 
 
 def join(blocks, first, capacity):
-    rows, width = len(blocks) * capacity, blocks[0].shape[1]
+    rows, width = len(blocks) * capacity, blocks[0].shape[1] * CHUNKS
     vmem = pl.BlockSpec(memory_space=pltpu.VMEM)
     return pl.pallas_call(
         functools.partial(join_kernel, first, capacity),
@@ -324,39 +332,37 @@
     return lax.ppermute(value, "dp", pairs)
 
 
-def total_kernel(terms, own_ref, *refs):
-    own_terms, other_terms, out_ref = refs[:terms], refs[terms:-1], refs[-1]
+def finish_kernel(terms, origins, *refs):
+    own_ref, own_terms, other_terms = refs[0], refs[1 : 1 + terms], refs[1 + terms : 2 + 2 * terms]
+    refs = refs[2 + 2 * terms :]
+    tables, ids_ref, slots_ref, gates_ref, hidden_ref = refs[:2], *refs[2:6]
+    weight_out, gate_out, hidden_out, halves_ref, gate_ref, sems = refs[6:]
     core = lax.axis_index("dp") % 2
     half = own_ref.shape[1]
-    own = own_ref[...]
+
+    def store(src, dst, n):
+        copy = pltpu.make_async_copy(src, dst, sems.at[n])
+        copy.start()
+        return copy
+
+    total = own_ref[...]
     for term in own_terms:
-        own += term[...].astype(F32)
-    other = other_terms[0][...].astype(F32)
+        total += term[...].astype(F32)
+    halves_ref[0] = total
+    columns = pl.ds(pl.multiple_of(core * half, 128), half)
+    copies = [store(halves_ref.at[0], weight_out.at[:, columns], 0)]
+    total = other_terms[0][...].astype(F32)
     for term in other_terms[1:]:
-        other += term[...].astype(F32)
-    out_ref[:, pl.ds(pl.multiple_of(core * half, 128), half)] = own
-    out_ref[:, pl.ds(pl.multiple_of((1 - core) * half, 128), half)] = other
-
-
-def total(own, own_terms, other_terms):
-    height, half = own.shape
-    vmem = pl.BlockSpec(memory_space=pltpu.VMEM)
-    return pl.pallas_call(
-        functools.partial(total_kernel, len(own_terms)),
-        in_specs=[vmem] * (1 + len(own_terms) + len(other_terms)),
-        out_specs=vmem,
-        out_shape=jax.ShapeDtypeStruct((height, 2 * half), F32),
-        compiler_params=params(),
-        name="total",
-    )(own, *own_terms, *other_terms)
-
-
-def gate_kernel(origins, padded, *refs):
-    tables = refs[:-4]
-    ids_ref, slots_ref, gates_ref, out_ref = refs[-4:]
+        total += term[...].astype(F32)
+    halves_ref[1] = total
+    columns = pl.ds(pl.multiple_of((1 - core) * half, 128), half)
+    copies.append(store(halves_ref.at[1], weight_out.at[:, columns], 1))
+    copies.append(store(hidden_ref, hidden_out, 2))
+
     experts = len(origins)
     me = lax.axis_index("expert")
     lanes = tables[0].shape[1]
+    padded = 2 * tables[0].shape[0] // experts
     ids = ids_ref[...]
     slots = slots_ref[...]
     gates = gates_ref[...].astype(F32)
@@ -372,20 +378,34 @@
             jnp.sum(jnp.where(row == target[k : k + 1, c : c + lanes], column, 0.0), axis=0, keepdims=True)
             for k in range(ids.shape[0])
         ]
-        out_ref[:, c : c + lanes] = jnp.concatenate(found, axis=0) / gates[:, c : c + lanes]
-
-
-def gate_part(tables, origins, ids, slots, gates):
-    vmem = pl.BlockSpec(memory_space=pltpu.VMEM)
-    padded = sum(t.shape[0] for t in tables) // len(origins)
-    return pl.pallas_call(
-        functools.partial(gate_kernel, tuple(origins), padded),
-        in_specs=[vmem] * (len(tables) + 3),
-        out_specs=vmem,
-        out_shape=jax.ShapeDtypeStruct(ids.shape, F32),
-        compiler_params=params(),
-        name="gate",
-    )(*tables, ids, slots, gates)
+        gate_ref[:, c : c + lanes] = jnp.concatenate(found, axis=0) / gates[:, c : c + lanes]
+    copies.append(store(gate_ref, gate_out, 3))
+    for copy in copies:
+        copy.wait()
+
+
+def finish(own, own_terms, other_terms, tables, origins, ids, slots, gates, hidden_grad):
+    height, half = own.shape
+    vmem = pl.BlockSpec(memory_space=pltpu.VMEM)
+    hbm = pl.BlockSpec(memory_space=pltpu.HBM)
+    arrays = (own, *own_terms, *other_terms, *tables, ids, slots, gates, hidden_grad)
+    return pl.pallas_call(
+        functools.partial(finish_kernel, len(own_terms), tuple(origins)),
+        in_specs=[vmem] * len(arrays),
+        out_specs=[hbm] * 3,
+        out_shape=[
+            jax.ShapeDtypeStruct((height, 2 * half), F32),
+            jax.ShapeDtypeStruct(ids.shape, F32),
+            jax.ShapeDtypeStruct(hidden_grad.shape, BF16),
+        ],
+        scratch_shapes=[
+            pltpu.VMEM((2, height, half), F32),
+            pltpu.VMEM(ids.shape, F32),
+            pltpu.SemaphoreType.DMA((4,)),
+        ],
+        compiler_params=params(),
+        name="finish",
+    )(*arrays)
 
 
 def on_device(out_grad, gates, expert_ids, route_slots, saved_hidden, down_weight):
@@ -398,7 +418,7 @@
     capacity = hidden.shape[0] // experts
     ids, slots, gate = expert_ids[0].T, route_slots[0].T, gates[0].T
 
-    sent = pack(ids, slots, gate, out_grad[0], experts, pad8(capacity))
+    sent = pack(ids, slots, gate, out_grad[0], experts, capacity)
     blocks = [sent[0]]
     for k in range(1, experts):
         pairs = [(i, i ^ k) for i in range(experts)]
@@ -430,9 +450,17 @@
     moved = []
     for n, mask in enumerate(owner_masks(side)[1:]):
         moved.append(exchange(cut[n + 1], replicas, mask))
-    weight_grad = total(cut[0], moved[1:side], [moved[0]] + moved[side:])
-
-    gate_grad = gate_part(tables, origins, ids, slots, gate)
+    weight_grad, gate_grad, hidden_grad = finish(
+        cut[0],
+        moved[1:side],
+        [moved[0]] + moved[side:],
+        tables,
+        origins,
+        ids,
+        slots,
+        gate,
+        hidden_grad,
+    )
     return hidden_grad[None, None], weight_grad[None], gate_grad.T[None]
 
 

time: 42.4 us -> 39.4 us (0.929)
  waiting for transfers between devices: 17.1 us -> 12.4 us
  starting transfers between devices: 15.7 us -> 18.6 us
  Pallas kernels: 8.66 us -> 7.5 us
    ppermute x3, waiting for transfers between devices: 8.21 us -> 4.91 us  [on_device(): blocks.append(lax.ppermute(sent[k], 'expert', pairs))]
    ppermute x12, starting transfers between devices: 8.81 us -> 10.7 us  [exchange(): return lax.ppermute(value, 'dp', pairs)]
    ppermute x12, waiting for transfers between devices: 1.8 us -> 0.93 us  [exchange(): return lax.ppermute(value, 'dp', pairs)]
    ppermute x2, starting transfers between devices: 1.41 us -> 2.08 us  [return_tables(): got = lax.ppermute(sent, 'expert', [(i, i ^ bit) for i in range(experts)])]
    pallas_call x3 -> x2, Pallas kernels: 3.54 us -> 2.9 us  [the longest x1 1.91 us: pack(): pl.pallas_call(functools.partial(pack_kernel, experts, capacity, pieces),...]
    ppermute x2, waiting for transfers between devices: 7.14 us -> 6.55 us  [return_tables(): got = lax.ppermute(sent, 'expert', [(i, i ^ bit) for i in range(experts)])]
    pallas_call x1, Pallas kernels: 1.75 us -> 1.18 us  [unit_part(): pl.pallas_call(functools.partial(unit_kernel, experts, capacity), in_spec...]
  transfers between devices with their start and end apart: 17 -> 17, of which waited for: 6 -> 5; matrix products, arithmetic and copies ran while one was open for 0% -> 0% of each run, Pallas kernels for 12% -> 10%
where the time goes in v3:
time: 39.4 us; the launch traced here: 39.2 us
  starting transfers between devices  18.6 us (47%)
  waiting for transfers between devices  12.4 us (31%)
  Pallas kernels  7.5 us (19%)
  between operations  0.75 us (2%)
    ppermute x12, starting transfers between devices, exchange(): return lax.ppermute(value, 'dp', pairs)  10.7 us
    ppermute x2, waiting for transfers between devices, return_tables(): got = lax.ppermute(sent, 'expert', [(i, i ^ bit) for i in range(experts)])  6.55 us
    ppermute x3, starting transfers between devices, on_device(): blocks.append(lax.ppermute(sent[k], 'expert', pairs))  5.79 us
    ppermute x3, waiting for transfers between devices, on_device(): blocks.append(lax.ppermute(sent[k], 'expert', pairs))  4.91 us
    ppermute x2, starting transfers between devices, return_tables(): got = lax.ppermute(sent, 'expert', [(i, i ^ bit) for i in range(experts)])  2.08 us
    pallas_call x1, Pallas kernels, pack(): pl.pallas_call(functools.partial(pack_kernel, experts, capacity, pieces),...  1.91 us
    pallas_call x1, Pallas kernels, load(): pl.pallas_call(load_kernel, in_specs=[pl.BlockSpec(memory_space=pltpu.HBM...  1.91 us
    pallas_call x1, Pallas kernels, unit_part(): pl.pallas_call(functools.partial(unit_kernel, experts, capacity), in_spec...  1.18 us
  transfers between devices with their start and end apart: 17, of which 5 were waited for; matrix products, arithmetic and copies ran while one was open for 0% of the time, Pallas kernels for 10%

profile of v3, /device:TPU:0, one launch (start us, length us, event | category | flops | bytes accessed | tf_op | source)
XLA Modules:
  0.0 39.2 jit_solution(14393703753710149004)
XLA Ops:
  0.6 1.9 %pack.1 = (bf16[168,256]{1,0:T(8,128)(2,1)S(1)}, bf16[168,256]{1,0:T(8,128)(2,1)S(1)}, bf16[168,256]{1,0:T(8,128)(2,1)S(1)}, bf16[168,256]{1,0:T(8,128)(2,1)S(1)}) custom-call(s32[8,256]{1,0:T(8,128)} %bitcast.17, s32[8,256]{1,0:T(8,128)} %bitcast.19, bf16[8,256]{1,0:T(8,128)(2,1)} %bitcast.21, bf16[256,2048]{1,0:T(8,128)(2,1)} %bitcast.24), custom_call_target="tpu_custom_call" | custom-call | tf_op jit(solution)/shard_map/pack/pallas_call | solution.py:84
  2.5 4.1 %collective-permute-start.4 = (bf16[168,256]{1,0:T(8,128)(2,1)S(1)}, bf16[168,256]{1,0:T(8,128)(2,1)S(1)}, u32[]{:S(2)}, u32[]{:S(2)}) collective-permute-start(bf16[168,256]{1,0:T(8,128)(2,1)S(1)} %get-tuple-element.31), channel_id=1, source_target_pairs={{0,2},{1,3},{2,0},{3,1},{4,6},{5,7},{6,4},{7,5},{8,10},{9,11},{10,... | collective-permute-start | bytes 258056 | tf_op jit(solution)/shard_map/ppermute | solution.py:425
  6.7 1.3 %collective-permute-start.5 = (bf16[168,256]{1,0:T(8,128)(2,1)S(1)}, bf16[168,256]{1,0:T(8,128)(2,1)S(1)}, u32[]{:S(2)}, u32[]{:S(2)}) collective-permute-start(bf16[168,256]{1,0:T(8,128)(2,1)S(1)} %get-tuple-element.32), channel_id=1, source_target_pairs={{0,3},{1,2},{2,1},{3,0},{4,7},{5,6},{6,5},{7,4},{8,11},{9,10},{10,... | collective-permute-start | bytes 258056 | tf_op jit(solution)/shard_map/ppermute | solution.py:425
  8.0 0.4 %collective-permute-start.2 = (bf16[84,768]{1,0:T(8,128)(2,1)}, bf16[84,768]{1,0:T(8,128)(2,1)S(1)}, u32[]{:S(2)}, u32[]{:S(2)}) collective-permute-start(bf16[84,768]{1,0:T(8,128)(2,1)} %bitcast.25), channel_id=1, source_target_pairs={{0,20},{4,8},{8,28},{12,0},{16,4},{20,24},{24,12},{28,16},{1,21},{... | collective-permute-start | bytes 387080 | tf_op jit(solution)/shard_map/ppermute | solution.py:332
  8.4 1.5 %collective-permute-start.1 = (bf16[84,768]{1,0:T(8,128)(2,1)}, bf16[84,768]{1,0:T(8,128)(2,1)S(1)}, u32[]{:S(2)}, u32[]{:S(2)}) collective-permute-start(bf16[84,768]{1,0:T(8,128)(2,1)} %bitcast.26), channel_id=1, source_target_pairs={{0,8},{4,20},{8,0},{12,28},{16,24},{20,4},{24,16},{28,12},{1,9},{5... | collective-permute-start | bytes 387080 | tf_op jit(solution)/shard_map/ppermute | solution.py:332
  9.9 0.9 %collective-permute-start = (bf16[84,768]{1,0:T(8,128)(2,1)}, bf16[84,768]{1,0:T(8,128)(2,1)S(1)}, u32[]{:S(2)}, u32[]{:S(2)}) collective-permute-start(bf16[84,768]{1,0:T(8,128)(2,1)} %bitcast.27), channel_id=1, source_target_pairs={{0,4},{4,0},{8,12},{12,8},{16,20},{20,16},{24,28},{28,24},{1,5},{5... | collective-permute-start | bytes 387080 | tf_op jit(solution)/shard_map/ppermute | solution.py:332
  10.9 2.6 %collective-permute-done.4.refs_0_ = bf16[168,256]{1,0:T(8,128)(2,1)S(1)} collective-permute-done((bf16[168,256]{1,0:T(8,128)(2,1)S(1)}, bf16[168,256]{1,0:T(8,128)(2,1)S(1)}, u32[]{:S(2)}, u32[]{:S(2)}) %collective-permute-start.4) | collective-permute-done | bytes 86048 | tf_op jit(solution)/shard_map/ppermute | solution.py:425
  13.5 0.3 collective-permute-start.3
  13.8 0.0 collective-permute-done.5.refs_1_
  13.8 0.3 join.3
  14.1 1.6 %collective-permute-start.9 = (bf16[42,1024]{1,0:T(8,128)(2,1)S(1)}, bf16[42,1024]{1,0:T(8,128)(2,1)S(1)}, u32[]{:S(2)}, u32[]{:S(2)}) collective-permute-start(bf16[42,1024]{1,0:T(8,128)(2,1)S(1)} %get-tuple-element.33.refs_1_), channel_id=1, source_target_pairs={{0,8},{4,20},{8,0},{12,28},{16,24},{20,4},{24,16},{28,12},{1,9},{5... | collective-permute-start | bytes 258056 | tf_op jit(solution)/shard_map/ppermute | solution.py:332
  15.6 2.3 %collective-permute-done.3.refs_1_ = bf16[168,256]{1,0:T(8,128)(2,1)S(1)} collective-permute-done((bf16[168,256]{1,0:T(8,128)(2,1)S(1)}, bf16[168,256]{1,0:T(8,128)(2,1)S(1)}, u32[]{:S(2)}, u32[]{:S(2)}) %collective-permute-start.3) | collective-permute-done | bytes 86048 | tf_op jit(solution)/shard_map/ppermute | solution.py:425
  18.0 0.0 collective-permute-start.11
  18.0 0.3 join.2
  18.3 0.0 collective-permute-done.2.refs_3_
  18.3 1.9 %collective-permute-start.7 = (bf16[42,1024]{1,0:T(8,128)(2,1)S(1)}, bf16[42,1024]{1,0:T(8,128)(2,1)S(1)}, u32[]{:S(2)}, u32[]{:S(2)}) collective-permute-start(bf16[42,1024]{1,0:T(8,128)(2,1)S(1)} %get-tuple-element.35), channel_id=1, source_target_pairs={{0,4},{4,0},{8,12},{12,8},{16,20},{20,16},{24,28},{28,24},{1,5},{5... | collective-permute-start | bytes 258056 | tf_op jit(solution)/shard_map/ppermute | solution.py:332
  20.2 0.0 collective-permute-done.1.refs_2_
  20.2 0.3 collective-permute-start.8
  20.5 0.0 collective-permute-done.refs_1_
  20.5 1.2 %collective-permute-start.10 = (bf16[42,1024]{1,0:T(8,128)(2,1)S(1)}, bf16[42,1024]{1,0:T(8,128)(2,1)S(1)}, u32[]{:S(2)}, u32[]{:S(2)}) collective-permute-start(bf16[42,1024]{1,0:T(8,128)(2,1)S(1)} %get-tuple-element.34), channel_id=1, source_target_pairs={{0,20},{4,8},{8,28},{12,0},{16,4},{20,24},{24,12},{28,16},{1,21},{... | collective-permute-start | bytes 258056 | tf_op jit(solution)/shard_map/ppermute | solution.py:332
  21.6 0.0 collective-permute-done.9.refs_5_
  21.7 0.7 %collective-permute-start.6 = (bf16[42,1024]{1,0:T(8,128)(2,1)S(1)}, bf16[42,1024]{1,0:T(8,128)(2,1)S(1)}, u32[]{:S(2)}, u32[]{:S(2)}) collective-permute-start(bf16[42,1024]{1,0:T(8,128)(2,1)S(1)} %get-tuple-element.34), channel_id=1, source_target_pairs={{0,4},{4,0},{8,12},{12,8},{16,20},{20,16},{24,28},{28,24},{1,5},{5... | collective-permute-start | bytes 258056 | tf_op jit(solution)/shard_map/ppermute | solution.py:332
  22.4 1.9 %load.1 = (bf16[768,2048]{1,0:T(8,128)(2,1)S(1)}, bf16[84,768]{1,0:T(8,128)(2,1)S(1)}) custom-call(bf16[768,2048]{1,0:T(8,128)(2,1)} %bitcast.23, bf16[84,768]{1,0:T(8,128)(2,1)} %bitcast.28), custom_call_target="tpu_custom_call" | custom-call | tf_op jit(solution)/shard_map/load/pallas_call | solution.py:147
  24.3 0.0 copy-start
  24.3 0.0 copy-start.1
  24.3 0.0 copy-start.2
  24.3 0.3 stack.1.left_ref
  24.6 0.0 collective-permute-done.11.refs_7_
  24.7 0.0 collective-permute-done.7.refs_3_
  24.7 0.9 %collective-permute-done.8.refs_4_ = bf16[42,1024]{1,0:T(8,128)(2,1)S(1)} collective-permute-done((bf16[42,1024]{1,0:T(8,128)(2,1)S(1)}, bf16[42,1024]{1,0:T(8,128)(2,1)S(1)}, u32[]{:S(2)}, u32[]{:S(2)}) %collective-permute-start.8) | collective-permute-done | bytes 86048 | tf_op jit(solution)/shard_map/ppermute | solution.py:332
  25.6 0.0 collective-permute-done.10.refs_6_
  25.6 0.0 collective-permute-done.6.refs_2_
  25.6 0.6 %partial.1 = (f32[96,1024]{1,0:T(8,128)S(1)}, bf16[96,1024]{1,0:T(8,128)(2,1)S(1)}, bf16[96,1024]{1,0:T(8,128)(2,1)S(1)}, bf16[96,1024]{1,0:T(8,128)(2,1)S(1)}) custom-call(bf16[384,384]{1,0:T(8,128)(2,1)S(1)} %stack.1.left_ref, bf16[42,1024]{1,0:T(8,128)(2,1)S(1)} %get-tuple-element.30.refs_0_, bf16[42,1024]{1,0:T(8,128)(2,1)S(1)} %get-tuple-element.33.refs_1_, ...), custom_call_target="tpu_custom_call" | custom-call | tf_op jit(solution)/shard_map/partial/pallas_call | solution.py:305
  26.2 1.9 %collective-permute-start.12 = (bf16[96,1024]{1,0:T(8,128)(2,1)S(1)}, bf16[96,1024]{1,0:T(8,128)(2,1)S(1)}, u32[]{:S(2)}, u32[]{:S(2)}) collective-permute-start(bf16[96,1024]{1,0:T(8,128)(2,1)S(1)} %get-tuple-element.37), channel_id=1, source_target_pairs={{0,16},{4,12},{8,24},{12,4},{16,0},{20,28},{24,8},{28,20},{1,17},{... | collective-permute-start | bytes 589832 | tf_op jit(solution)/shard_map/ppermute | solution.py:332
  28.0 0.0 collective-permute-start.13
  28.0 0.3 collective-permute-start.14
  28.4 1.2 %unit.1 = (bf16[84,768]{1,0:T(8,128)(2,1)S(1)}, f32[48,128]{1,0:T(8,128)S(1)}, f32[48,128]{1,0:T(8,128)S(1)}) custom-call(bf16[42,2048]{1,0:T(8,128)(2,1)S(1)} %get-tuple-element.40.near_ref, bf16[42,2048]{1,0:T(8,128)(2,1)S(1)} %get-tuple-element.41.far_ref, bf16[768,2048]{1,0:T(8,128)(2,1)S(1)} %get-tuple-element.42.weight_ref, ...), custom_call_target="tpu_custom_call" | custom-call | tf_op jit(solution)/shard_map/unit/pallas_call | solution.py:227
  29.5 0.4 collective-permute-start.15
  29.9 3.5 %collective-permute-done.15.got_ref = f32[48,128]{1,0:T(8,128)S(1)} collective-permute-done((f32[48,128]{1,0:T(8,128)S(1)}, f32[48,128]{1,0:T(8,128)S(1)}, u32[]{:S(2)}, u32[]{:S(2)}) %collective-permute-start.15) | collective-permute-done | bytes 24608 | tf_op jit(solution)/shard_map/ppermute | solution.py:263
  33.4 1.7 %collective-permute-start.16 = (f32[48,128]{1,0:T(8,128)S(1)}, f32[48,128]{1,0:T(8,128)S(1)}, u32[]{:S(2)}, u32[]{:S(2)}) collective-permute-start(f32[48,128]{1,0:T(8,128)S(1)} %get-tuple-element.46), channel_id=1, source_target_pairs={{0,2},{1,3},{2,0},{3,1},{4,6},{5,7},{6,4},{7,5},{8,10},{9,11},{10,... | collective-permute-start | bytes 73736 | tf_op jit(solution)/shard_map/ppermute | solution.py:263
  35.1 3.0 %collective-permute-done.16.refs_5_ = f32[48,128]{1,0:T(8,128)S(1)} collective-permute-done((f32[48,128]{1,0:T(8,128)S(1)}, f32[48,128]{1,0:T(8,128)S(1)}, u32[]{:S(2)}, u32[]{:S(2)}) %collective-permute-start.16) | collective-permute-done | bytes 24608 | tf_op jit(solution)/shard_map/ppermute | solution.py:263
  38.2 0.0 collective-permute-done.12.refs_1_
  38.2 0.0 collective-permute-done.13.refs_2_
  38.2 0.0 collective-permute-done.14.refs_3_
  38.2 0.0 copy-done
  38.2 0.0 copy-done.1
  38.2 0.0 copy-done.2
  38.2 1.0 %finish.1 = (f32[96,2048]{1,0:T(8,128)}, f32[8,256]{1,0:T(8,128)}, bf16[84,768]{1,0:T(8,128)(2,1)}) custom-call(f32[96,1024]{1,0:T(8,128)S(1)} %get-tuple-element.36.refs_0_, bf16[96,1024]{1,0:T(8,128)(2,1)S(1)} %collective-permute-done.12.refs_1_, bf16[96,1024]{1,0:T(8,128)(2,1)S(1)} %collective-permute-done.13.refs_2_, ...), custom_call_target="tpu_custom_call" | custom-call | tf_op jit(solution)/shard_map/finish/pallas_call | solution.py:392
  (1 shorter events, 0.0 us)
Async XLA Ops:
  2.5 10.9 %collective-permute-start.4 = (bf16[168,256]{1,0:T(8,128)(2,1)S(1)}, bf16[168,256]{1,0:T(8,128)(2,1)S(1)}, u32[]{:S(2)}, u32[]{:S(2)}) collective-permute-start(bf16[168,256]{1,0:T(8,128)(2,1)S(1)} %get-tuple-element.31), channel_id=1, source_target_pairs={{0,2},{1,3},{2,0},{3,1},{4,6},{5,7},{6,4},{7,5},{8,10},{9,11},{10,... | collective-permute-start | bytes 258056 | tf_op jit(solution)/shard_map/ppermute | solution.py:425
  6.7 7.1 %collective-permute-start.5 = (bf16[168,256]{1,0:T(8,128)(2,1)S(1)}, bf16[168,256]{1,0:T(8,128)(2,1)S(1)}, u32[]{:S(2)}, u32[]{:S(2)}) collective-permute-start(bf16[168,256]{1,0:T(8,128)(2,1)S(1)} %get-tuple-element.32), channel_id=1, source_target_pairs={{0,3},{1,2},{2,1},{3,0},{4,7},{5,6},{6,5},{7,4},{8,11},{9,10},{10,... | collective-permute-start | bytes 258056 | tf_op jit(solution)/shard_map/ppermute | solution.py:425
  8.0 10.2 %collective-permute-start.2 = (bf16[84,768]{1,0:T(8,128)(2,1)}, bf16[84,768]{1,0:T(8,128)(2,1)S(1)}, u32[]{:S(2)}, u32[]{:S(2)}) collective-permute-start(bf16[84,768]{1,0:T(8,128)(2,1)} %bitcast.25), channel_id=1, source_target_pairs={{0,20},{4,8},{8,28},{12,0},{16,4},{20,24},{24,12},{28,16},{1,21},{... | collective-permute-start | bytes 387080 | tf_op jit(solution)/shard_map/ppermute | solution.py:332
  8.4 11.8 %collective-permute-start.1 = (bf16[84,768]{1,0:T(8,128)(2,1)}, bf16[84,768]{1,0:T(8,128)(2,1)S(1)}, u32[]{:S(2)}, u32[]{:S(2)}) collective-permute-start(bf16[84,768]{1,0:T(8,128)(2,1)} %bitcast.26), channel_id=1, source_target_pairs={{0,8},{4,20},{8,0},{12,28},{16,24},{20,4},{24,16},{28,12},{1,9},{5... | collective-permute-start | bytes 387080 | tf_op jit(solution)/shard_map/ppermute | solution.py:332
  9.9 10.5 %collective-permute-start = (bf16[84,768]{1,0:T(8,128)(2,1)}, bf16[84,768]{1,0:T(8,128)(2,1)S(1)}, u32[]{:S(2)}, u32[]{:S(2)}) collective-permute-start(bf16[84,768]{1,0:T(8,128)(2,1)} %bitcast.27), channel_id=1, source_target_pairs={{0,4},{4,0},{8,12},{12,8},{16,20},{20,16},{24,28},{28,24},{1,5},{5... | collective-permute-start | bytes 387080 | tf_op jit(solution)/shard_map/ppermute | solution.py:332
  13.5 4.5 %collective-permute-start.3 = (bf16[168,256]{1,0:T(8,128)(2,1)S(1)}, bf16[168,256]{1,0:T(8,128)(2,1)S(1)}, u32[]{:S(2)}, u32[]{:S(2)}) collective-permute-start(bf16[168,256]{1,0:T(8,128)(2,1)S(1)} %get-tuple-element.29), channel_id=1, source_target_pairs={{0,1},{1,0},{2,3},{3,2},{4,5},{5,4},{6,7},{7,6},{8,9},{9,8},{10,11... | collective-permute-start | bytes 258056 | tf_op jit(solution)/shard_map/ppermute | solution.py:425
  14.1 7.6 %collective-permute-start.9 = (bf16[42,1024]{1,0:T(8,128)(2,1)S(1)}, bf16[42,1024]{1,0:T(8,128)(2,1)S(1)}, u32[]{:S(2)}, u32[]{:S(2)}) collective-permute-start(bf16[42,1024]{1,0:T(8,128)(2,1)S(1)} %get-tuple-element.33.refs_1_), channel_id=1, source_target_pairs={{0,8},{4,20},{8,0},{12,28},{16,24},{20,4},{24,16},{28,12},{1,9},{5... | collective-permute-start | bytes 258056 | tf_op jit(solution)/shard_map/ppermute | solution.py:332
  18.0 6.7 %collective-permute-start.11 = (bf16[42,1024]{1,0:T(8,128)(2,1)S(1)}, bf16[42,1024]{1,0:T(8,128)(2,1)S(1)}, u32[]{:S(2)}, u32[]{:S(2)}) collective-permute-start(bf16[42,1024]{1,0:T(8,128)(2,1)S(1)} %get-tuple-element.35), channel_id=1, source_target_pairs={{0,20},{4,8},{8,28},{12,0},{16,4},{20,24},{24,12},{28,16},{1,21},{... | collective-permute-start | bytes 258056 | tf_op jit(solution)/shard_map/ppermute | solution.py:332
  18.3 6.4 %collective-permute-start.7 = (bf16[42,1024]{1,0:T(8,128)(2,1)S(1)}, bf16[42,1024]{1,0:T(8,128)(2,1)S(1)}, u32[]{:S(2)}, u32[]{:S(2)}) collective-permute-start(bf16[42,1024]{1,0:T(8,128)(2,1)S(1)} %get-tuple-element.35), channel_id=1, source_target_pairs={{0,4},{4,0},{8,12},{12,8},{16,20},{20,16},{24,28},{28,24},{1,5},{5... | collective-permute-start | bytes 258056 | tf_op jit(solution)/shard_map/ppermute | solution.py:332
  20.2 5.4 %collective-permute-start.8 = (bf16[42,1024]{1,0:T(8,128)(2,1)S(1)}, bf16[42,1024]{1,0:T(8,128)(2,1)S(1)}, u32[]{:S(2)}, u32[]{:S(2)}) collective-permute-start(bf16[42,1024]{1,0:T(8,128)(2,1)S(1)} %get-tuple-element.30.refs_0_), channel_id=1, source_target_pairs={{0,8},{4,20},{8,0},{12,28},{16,24},{20,4},{24,16},{28,12},{1,9},{5... | collective-permute-start | bytes 258056 | tf_op jit(solution)/shard_map/ppermute | solution.py:332
  20.5 5.1 %collective-permute-start.10 = (bf16[42,1024]{1,0:T(8,128)(2,1)S(1)}, bf16[42,1024]{1,0:T(8,128)(2,1)S(1)}, u32[]{:S(2)}, u32[]{:S(2)}) collective-permute-start(bf16[42,1024]{1,0:T(8,128)(2,1)S(1)} %get-tuple-element.34), channel_id=1, source_target_pairs={{0,20},{4,8},{8,28},{12,0},{16,4},{20,24},{24,12},{28,16},{1,21},{... | collective-permute-start | bytes 258056 | tf_op jit(solution)/shard_map/ppermute | solution.py:332
  21.7 3.9 %collective-permute-start.6 = (bf16[42,1024]{1,0:T(8,128)(2,1)S(1)}, bf16[42,1024]{1,0:T(8,128)(2,1)S(1)}, u32[]{:S(2)}, u32[]{:S(2)}) collective-permute-start(bf16[42,1024]{1,0:T(8,128)(2,1)S(1)} %get-tuple-element.34), channel_id=1, source_target_pairs={{0,4},{4,0},{8,12},{12,8},{16,20},{20,16},{24,28},{28,24},{1,5},{5... | collective-permute-start | bytes 258056 | tf_op jit(solution)/shard_map/ppermute | solution.py:332
  24.3 13.9 %copy-start = (s32[1,256,8]{1,2,0:T(8,128)S(1)}, s32[1,256,8]{1,2,0:T(8,128)}, u32[]{:S(2)}) copy-start(s32[1,256,8]{1,2,0:T(8,128)} %param.8) | copy-start | bytes 24580
  24.3 13.9 %copy-start.1 = (s32[1,256,8]{1,2,0:T(8,128)S(1)}, s32[1,256,8]{1,2,0:T(8,128)}, u32[]{:S(2)}) copy-start(s32[1,256,8]{1,2,0:T(8,128)} %param.9) | copy-start | bytes 24580
  24.3 13.9 %copy-start.2 = (bf16[1,256,8]{1,2,0:T(8,128)(2,1)S(1)}, bf16[1,256,8]{1,2,0:T(8,128)(2,1)}, u32[]{:S(2)}) copy-start(bf16[1,256,8]{1,2,0:T(8,128)(2,1)} %param.7) | copy-start | bytes 12292
  26.2 12.0 %collective-permute-start.12 = (bf16[96,1024]{1,0:T(8,128)(2,1)S(1)}, bf16[96,1024]{1,0:T(8,128)(2,1)S(1)}, u32[]{:S(2)}, u32[]{:S(2)}) collective-permute-start(bf16[96,1024]{1,0:T(8,128)(2,1)S(1)} %get-tuple-element.37), channel_id=1, source_target_pairs={{0,16},{4,12},{8,24},{12,4},{16,0},{20,28},{24,8},{28,20},{1,17},{... | collective-permute-start | bytes 589832 | tf_op jit(solution)/shard_map/ppermute | solution.py:332
  28.0 10.2 %collective-permute-start.13 = (bf16[96,1024]{1,0:T(8,128)(2,1)S(1)}, bf16[96,1024]{1,0:T(8,128)(2,1)S(1)}, u32[]{:S(2)}, u32[]{:S(2)}) collective-permute-start(bf16[96,1024]{1,0:T(8,128)(2,1)S(1)} %get-tuple-element.38), channel_id=1, source_target_pairs={{0,4},{4,0},{8,12},{12,8},{16,20},{20,16},{24,28},{28,24},{1,5},{5... | collective-permute-start | bytes 589832 | tf_op jit(solution)/shard_map/ppermute | solution.py:332
  28.0 10.2 %collective-permute-start.14 = (bf16[96,1024]{1,0:T(8,128)(2,1)S(1)}, bf16[96,1024]{1,0:T(8,128)(2,1)S(1)}, u32[]{:S(2)}, u32[]{:S(2)}) collective-permute-start(bf16[96,1024]{1,0:T(8,128)(2,1)S(1)} %get-tuple-element.39), channel_id=1, source_target_pairs={{0,20},{4,8},{8,28},{12,0},{16,4},{20,24},{24,12},{28,16},{1,21},{... | collective-permute-start | bytes 589832 | tf_op jit(solution)/shard_map/ppermute | solution.py:332
  29.5 3.9 %collective-permute-start.15 = (f32[48,128]{1,0:T(8,128)S(1)}, f32[48,128]{1,0:T(8,128)S(1)}, u32[]{:S(2)}, u32[]{:S(2)}) collective-permute-start(f32[48,128]{1,0:T(8,128)S(1)} %get-tuple-element.44), channel_id=1, source_target_pairs={{0,1},{1,0},{2,3},{3,2},{4,5},{5,4},{6,7},{7,6},{8,9},{9,8},{10,11... | collective-permute-start | bytes 73736 | tf_op jit(solution)/shard_map/ppermute | solution.py:263
  33.4 4.7 %collective-permute-start.16 = (f32[48,128]{1,0:T(8,128)S(1)}, f32[48,128]{1,0:T(8,128)S(1)}, u32[]{:S(2)}, u32[]{:S(2)}) collective-permute-start(f32[48,128]{1,0:T(8,128)S(1)} %get-tuple-element.46), channel_id=1, source_target_pairs={{0,2},{1,3},{2,0},{3,1},{4,6},{5,7},{6,4},{7,5},{8,10},{9,11},{10,... | collective-permute-start | bytes 73736 | tf_op jit(solution)/shard_map/ppermute | solution.py:263

commit v4 on v3

--- a/solution.py
+++ b/solution.py
@@ -79,7 +79,7 @@
 
 def pack(ids, slots, gates, grad, experts, capacity):
     dense = (CHUNKS * capacity, grad.shape[1] // CHUNKS)
-    pieces = 4
+    pieces = 2
     arrays = (ids, slots, gates, grad)
     return pl.pallas_call(
         functools.partial(pack_kernel, experts, capacity, pieces),
@@ -93,8 +93,26 @@
     )(*map(in_hbm, arrays))
 
 
+def reorder(pieces):
+    me = lax.axis_index("expert")
+    bit = 1
+    while bit < len(pieces):
+        swap = (me // bit) % 2 == 1
+        pieces = [jnp.where(swap, pieces[n ^ bit], piece) for n, piece in enumerate(pieces)]
+        bit *= 2
+    return pieces
+
+
+def cut_rows(values, starts, capacity):
+    return [values[start : start + capacity, :] for start in starts]
+
+
+def pad16(n):
+    return -(-n // 16) * 16
+
+
 def rows_of(block, first, rows, capacity):
-    shape = (CHUNKS, -(-rows // 16) * 16, CHUNKS * capacity)
+    shape = (CHUNKS, pad16(rows), CHUNKS * capacity)
     chunk = lax.broadcasted_iota(jnp.int32, shape, 0)
     slot = lax.broadcasted_iota(jnp.int32, shape, 1) - first
     source = lax.broadcasted_iota(jnp.int32, shape, 2)
@@ -103,33 +121,40 @@
     return jnp.dot(place, block[...], preferred_element_type=F32)
 
 
-def join_kernel(first, capacity, *refs):
-    count = len(refs) - 3
-    me = lax.axis_index("expert")
+def join_kernel(count, capacity, *refs):
     core = lax.axis_index("dp") % 2
-    part_ref, own_ref, other_ref = refs[count:]
+    extra = (len(refs) - count - 3) // 2
+    before, (part_ref, own_ref, other_ref, *pair) = refs[count : count + extra], refs[count + extra :]
     rows, half = own_ref.shape
     total = 0.0
     for k, block in enumerate(refs[:count]):
-        total += rows_of(block, ((me ^ (first + k)) % count) * capacity, rows, capacity)
+        total += rows_of(block, k * capacity, rows, capacity)
     tall, chunk = total.shape[0] // CHUNKS, total.shape[1]
     for c in range(CHUNKS):
         part_ref[:, c * chunk : (c + 1) * chunk] = total[c * tall : c * tall + rows, :].astype(BF16)
     own_ref[...] = part_ref[:, pl.ds(pl.multiple_of(core * half, 128), half)]
     other_ref[...] = part_ref[:, pl.ds(pl.multiple_of((1 - core) * half, 128), half)]
-
-
-def join(blocks, first, capacity):
+    if before:
+        pair[0][...] = jnp.zeros_like(pair[0])
+        at = before[0].shape[0]
+        pair[0][:at, :] = before[0][...]
+        pair[0][pad16(at) : pad16(at) + rows, :] = other_ref[...]
+
+
+def join(blocks, capacity, before=()):
     rows, width = len(blocks) * capacity, blocks[0].shape[1] * CHUNKS
     vmem = pl.BlockSpec(memory_space=pltpu.VMEM)
     return pl.pallas_call(
-        functools.partial(join_kernel, first, capacity),
-        in_specs=[vmem] * len(blocks),
-        out_specs=[vmem] * 3,
-        out_shape=[jax.ShapeDtypeStruct((rows, w), BF16) for w in (width, width // 2, width // 2)],
+        functools.partial(join_kernel, len(blocks), capacity),
+        in_specs=[vmem] * (len(blocks) + len(before)),
+        out_specs=[vmem] * (3 + len(before)),
+        out_shape=[jax.ShapeDtypeStruct((rows, w), BF16) for w in (width, width // 2, width // 2)]
+        + [
+            jax.ShapeDtypeStruct((pad16(b.shape[0]) + pad16(rows), b.shape[1]), BF16) for b in before
+        ],
         compiler_params=params(),
         name="join",
-    )(*blocks)
+    )(*blocks, *before)
 
 
 def load_kernel(weight_hbm, hidden_hbm, weight_ref, hidden_ref, sems):
@@ -157,17 +182,22 @@
 
 def stack_kernel(side, count, depth, *refs):
     hiddens, (left_ref, stack_ref, turned_ref) = refs[:count], refs[count:]
-    slots, units = hiddens[0].shape
-    rows = slots // 2
-    upper = lax.axis_index("expert") // (lax.axis_size("expert") // 2)
+    slots, _ = hiddens[0].shape
+    experts = lax.axis_size("expert")
+    capacity = slots // experts
+    me = lax.axis_index("expert")
+    row = lax.broadcasted_iota(jnp.int32, (depth, slots), 0)
+    col = lax.broadcasted_iota(jnp.int32, (depth, slots), 1)
+    place = jnp.zeros(row.shape, F32)
+    for k in range(experts):
+        start = k * capacity if k < experts - 1 else pad16(slots - capacity)
+        inside = (row >= start) & (row < start + capacity)
+        place = jnp.where(inside & (col == row - start + (me ^ k) * capacity), 1.0, place)
+    place = place.astype(BF16)
     for n, hidden in enumerate(hiddens):
-        values = hidden[...].astype(F32)
-        lower, higher = values[:rows, :], values[rows:, :]
-        for part in range(2):
-            at = (2 * n + part) * depth
-            stack_ref[at : at + rows, :] = jnp.where(upper == part, lower, higher)
-            if rows < depth:
-                stack_ref[at + rows : at + depth, :] = jnp.zeros((depth - rows, units), F32)
+        stack_ref[n * depth : (n + 1) * depth, :] = jnp.dot(
+            place, hidden[...], preferred_element_type=F32
+        )
     turned_ref[...] = stack_ref[...].T
     index = lax.axis_index("dp")
     masks = owner_masks(side)
@@ -186,10 +216,10 @@
         functools.partial(stack_kernel, side, count, depth),
         in_specs=[vmem] * count,
         out_specs=vmem,
-        out_shape=jax.ShapeDtypeStruct((2 * side * height, 2 * count * depth), BF16),
+        out_shape=jax.ShapeDtypeStruct((2 * side * height, count * depth), BF16),
         scratch_shapes=[
-            pltpu.VMEM((2 * count * depth, units), F32),
-            pltpu.VMEM((units, 2 * count * depth), F32),
+            pltpu.VMEM((count * depth, units), F32),
+            pltpu.VMEM((units, count * depth), F32),
         ],
         compiler_params=params(),
         name="stack",
@@ -197,15 +227,16 @@
 
 
 def unit_kernel(experts, capacity, near_ref, far_ref, weight_ref, hidden_ref, *refs):
-    grad_ref, kept_ref, sent_ref, full_ref, sums_ref = refs
+    grad_ref, kept_ref, sent_ref, full_ref, unit_ref, sums_ref = refs
     me = lax.axis_index("expert")
-    rows = near_ref.shape[0]
-    lower = me // (experts // 2) == 0
-    near = near_ref[...]
-    far = far_ref[...]
-    full_ref[:rows, :] = jnp.where(lower, near, far)
-    full_ref[rows : 2 * rows, :] = jnp.where(lower, far, near)
-    unit = matmul_t(full_ref[...], weight_ref[...], (1, 1))
+    far_at = pad16(near_ref.shape[0])
+    full_ref[: near_ref.shape[0], :] = near_ref[...]
+    full_ref[far_at : far_at + capacity, :] = far_ref[...]
+    moved = matmul_t(full_ref[...], weight_ref[...], (1, 1))
+    starts = [n * capacity for n in range(experts - 1)] + [far_at]
+    for n, piece in enumerate(reorder(cut_rows(moved, starts, capacity))):
+        unit_ref[n * capacity : (n + 1) * capacity, :] = piece
+    unit = unit_ref[...]
     grad_ref[...] = unit.astype(BF16)
     sums = jnp.sum(unit * hidden_ref[...].astype(F32), axis=1, keepdims=True)
     sums_ref[...] = jnp.zeros_like(sums_ref)
@@ -218,10 +249,10 @@
 
 
 def unit_part(near, far, weight, hidden, experts):
-    rows, width = near.shape
-    slots = 2 * rows
+    width = near.shape[1]
+    capacity = far.shape[0]
+    slots = capacity * experts
     units = weight.shape[0]
-    capacity = slots // experts
     table = jax.ShapeDtypeStruct((experts // 2 * pad8(capacity), 128), F32)
     vmem = pl.BlockSpec(memory_space=pltpu.VMEM)
     return pl.pallas_call(
@@ -230,7 +261,8 @@
         out_specs=[vmem] * 3,
         out_shape=[jax.ShapeDtypeStruct((slots, units), BF16), table, table],
         scratch_shapes=[
-            pltpu.VMEM((slots, width), BF16),
+            pltpu.VMEM((pad16(near.shape[0]) + pad16(capacity), width), BF16),
+            pltpu.VMEM((slots, units), F32),
             pltpu.VMEM((pad8(slots) + 8, 128), F32),
         ],
         compiler_params=params(),
@@ -280,37 +312,36 @@
         slots = [slot for slot in slots if not slot & bit]
 
 
-def partial_kernel(depth, left_ref, *refs):
-    count = (len(refs) - 1) // 3 * 2
-    rows, outs, right_ref = refs[:count], refs[count:-1], refs[-1]
-    slots = rows[0].shape[0]
-    for n, row in enumerate(rows):
-        right_ref[n * depth : n * depth + slots, :] = row[...]
-        if slots < depth:
-            right_ref[n * depth + slots : (n + 1) * depth, :] = jnp.zeros(
-                (depth - slots, right_ref.shape[1]), BF16
-            )
+def partial_kernel(depth, left_ref, pair_ref, *refs):
+    count = (len(refs) - 2) // 3
+    nears, fars, outs, right_ref = refs[:count], refs[count : 2 * count], refs[2 * count : -1], refs[-1]
+    for n, (near, far) in enumerate(zip(nears, fars)):
+        right_ref[n * depth : (n + 1) * depth, :] = jnp.zeros((depth, right_ref.shape[1]), BF16)
+        at = n * depth
+        right_ref[at : at + near.shape[0], :] = near[...]
+        at += pad16(near.shape[0])
+        right_ref[at : at + far.shape[0], :] = far[...]
+    right_ref[count * depth :, :] = pair_ref[...]
     height = outs[0].shape[0]
     total = jnp.dot(left_ref[...], right_ref[...], preferred_element_type=F32)
     for n, out in enumerate(outs):
         out[...] = total[n * height : (n + 1) * height, :].astype(out.dtype)
 
 
-def partial(left, rows, depth):
-    count = len(rows)
-    half = rows[0].shape[1]
-    owners = count // 2
-    height = left.shape[0] // owners
+def partial(left, nears, fars, pair):
+    count = len(nears) + 1
+    depth, half = pair.shape
+    height = left.shape[0] // count
     vmem = pl.BlockSpec(memory_space=pltpu.VMEM)
     return pl.pallas_call(
         functools.partial(partial_kernel, depth),
-        in_specs=[vmem] * (1 + count),
-        out_specs=[vmem] * owners,
-        out_shape=[jax.ShapeDtypeStruct((height, half), F32 if n == 0 else BF16) for n in range(owners)],
+        in_specs=[vmem] * (2 * count),
+        out_specs=[vmem] * count,
+        out_shape=[jax.ShapeDtypeStruct((height, half), F32 if n == 0 else BF16) for n in range(count)],
         scratch_shapes=[pltpu.VMEM((count * depth, half), BF16)],
         compiler_params=params(),
         name="partial",
-    )(left, *rows)
+    )(left, pair, *nears, *fars)
 
 
 def gather_masks(side):
@@ -430,23 +461,25 @@
     for mask in routes:
         moved_hiddens.append(exchange(hidden, replicas, mask))
 
-    depth = -(-hidden.shape[0] // 32) * 16
+    depth = pad16(hidden.shape[0] - capacity) + pad16(capacity)
     height = hidden.shape[1] // replicas
     weight, hidden = load(weight, hidden)
-    left = stack([hidden] + moved_hiddens, side, depth, height)
-
-    parts, rows = [], []
-    for first in (0, experts // 2):
-        part, own, other = join(blocks[first : first + experts // 2], first, capacity)
+    left = stack([hidden] + moved_hiddens[1:] + moved_hiddens[:1], side, depth, height)
+
+    parts, rows, before = [], [], []
+    for received in (blocks[:-1], blocks[-1:]):
+        part, own, other, *pair = join(received, capacity, before)
         parts.append(part)
         rows.append([own])
-        for mask in routes:
+        before = [other]
+        for n, mask in enumerate(routes[1:], 1):
             rows[-1].append(exchange(own if mask in same else other, replicas, mask))
+    pair = exchange(pair[0], replicas, routes[0])
 
     hidden_grad, kept, sent = unit_part(*parts, weight, hidden, experts)
     tables, origins = return_tables(kept, sent, experts, pad8(capacity))
 
-    cut = partial(left, [r for pair in zip(*rows) for r in pair], depth)
+    cut = partial(left, *rows, pair)
     moved = []
     for n, mask in enumerate(owner_masks(side)[1:]):
         moved.append(exchange(cut[n + 1], replicas, mask))

time: 39.4 us -> 40.4 us (1.025)
  waiting for transfers between devices: 12.4 us -> 13.4 us
    ppermute x12 -> x11, waiting for transfers between devices: 0.93 us -> 2.69 us  [exchange(): return lax.ppermute(value, 'dp', pairs)]
    ppermute x2, starting transfers between devices: 2.08 us -> 3.21 us  [return_tables(): got = lax.ppermute(sent, 'expert', [(i, i ^ bit) for i in range(experts)])]
    ppermute x12 -> x11, starting transfers between devices: 10.7 us -> 9.56 us  [exchange(): return lax.ppermute(value, 'dp', pairs)]
    ppermute x2, waiting for transfers between devices: 6.55 us -> 5.49 us  [return_tables(): got = lax.ppermute(sent, 'expert', [(i, i ^ bit) for i in range(experts)])]
  transfers between devices with their start and end apart: 17 -> 16, of which waited for: 5 -> 5; matrix products, arithmetic and copies ran while one was open for 0% -> 0% of each run, Pallas kernels for 10% -> 11%
where the time goes in v4:
time: 40.4 us; the launch traced here: 40.1 us
  starting transfers between devices  18.5 us (46%)
  waiting for transfers between devices  13.4 us (33%)
  Pallas kernels  7.5 us (19%)
  between operations  0.76 us (2%)
    ppermute x11, starting transfers between devices, exchange(): return lax.ppermute(value, 'dp', pairs)  9.56 us
    ppermute x3, starting transfers between devices, on_device(): blocks.append(lax.ppermute(sent[k], 'expert', pairs))  5.71 us
    ppermute x2, waiting for transfers between devices, return_tables(): got = lax.ppermute(sent, 'expert', [(i, i ^ bit) for i in range(experts)])  5.49 us
    ppermute x3, waiting for transfers between devices, on_device(): blocks.append(lax.ppermute(sent[k], 'expert', pairs))  5.2 us
    ppermute x2, starting transfers between devices, return_tables(): got = lax.ppermute(sent, 'expert', [(i, i ^ bit) for i in range(experts)])  3.21 us
    ppermute x11, waiting for transfers between devices, exchange(): return lax.ppermute(value, 'dp', pairs)  2.69 us
    pallas_call x1, Pallas kernels, load(): pl.pallas_call(load_kernel, in_specs=[pl.BlockSpec(memory_space=pltpu.HBM...  1.91 us
    pallas_call x1, Pallas kernels, pack(): pl.pallas_call(functools.partial(pack_kernel, experts, capacity, pieces),...  1.6 us
  transfers between devices with their start and end apart: 16, of which 5 were waited for; matrix products, arithmetic and copies ran while one was open for 0% of the time, Pallas kernels for 11%

profile of v4, /device:TPU:0, one launch (start us, length us, event | category | flops | bytes accessed | tf_op | source)
XLA Modules:
  0.0 40.1 jit_solution(15985429263596258459)
XLA Ops:
  0.6 1.6 %pack.1 = (bf16[168,256]{1,0:T(8,128)(2,1)S(1)}, bf16[168,256]{1,0:T(8,128)(2,1)S(1)}, bf16[168,256]{1,0:T(8,128)(2,1)S(1)}, bf16[168,256]{1,0:T(8,128)(2,1)S(1)}) custom-call(s32[8,256]{1,0:T(8,128)} %bitcast.17, s32[8,256]{1,0:T(8,128)} %bitcast.19, bf16[8,256]{1,0:T(8,128)(2,1)} %bitcast.21, bf16[256,2048]{1,0:T(8,128)(2,1)} %bitcast.24), custom_call_target="tpu_custom_call" | custom-call | tf_op jit(solution)/shard_map/pack/pallas_call | solution.py:84
  2.2 3.1 %collective-permute-start.4 = (bf16[168,256]{1,0:T(8,128)(2,1)S(1)}, bf16[168,256]{1,0:T(8,128)(2,1)S(1)}, u32[]{:S(2)}, u32[]{:S(2)}) collective-permute-start(bf16[168,256]{1,0:T(8,128)(2,1)S(1)} %get-tuple-element.31), channel_id=1, source_target_pairs={{0,1},{1,0},{2,3},{3,2},{4,5},{5,4},{6,7},{7,6},{8,9},{9,8},{10,11... | collective-permute-start | bytes 258056 | tf_op jit(solution)/shard_map/ppermute | solution.py:456
  5.4 2.6 %collective-permute-start.5 = (bf16[168,256]{1,0:T(8,128)(2,1)S(1)}, bf16[168,256]{1,0:T(8,128)(2,1)S(1)}, u32[]{:S(2)}, u32[]{:S(2)}) collective-permute-start(bf16[168,256]{1,0:T(8,128)(2,1)S(1)} %get-tuple-element.32), channel_id=1, source_target_pairs={{0,2},{1,3},{2,0},{3,1},{4,6},{5,7},{6,4},{7,5},{8,10},{9,11},{10,... | collective-permute-start | bytes 258056 | tf_op jit(solution)/shard_map/ppermute | solution.py:456
  7.9 0.0 collective-permute-start.3
  8.0 1.7 %collective-permute-start = (bf16[84,768]{1,0:T(8,128)(2,1)}, bf16[84,768]{1,0:T(8,128)(2,1)S(1)}, u32[]{:S(2)}, u32[]{:S(2)}) collective-permute-start(bf16[84,768]{1,0:T(8,128)(2,1)} %bitcast.25), channel_id=1, source_target_pairs={{0,8},{4,20},{8,0},{12,28},{16,24},{20,4},{24,16},{28,12},{1,9},{5... | collective-permute-start | bytes 387080 | tf_op jit(solution)/shard_map/ppermute | solution.py:363
  9.7 0.0 collective-permute-done.4.refs_1_
  9.7 5.2 %collective-permute-done.5.refs_2_ = bf16[168,256]{1,0:T(8,128)(2,1)S(1)} collective-permute-done((bf16[168,256]{1,0:T(8,128)(2,1)S(1)}, bf16[168,256]{1,0:T(8,128)(2,1)S(1)}, u32[]{:S(2)}, u32[]{:S(2)}) %collective-permute-start.5) | collective-permute-done | bytes 86048 | tf_op jit(solution)/shard_map/ppermute | solution.py:456
  14.9 0.4 %join.2 = (bf16[63,2048]{1,0:T(8,128)(2,1)S(1)}, bf16[63,1024]{1,0:T(8,128)(2,1)S(1)}, bf16[63,1024]{1,0:T(8,128)(2,1)S(1)}) custom-call(bf16[168,256]{1,0:T(8,128)(2,1)S(1)} %get-tuple-element.30.refs_0_, bf16[168,256]{1,0:T(8,128)(2,1)S(1)} %collective-permute-done.4.refs_1_, bf16[168,256]{1,0:T(8,128)(2,1)S(1)} %collective-permute-done.5.refs_2_), custom_call_target="tpu_custom_call" | custom-call | tf_op jit(solution)/shard_map/join/pallas_call | solution.py:147
  15.3 0.0 collective-permute-done.3.refs_0_
  15.3 0.2 join.3
  15.5 0.1 collective-permute-start.6
  15.6 1.6 %collective-permute-start.1 = (bf16[84,768]{1,0:T(8,128)(2,1)}, bf16[84,768]{1,0:T(8,128)(2,1)S(1)}, u32[]{:S(2)}, u32[]{:S(2)}) collective-permute-start(bf16[84,768]{1,0:T(8,128)(2,1)} %bitcast.26), channel_id=1, source_target_pairs={{0,20},{4,8},{8,28},{12,0},{16,4},{20,24},{24,12},{28,16},{1,21},{... | collective-permute-start | bytes 387080 | tf_op jit(solution)/shard_map/ppermute | solution.py:363
  17.2 0.0 collective-permute-start.2
  17.2 1.5 %collective-permute-start.7 = (bf16[63,1024]{1,0:T(8,128)(2,1)S(1)}, bf16[63,1024]{1,0:T(8,128)(2,1)S(1)}, u32[]{:S(2)}, u32[]{:S(2)}) collective-permute-start(bf16[63,1024]{1,0:T(8,128)(2,1)S(1)} %get-tuple-element.35.refs_0_), channel_id=1, source_target_pairs={{0,8},{4,20},{8,0},{12,28},{16,24},{20,4},{24,16},{28,12},{1,9},{5... | collective-permute-start | bytes 387080 | tf_op jit(solution)/shard_map/ppermute | solution.py:363
  18.7 0.0 collective-permute-done.refs_1_
  18.7 0.4 collective-permute-start.8
  19.1 2.0 %collective-permute-done.1.refs_2_ = bf16[84,768]{1,0:T(8,128)(2,1)S(1)} collective-permute-done((bf16[84,768]{1,0:T(8,128)(2,1)}, bf16[84,768]{1,0:T(8,128)(2,1)S(1)}, u32[]{:S(2)}, u32[]{:S(2)}) %collective-permute-start.1) | collective-permute-done | bytes 129056 | tf_op jit(solution)/shard_map/ppermute | solution.py:363
  21.1 1.7 %collective-permute-start.9 = (bf16[21,1024]{1,0:T(8,128)(2,1)S(1)}, bf16[21,1024]{1,0:T(8,128)(2,1)S(1)}, u32[]{:S(2)}, u32[]{:S(2)}) collective-permute-start(bf16[21,1024]{1,0:T(8,128)(2,1)S(1)} %get-tuple-element.36.refs_3_), channel_id=1, source_target_pairs={{0,8},{4,20},{8,0},{12,28},{16,24},{20,4},{24,16},{28,12},{1,9},{5... | collective-permute-start | bytes 129032 | tf_op jit(solution)/shard_map/ppermute | solution.py:363
  22.8 0.0 collective-permute-done.2.refs_3_
  22.8 0.4 %collective-permute-start.10 = (bf16[21,1024]{1,0:T(8,128)(2,1)S(1)}, bf16[21,1024]{1,0:T(8,128)(2,1)S(1)}, u32[]{:S(2)}, u32[]{:S(2)}) collective-permute-start(bf16[21,1024]{1,0:T(8,128)(2,1)S(1)} %get-tuple-element.37), channel_id=1, source_target_pairs={{0,20},{4,8},{8,28},{12,0},{16,4},{20,24},{24,12},{28,16},{1,21},{... | collective-permute-start | bytes 129032 | tf_op jit(solution)/shard_map/ppermute | solution.py:363
  23.2 1.9 %load.1 = (bf16[768,2048]{1,0:T(8,128)(2,1)S(1)}, bf16[84,768]{1,0:T(8,128)(2,1)S(1)}) custom-call(bf16[768,2048]{1,0:T(8,128)(2,1)} %bitcast.23, bf16[84,768]{1,0:T(8,128)(2,1)} %bitcast.28), custom_call_target="tpu_custom_call" | custom-call | tf_op jit(solution)/shard_map/load/pallas_call | solution.py:172
  25.1 0.0 copy-start
  25.1 0.0 copy-start.1
  25.1 0.0 copy-start.2
  25.2 0.6 %stack.1.left_ref = bf16[384,384]{1,0:T(8,128)(2,1)S(1)} custom-call(bf16[84,768]{1,0:T(8,128)(2,1)S(1)} %get-tuple-element.28.refs_0_.hidden_ref, bf16[84,768]{1,0:T(8,128)(2,1)S(1)} %collective-permute-done.refs_1_, bf16[84,768]{1,0:T(8,128)(2,1)S(1)} %collective-permute-done.1.refs_2_, bf16[84,768]{1,0:T(8,128)(2,1)S(1)} %collective-permute-done.2.refs_3_), custom_call_target="tpu_custom_call" | custom-call | tf_op jit(solution)/shard_map/stack/pallas_call | solution.py:215
  25.7 0.0 collective-permute-done.9.refs_4_
  25.7 0.6 %collective-permute-done.10.refs_5_ = bf16[21,1024]{1,0:T(8,128)(2,1)S(1)} collective-permute-done((bf16[21,1024]{1,0:T(8,128)(2,1)S(1)}, bf16[21,1024]{1,0:T(8,128)(2,1)S(1)}, u32[]{:S(2)}, u32[]{:S(2)}) %collective-permute-start.10) | collective-permute-done | bytes 43040 | tf_op jit(solution)/shard_map/ppermute | solution.py:363
  26.4 0.0 collective-permute-done.7.refs_1_
  26.4 0.0 collective-permute-done.8.refs_2_
  26.4 0.0 collective-permute-done.6.pair_ref
  26.4 0.6 %partial.1 = (f32[96,1024]{1,0:T(8,128)S(1)}, bf16[96,1024]{1,0:T(8,128)(2,1)S(1)}, bf16[96,1024]{1,0:T(8,128)(2,1)S(1)}, bf16[96,1024]{1,0:T(8,128)(2,1)S(1)}) custom-call(bf16[384,384]{1,0:T(8,128)(2,1)S(1)} %stack.1.left_ref, bf16[96,1024]{1,0:T(8,128)(2,1)S(1)} %collective-permute-done.6.pair_ref, bf16[63,1024]{1,0:T(8,128)(2,1)S(1)} %get-tuple-element.35.refs_0_, ...), custom_call_target="tpu_custom_call" | custom-call | tf_op jit(solution)/shard_map/partial/pallas_call | solution.py:336
  27.0 1.2 %collective-permute-start.11 = (bf16[96,1024]{1,0:T(8,128)(2,1)S(1)}, bf16[96,1024]{1,0:T(8,128)(2,1)S(1)}, u32[]{:S(2)}, u32[]{:S(2)}) collective-permute-start(bf16[96,1024]{1,0:T(8,128)(2,1)S(1)} %get-tuple-element.39), channel_id=1, source_target_pairs={{0,16},{4,12},{8,24},{12,4},{16,0},{20,28},{24,8},{28,20},{1,17},{... | collective-permute-start | bytes 589832 | tf_op jit(solution)/shard_map/ppermute | solution.py:363
  28.2 0.7 %collective-permute-start.12 = (bf16[96,1024]{1,0:T(8,128)(2,1)S(1)}, bf16[96,1024]{1,0:T(8,128)(2,1)S(1)}, u32[]{:S(2)}, u32[]{:S(2)}) collective-permute-start(bf16[96,1024]{1,0:T(8,128)(2,1)S(1)} %get-tuple-element.40), channel_id=1, source_target_pairs={{0,4},{4,0},{8,12},{12,8},{16,20},{20,16},{24,28},{28,24},{1,5},{5... | collective-permute-start | bytes 589832 | tf_op jit(solution)/shard_map/ppermute | solution.py:363
  28.9 0.3 collective-permute-start.13
  29.2 1.2 %unit.1 = (bf16[84,768]{1,0:T(8,128)(2,1)S(1)}, f32[48,128]{1,0:T(8,128)S(1)}, f32[48,128]{1,0:T(8,128)S(1)}) custom-call(bf16[63,2048]{1,0:T(8,128)(2,1)S(1)} %get-tuple-element.42.near_ref, bf16[21,2048]{1,0:T(8,128)(2,1)S(1)} %get-tuple-element.43.far_ref, bf16[768,2048]{1,0:T(8,128)(2,1)S(1)} %get-tuple-element.44.weight_ref, ...), custom_call_target="tpu_custom_call" | custom-call | tf_op jit(solution)/shard_map/unit/pallas_call | solution.py:258
  30.4 1.1 %collective-permute-start.14 = (f32[48,128]{1,0:T(8,128)S(1)}, f32[48,128]{1,0:T(8,128)S(1)}, u32[]{:S(2)}, u32[]{:S(2)}) collective-permute-start(f32[48,128]{1,0:T(8,128)S(1)} %get-tuple-element.46), channel_id=1, source_target_pairs={{0,1},{1,0},{2,3},{3,2},{4,5},{5,4},{6,7},{7,6},{8,9},{9,8},{10,11... | collective-permute-start | bytes 73736 | tf_op jit(solution)/shard_map/ppermute | solution.py:295
  31.5 2.8 %collective-permute-done.14.got_ref = f32[48,128]{1,0:T(8,128)S(1)} collective-permute-done((f32[48,128]{1,0:T(8,128)S(1)}, f32[48,128]{1,0:T(8,128)S(1)}, u32[]{:S(2)}, u32[]{:S(2)}) %collective-permute-start.14) | collective-permute-done | bytes 24608 | tf_op jit(solution)/shard_map/ppermute | solution.py:295
  34.4 2.1 %collective-permute-start.15 = (f32[48,128]{1,0:T(8,128)S(1)}, f32[48,128]{1,0:T(8,128)S(1)}, u32[]{:S(2)}, u32[]{:S(2)}) collective-permute-start(f32[48,128]{1,0:T(8,128)S(1)} %get-tuple-element.48), channel_id=1, source_target_pairs={{0,2},{1,3},{2,0},{3,1},{4,6},{5,7},{6,4},{7,5},{8,10},{9,11},{10,... | collective-permute-start | bytes 73736 | tf_op jit(solution)/shard_map/ppermute | solution.py:295
  36.5 2.6 %collective-permute-done.15.refs_5_ = f32[48,128]{1,0:T(8,128)S(1)} collective-permute-done((f32[48,128]{1,0:T(8,128)S(1)}, f32[48,128]{1,0:T(8,128)S(1)}, u32[]{:S(2)}, u32[]{:S(2)}) %collective-permute-start.15) | collective-permute-done | bytes 24608 | tf_op jit(solution)/shard_map/ppermute | solution.py:295
  39.1 0.0 collective-permute-done.11.refs_1_
  39.1 0.0 collective-permute-done.12.refs_2_
  39.1 0.0 collective-permute-done.13.refs_3_
  39.1 0.0 copy-done
  39.1 0.0 copy-done.1
  39.1 0.0 copy-done.2
  39.2 1.0 %finish.1 = (f32[96,2048]{1,0:T(8,128)}, f32[8,256]{1,0:T(8,128)}, bf16[84,768]{1,0:T(8,128)(2,1)}) custom-call(f32[96,1024]{1,0:T(8,128)S(1)} %get-tuple-element.38.refs_0_, bf16[96,1024]{1,0:T(8,128)(2,1)S(1)} %collective-permute-done.11.refs_1_, bf16[96,1024]{1,0:T(8,128)(2,1)S(1)} %collective-permute-done.12.refs_2_, ...), custom_call_target="tpu_custom_call" | custom-call | tf_op jit(solution)/shard_map/finish/pallas_call | solution.py:423
  (1 shorter events, 0.0 us)
Async XLA Ops:
  2.2 7.4 %collective-permute-start.4 = (bf16[168,256]{1,0:T(8,128)(2,1)S(1)}, bf16[168,256]{1,0:T(8,128)(2,1)S(1)}, u32[]{:S(2)}, u32[]{:S(2)}) collective-permute-start(bf16[168,256]{1,0:T(8,128)(2,1)S(1)} %get-tuple-element.31), channel_id=1, source_target_pairs={{0,1},{1,0},{2,3},{3,2},{4,5},{5,4},{6,7},{7,6},{8,9},{9,8},{10,11... | collective-permute-start | bytes 258056 | tf_op jit(solution)/shard_map/ppermute | solution.py:456
  5.4 9.5 %collective-permute-start.5 = (bf16[168,256]{1,0:T(8,128)(2,1)S(1)}, bf16[168,256]{1,0:T(8,128)(2,1)S(1)}, u32[]{:S(2)}, u32[]{:S(2)}) collective-permute-start(bf16[168,256]{1,0:T(8,128)(2,1)S(1)} %get-tuple-element.32), channel_id=1, source_target_pairs={{0,2},{1,3},{2,0},{3,1},{4,6},{5,7},{6,4},{7,5},{8,10},{9,11},{10,... | collective-permute-start | bytes 258056 | tf_op jit(solution)/shard_map/ppermute | solution.py:456
  7.9 7.3 %collective-permute-start.3 = (bf16[168,256]{1,0:T(8,128)(2,1)S(1)}, bf16[168,256]{1,0:T(8,128)(2,1)S(1)}, u32[]{:S(2)}, u32[]{:S(2)}) collective-permute-start(bf16[168,256]{1,0:T(8,128)(2,1)S(1)} %get-tuple-element.29), channel_id=1, source_target_pairs={{0,3},{1,2},{2,1},{3,0},{4,7},{5,6},{6,5},{7,4},{8,11},{9,10},{10,... | collective-permute-start | bytes 258056 | tf_op jit(solution)/shard_map/ppermute | solution.py:456
  8.0 10.7 %collective-permute-start = (bf16[84,768]{1,0:T(8,128)(2,1)}, bf16[84,768]{1,0:T(8,128)(2,1)S(1)}, u32[]{:S(2)}, u32[]{:S(2)}) collective-permute-start(bf16[84,768]{1,0:T(8,128)(2,1)} %bitcast.25), channel_id=1, source_target_pairs={{0,8},{4,20},{8,0},{12,28},{16,24},{20,4},{24,16},{28,12},{1,9},{5... | collective-permute-start | bytes 387080 | tf_op jit(solution)/shard_map/ppermute | solution.py:363
  15.5 10.9 %collective-permute-start.6 = (bf16[96,1024]{1,0:T(8,128)(2,1)S(1)}, bf16[96,1024]{1,0:T(8,128)(2,1)S(1)}, u32[]{:S(2)}, u32[]{:S(2)}) collective-permute-start(bf16[96,1024]{1,0:T(8,128)(2,1)S(1)} %get-tuple-element.34), channel_id=1, source_target_pairs={{0,4},{4,0},{8,12},{12,8},{16,20},{20,16},{24,28},{28,24},{1,5},{5... | collective-permute-start | bytes 589832 | tf_op jit(solution)/shard_map/ppermute | solution.py:363
  15.6 5.5 %collective-permute-start.1 = (bf16[84,768]{1,0:T(8,128)(2,1)}, bf16[84,768]{1,0:T(8,128)(2,1)S(1)}, u32[]{:S(2)}, u32[]{:S(2)}) collective-permute-start(bf16[84,768]{1,0:T(8,128)(2,1)} %bitcast.26), channel_id=1, source_target_pairs={{0,20},{4,8},{8,28},{12,0},{16,4},{20,24},{24,12},{28,16},{1,21},{... | collective-permute-start | bytes 387080 | tf_op jit(solution)/shard_map/ppermute | solution.py:363
  17.2 5.6 %collective-permute-start.2 = (bf16[84,768]{1,0:T(8,128)(2,1)}, bf16[84,768]{1,0:T(8,128)(2,1)S(1)}, u32[]{:S(2)}, u32[]{:S(2)}) collective-permute-start(bf16[84,768]{1,0:T(8,128)(2,1)} %bitcast.27), channel_id=1, source_target_pairs={{0,4},{4,0},{8,12},{12,8},{16,20},{20,16},{24,28},{28,24},{1,5},{5... | collective-permute-start | bytes 387080 | tf_op jit(solution)/shard_map/ppermute | solution.py:363
  17.2 9.1 %collective-permute-start.7 = (bf16[63,1024]{1,0:T(8,128)(2,1)S(1)}, bf16[63,1024]{1,0:T(8,128)(2,1)S(1)}, u32[]{:S(2)}, u32[]{:S(2)}) collective-permute-start(bf16[63,1024]{1,0:T(8,128)(2,1)S(1)} %get-tuple-element.35.refs_0_), channel_id=1, source_target_pairs={{0,8},{4,20},{8,0},{12,28},{16,24},{20,4},{24,16},{28,12},{1,9},{5... | collective-permute-start | bytes 387080 | tf_op jit(solution)/shard_map/ppermute | solution.py:363
  18.7 7.7 %collective-permute-start.8 = (bf16[63,1024]{1,0:T(8,128)(2,1)S(1)}, bf16[63,1024]{1,0:T(8,128)(2,1)S(1)}, u32[]{:S(2)}, u32[]{:S(2)}) collective-permute-start(bf16[63,1024]{1,0:T(8,128)(2,1)S(1)} %get-tuple-element.33.refs_1_), channel_id=1, source_target_pairs={{0,20},{4,8},{8,28},{12,0},{16,4},{20,24},{24,12},{28,16},{1,21},{... | collective-permute-start | bytes 387080 | tf_op jit(solution)/shard_map/ppermute | solution.py:363
  21.1 4.6 %collective-permute-start.9 = (bf16[21,1024]{1,0:T(8,128)(2,1)S(1)}, bf16[21,1024]{1,0:T(8,128)(2,1)S(1)}, u32[]{:S(2)}, u32[]{:S(2)}) collective-permute-start(bf16[21,1024]{1,0:T(8,128)(2,1)S(1)} %get-tuple-element.36.refs_3_), channel_id=1, source_target_pairs={{0,8},{4,20},{8,0},{12,28},{16,24},{20,4},{24,16},{28,12},{1,9},{5... | collective-permute-start | bytes 129032 | tf_op jit(solution)/shard_map/ppermute | solution.py:363
  22.8 3.6 %collective-permute-start.10 = (bf16[21,1024]{1,0:T(8,128)(2,1)S(1)}, bf16[21,1024]{1,0:T(8,128)(2,1)S(1)}, u32[]{:S(2)}, u32[]{:S(2)}) collective-permute-start(bf16[21,1024]{1,0:T(8,128)(2,1)S(1)} %get-tuple-element.37), channel_id=1, source_target_pairs={{0,20},{4,8},{8,28},{12,0},{16,4},{20,24},{24,12},{28,16},{1,21},{... | collective-permute-start | bytes 129032 | tf_op jit(solution)/shard_map/ppermute | solution.py:363
  25.1 14.0 %copy-start = (s32[1,256,8]{1,2,0:T(8,128)S(1)}, s32[1,256,8]{1,2,0:T(8,128)}, u32[]{:S(2)}) copy-start(s32[1,256,8]{1,2,0:T(8,128)} %param.8) | copy-start | bytes 24580
  25.1 14.0 %copy-start.1 = (s32[1,256,8]{1,2,0:T(8,128)S(1)}, s32[1,256,8]{1,2,0:T(8,128)}, u32[]{:S(2)}) copy-start(s32[1,256,8]{1,2,0:T(8,128)} %param.9) | copy-start | bytes 24580
  25.1 14.0 %copy-start.2 = (bf16[1,256,8]{1,2,0:T(8,128)(2,1)S(1)}, bf16[1,256,8]{1,2,0:T(8,128)(2,1)}, u32[]{:S(2)}) copy-start(bf16[1,256,8]{1,2,0:T(8,128)(2,1)} %param.7) | copy-start | bytes 12292
  27.0 12.2 %collective-permute-start.11 = (bf16[96,1024]{1,0:T(8,128)(2,1)S(1)}, bf16[96,1024]{1,0:T(8,128)(2,1)S(1)}, u32[]{:S(2)}, u32[]{:S(2)}) collective-permute-start(bf16[96,1024]{1,0:T(8,128)(2,1)S(1)} %get-tuple-element.39), channel_id=1, source_target_pairs={{0,16},{4,12},{8,24},{12,4},{16,0},{20,28},{24,8},{28,20},{1,17},{... | collective-permute-start | bytes 589832 | tf_op jit(solution)/shard_map/ppermute | solution.py:363
  28.2 10.9 %collective-permute-start.12 = (bf16[96,1024]{1,0:T(8,128)(2,1)S(1)}, bf16[96,1024]{1,0:T(8,128)(2,1)S(1)}, u32[]{:S(2)}, u32[]{:S(2)}) collective-permute-start(bf16[96,1024]{1,0:T(8,128)(2,1)S(1)} %get-tuple-element.40), channel_id=1, source_target_pairs={{0,4},{4,0},{8,12},{12,8},{16,20},{20,16},{24,28},{28,24},{1,5},{5... | collective-permute-start | bytes 589832 | tf_op jit(solution)/shard_map/ppermute | solution.py:363
  28.9 10.2 %collective-permute-start.13 = (bf16[96,1024]{1,0:T(8,128)(2,1)S(1)}, bf16[96,1024]{1,0:T(8,128)(2,1)S(1)}, u32[]{:S(2)}, u32[]{:S(2)}) collective-permute-start(bf16[96,1024]{1,0:T(8,128)(2,1)S(1)} %get-tuple-element.41), channel_id=1, source_target_pairs={{0,20},{4,8},{8,28},{12,0},{16,4},{20,24},{24,12},{28,16},{1,21},{... | collective-permute-start | bytes 589832 | tf_op jit(solution)/shard_map/ppermute | solution.py:363
  30.4 4.0 %collective-permute-start.14 = (f32[48,128]{1,0:T(8,128)S(1)}, f32[48,128]{1,0:T(8,128)S(1)}, u32[]{:S(2)}, u32[]{:S(2)}) collective-permute-start(f32[48,128]{1,0:T(8,128)S(1)} %get-tuple-element.46), channel_id=1, source_target_pairs={{0,1},{1,0},{2,3},{3,2},{4,5},{5,4},{6,7},{7,6},{8,9},{9,8},{10,11... | collective-permute-start | bytes 73736 | tf_op jit(solution)/shard_map/ppermute | solution.py:295
  34.4 4.7 %collective-permute-start.15 = (f32[48,128]{1,0:T(8,128)S(1)}, f32[48,128]{1,0:T(8,128)S(1)}, u32[]{:S(2)}, u32[]{:S(2)}) collective-permute-start(f32[48,128]{1,0:T(8,128)S(1)} %get-tuple-element.48), channel_id=1, source_target_pairs={{0,2},{1,3},{2,0},{3,1},{4,6},{5,7},{6,4},{7,5},{8,10},{9,11},{10,... | collective-permute-start | bytes 73736 | tf_op jit(solution)/shard_map/ppermute | solution.py:295
